TPU v7x, 512 devices: a whole 4x8x8 slice. The times are simulated.
512 devices in a mesh: section: 4 (over x_hi, core), head: 16 (over y, x_lo), kv: 8 (over z).
Axes of the slice: x: 4 (x_hi: 2, x_lo: 2; x = x_hi * 2 + x_lo), y: 8, z: 8, core: 2. Of those that a mesh axis runs over, the one named last changes fastest.
Arguments:
- tokens: bfloat16 [4, 1024, 4096], P('section', 'kv', 'head'), may hold values from -40 to 40
- w_query: bfloat16 [4096, 4096], P(('section', 'kv'), 'head'), may hold values from -0.21875 to 0.21875
- w_keyvalue: bfloat16 [4096, 2, 4096], P(('section', 'kv'), None, 'head'), may hold values from -0.09375 to 0.09375
- cache_keys: bfloat16 [4, 16384, 4096], P('section', 'kv', 'head'), may hold values from -800 to 800
- cache_values: bfloat16 [4, 16384, 4096], P('section', 'kv', 'head'), may hold values from -6 to 6
- key_start: int32 [4], P('section'), may hold values from 0 to 8191
- key_end: int32 [4], P('section'), may hold values from 12288 to 16384
- w_out: bfloat16 [4096, 4096], P('head', ('section', 'kv')), may hold values from -0.375 to 0.375
Outputs:
- attention_out: bfloat16 [4, 1024, 4096], P('section', 'kv', 'head')
All inputs are finite; a program needn't handle non-finite values.
Results may differ from a plain program's by a relative error of at most 0.014.
The roundings to bfloat16 on the way count: a program that leaves them out, or rounds other values in their place, can miss the bound.
Values may be sent and summed in bfloat16 or wider, within the bound.
No kernel may reach another device: no remote copies, remote signals or barrier semaphores. Data moves between devices by JAX's collectives and lax.ppermute only.
A program may use at most 64 MiB of HBM per device.

v0:
```python
import jax
import jax.numpy as jnp
from jax import lax
from jax.sharding import Mesh
from jax.sharding import PartitionSpec as P

HD = 128
HEAD = ("head_0", "head_1")


def joined_along(tiles, dim):
    shape = list(tiles.shape[1:])
    shape[dim] *= tiles.shape[0]
    return jnp.moveaxis(tiles, 0, dim).reshape(shape)


def sent_to_all(value, axis):
    copies = jnp.broadcast_to(value, (lax.axis_size(axis), *value.shape))
    return lax.all_to_all(copies, axis, split_axis=0, concat_axis=0, tiled=True)


def gather_directly(value, axis, dim):
    return joined_along(sent_to_all(value, axis), dim)


def side_by_side(arrays, axis, dim, along):
    columns = [a.reshape(*a.shape[:along], -1) for a in arrays]
    both = jnp.concatenate(columns, axis=along)
    out, at, gathered = (lax.all_gather(both, axis, axis=dim, tiled=True), 0, [])
    for a, column in zip(arrays, columns):
        slab = out[..., at : at + column.shape[along]]
        gathered.append(slab.reshape(*slab.shape[:along], *a.shape[along:]))
        at += column.shape[along]
    return tuple(gathered)


def in_blocks(value, dim, length):
    shape = value.shape
    tiles = value.reshape(*shape[:dim], length, shape[dim] // length, *shape[dim + 1 :])
    return jnp.moveaxis(tiles, dim, 0)


def sent_and_summed(value, axis, dim):
    tiles = in_blocks(value, dim, lax.axis_size(axis))
    arrived = lax.all_to_all(tiles, axis, split_axis=0, concat_axis=0, tiled=True)
    return arrived.sum(axis=0)


def sent_together(arrays, axis, dim, along):
    ends, at = ([], 0)
    for a in arrays[:-1]:
        at += a.shape[along]
        ends.append(at)
    both = jnp.concatenate(arrays, axis=along)
    return tuple(jnp.split(sent_and_summed(both, axis, dim), ends, axis=along))


def side_by_side_2(arrays, axis, split_dim, concat_dim, along):
    ends, at = ([], 0)
    for a in arrays[:-1]:
        at += a.shape[along]
        ends.append(at)
    both = jnp.concatenate(arrays, axis=along)
    return tuple(
        jnp.split(
            lax.all_to_all(both, axis, split_axis=split_dim, concat_axis=concat_dim, tiled=True),
            ends,
            axis=along,
        )
    )


def gather_axes(value, axes, dim):
    out = value
    for number in range(len(axes) - 1, -1, -1):
        out = lax.all_gather(out, axes[number], axis=dim, tiled=True)
    return out


def add_projection(pieces, inputs):
    query_rows = jnp.dot(inputs, pieces[0], preferred_element_type=jnp.float32)
    pair_weight = pieces[1].reshape(pieces[1].shape[0], -1)
    pair_rows = jnp.dot(inputs, pair_weight, preferred_element_type=jnp.float32)
    return (query_rows, pair_rows)


def shards(tokens, w_query, w_keyvalue, cache_keys, cache_values, key_start, key_end, w_out):
    local_rows = tokens.shape[1]
    head_width = tokens.shape[2]
    heads_here = head_width // HD
    gathered = gather_directly(tokens, HEAD, 2)[0]
    widened = gathered.astype(jnp.float32)
    scaled = widened * lax.rsqrt(jnp.mean(widened * widened, axis=1, keepdims=True) + 1e-05)
    normed = scaled.astype(jnp.bfloat16)
    blocks = lax.all_to_all(normed, "section", split_axis=1, concat_axis=0, tiled=True)
    query_part, pair_part = add_projection(side_by_side((w_query, w_keyvalue), "kv", 0, 1), blocks)
    query_sum, pair_sum = sent_together((query_part, pair_part), "section", 0, 1)
    queries_own = query_sum.astype(jnp.bfloat16)
    new_keys = pair_sum[:, :head_width].astype(jnp.bfloat16)
    new_values = pair_sum[:, head_width:].astype(jnp.bfloat16)
    queries = gather_directly(queries_own, "kv", 0)
    total_rows = queries.shape[0]
    kv_index = lax.axis_index("kv")
    cache_rows = cache_keys.shape[1]
    keys_all = jnp.concatenate([cache_keys[0], new_keys], axis=0).reshape(-1, heads_here, HD)
    values_all = jnp.concatenate([cache_values[0], new_values], axis=0).reshape(-1, heads_here, HD)
    cache_place = kv_index * cache_rows + lax.iota(jnp.int32, cache_rows)
    cache_usable = (cache_place >= key_start[0]) & (cache_place < key_end[0])
    new_place = kv_index * local_rows + lax.iota(jnp.int32, local_rows)
    block_rows = 512
    count_blocks = total_rows // block_rows
    grouped = queries.reshape(count_blocks, block_rows, heads_here, HD)
    score_scale = HD ** (-0.5)

    def attend(packed):
        query_block, block_index = packed
        query_place = block_index * block_rows + lax.iota(jnp.int32, block_rows)
        scores = (
            jnp.einsum("qhd,khd->hqk", query_block, keys_all, preferred_element_type=jnp.float32)
            * score_scale
        )
        usable = jnp.concatenate(
            [
                jnp.broadcast_to(cache_usable[None, :], (block_rows, cache_rows)),
                new_place[None, :] <= query_place[:, None],
            ],
            axis=1,
        )
        masked = jnp.where(usable[None], scores, -1e30)
        row_peak = jnp.max(masked, axis=2)
        weights = jnp.where(usable[None], jnp.exp(masked - row_peak[:, :, None]), 0.0).astype(
            jnp.bfloat16
        )
        row_total = jnp.sum(weights.astype(jnp.float32), axis=2)
        mixture = jnp.einsum(
            "hqk,khd->qhd", weights, values_all, preferred_element_type=jnp.float32
        )
        return (row_peak.T, row_total.T, mixture.reshape(block_rows, head_width))

    peaks, totals, mixtures = lax.map(attend, (grouped, jnp.arange(count_blocks, dtype=jnp.int32)))
    peaks = peaks.reshape(total_rows, heads_here)
    totals = totals.reshape(total_rows, heads_here)
    mixtures = mixtures.reshape(total_rows, head_width)
    gathered_peaks, gathered_totals, gathered_mixtures = side_by_side_2(
        (peaks[None], totals[None], mixtures[None]), "kv", 1, 0, 2
    )
    highest = jnp.max(gathered_peaks, axis=0)
    factors = jnp.exp(gathered_peaks - highest[None])
    own_total = jnp.sum(gathered_totals * factors, axis=0)
    split_mixture = gathered_mixtures.reshape(
        gathered_mixtures.shape[0], local_rows, heads_here, HD
    )
    own_mixture = jnp.sum(split_mixture * factors[..., None], axis=0).reshape(
        local_rows, head_width
    )
    attended = (
        (own_mixture.reshape(local_rows, heads_here, HD) / own_total[..., None])
        .reshape(local_rows, head_width)
        .astype(jnp.bfloat16)
    )
    attended_full = gather_axes(attended, HEAD, 1)
    row_block = lax.all_gather(w_out, ("section", "kv"), axis=1, tiled=True)
    column_block = lax.all_to_all(row_block, HEAD, split_axis=1, concat_axis=0, tiled=True)
    summed = jnp.dot(attended_full, column_block, preferred_element_type=jnp.float32)
    return summed.astype(jnp.bfloat16)[None]


def solution(mesh):
    torus = Mesh(
        mesh.devices.reshape(mesh.shape["section"], 8, 2, mesh.shape["kv"]),
        ("section", "head_0", "head_1", "kv"),
    )
    return jax.shard_map(
        shards,
        mesh=torus,
        in_specs=(
            P("section", "kv", HEAD),
            P(("section", "kv"), HEAD),
            P(("section", "kv"), None, HEAD),
            P("section", "kv", HEAD),
            P("section", "kv", HEAD),
            P("section"),
            P("section"),
            P(HEAD, ("section", "kv")),
        ),
        out_specs=P("section", "kv", HEAD),
        check_vma=False,
    )
```

profile of v0, /device:TPU:16, one launch (start us, length us, event | category | flops | bytes accessed | tf_op | source)
XLA Modules:
  0.0 283.1 jit_solution(13094766930239669470)
XLA Ops:
  7.4 1.0 copy.64
  8.4 1.2 broadcast_in_dim.57
  9.6 9.1 %all-to-all-start = ((bf16[16,1,128,256]{2,3,1,0:T(8,128)(2,1)}), bf16[16,1,128,256]{2,3,1,0:T(8,128)(2,1)S(1)}, u32[]{:S(2)}, u32[]{:S(2)}) async-start(bf16[16,1,128,256]{2,3,1,0:T(8,128)(2,1)} %broadcast_in_dim.57), calls=%async_computation | async-start | bytes 2097152 | tf_op jit(solution)/shard_map/all_to_all | solution.py:19
  18.8 0.7 pad_maximum_fusion.3
  19.5 24.6 %all-to-all-done = bf16[16,1,128,256]{2,3,1,0:T(8,128)(2,1)S(1)} async-done(((bf16[16,1,128,256]{2,3,1,0:T(8,128)(2,1)}), bf16[16,1,128,256]{2,3,1,0:T(8,128)(2,1)S(1)}, u32[]{:S(2)}, u32[]{:S(2)}) %all-to-all-start) | async-done | bytes 1048608 | tf_op jit(solution)/shard_map/all_to_all | solution.py:19
  44.1 0.6 multiply_reduce_fusion
  44.7 0.2 bitcast_convert_fusion
  44.9 0.2 multiply_convert_fusion
  45.1 19.8 %all_to_all.62 = bf16[128,4,1024]{0,2,1:T(8,128)(2,1)S(1)} all-to-all(bf16[128,4,1024]{0,2,1:T(8,128)(2,1)S(1)} %multiply_convert_fusion), channel_id=1, replica_groups=mesh['section'=4,'head_0'=8,'head_1'=2,'kv'=8] {'section'}, dimensions={1} | all-to-all | bytes 2097152 | tf_op jit(solution)/shard_map/all_to_all | solution.py:95
  64.9 0.5 copy.66
  65.4 2.3 all-gather.4.cloned.1.call-done
  67.7 2.0 fusion.12
  69.7 1.5 fusion.14
  71.2 0.1 copy_bitcast_fusion.2
  71.3 25.6 %all_to_all.63 = f32[4,128,768]{1,2,0:T(8,128)S(1)} all-to-all(f32[4,128,768]{1,2,0:T(8,128)S(1)} %copy_bitcast_fusion.2), channel_id=1, replica_groups=mesh['section'=4,'head_0'=8,'head_1'=2,'kv'=8] {'section'}, dimensions={0} | all-to-all | bytes 3145728 | tf_op jit(solution)/shard_map/all_to_all | solution.py:45
  97.0 0.1 copy.68
  97.2 0.8 broadcast_in_dim.58
  98.0 6.4 %all-to-all-start.3 = ((bf16[8,128,256]{2,1,0:T(8,128)(2,1)}), bf16[8,128,256]{2,1,0:T(8,128)(2,1)}, u32[]{:S(2)}, u32[]{:S(2)}) async-start(bf16[8,128,256]{2,1,0:T(8,128)(2,1)} %broadcast_in_dim.58), calls=%async_computation.3 | async-start | bytes 1048576 | tf_op jit(solution)/shard_map/all_to_all | solution.py:19
  104.4 0.2 all-gather.8.cloned.1.call-start
  104.7 0.7 copy.78
  105.5 0.6 copy.69
  106.1 1.5 copy.70
  107.8 1.4 copy.72
  109.1 1.1 pad_maximum_fusion.2
  110.2 11.4 %all-to-all-done.3 = bf16[8,128,256]{2,1,0:T(8,128)(2,1)} async-done(((bf16[8,128,256]{2,1,0:T(8,128)(2,1)}), bf16[8,128,256]{2,1,0:T(8,128)(2,1)}, u32[]{:S(2)}, u32[]{:S(2)}) %all-to-all-start.3) | async-done | bytes 524320 | tf_op jit(solution)/shard_map/all_to_all | solution.py:19
  121.7 1.2 reshape_reshape.3
  122.9 27.7 %while.15 = (s32[]{:T(128)}, f32[2,512,2]{1,2,0:T(2,128)S(1)}, f32[2,512,2]{1,2,0:T(2,128)S(1)}, f32[2,512,256]{2,1,0:T(8,128)}, s32[2]{0:T(128)S(1)}, /*index=5...) while((s32[]{:T(128)}, f32[2,512,2]{1,2,0:T(2,128)S(1)}, ...), condition=%wide.region_5.6_spmd.clone, body=%wide.region_2.5_spmd.clone.sunk | while | flops 1175460480 | bytes 37008844 | solution.py:140
  122.9 0.6 dynamic_slice.14
  124.0 0.1 broadcast_compare_fusion.2
  124.2 1.3 fusion.37
  125.5 0.3 pad_add_fusion.2
  125.8 0.2 constant_dynamic-slice_fusion.2
  126.0 2.4 fusion.38
  128.4 3.0 %convert_reduce_fusion.2 = f32[2,512]{1,0:T(2,128)S(1)} fusion(f32[2,512]{1,0:T(2,128)S(1)} %get-tuple-element.263, f32[2,512,2176]{2,1,0:T(8,128)S(1)} %get-tuple-element.264, pred[512,2176]{1,0:T(8,128)(4,1)S(1)} %pad_add_fusion.2), kind=kLoop, calls=%fused_computation.2.clone.1 | loop fusion | flops 15596544 | bytes 10035200 | tf_op jit(solution)/shard_map/while/body/eval_jaxpr/reduce_sum | solution.py:134
  131.5 4.2 %fusion.39 = f32[2,512,128]{1,2,0:T(8,128)S(1)} fusion(bf16[2176,2,128]{0,2,1:T(8,128)(2,1)} %get-tuple-element.304, f32[2,512,2176]{2,1,0:T(8,128)S(1)} %get-tuple-element.264, f32[2,512]{1,0:T(2,128)S(1)} %get-tuple-element.263, pred[512,2176]{1,0:T(8,128)(4,1)S(1)} %pad_add_fusion.2), kind=kOutput, calls=%fused_computation.20.clone.1 | convolution fusion | flops 581566464 | bytes 11669504 | tf_op jit(solution)/shard_map/while/body/eval_jaxpr/hqk,khd->qhd/dot_general | solution.py:135
  135.7 0.2 copy.98
  135.9 0.8 constant_dynamic-update-slice_fusion.2
  136.7 0.5 dynamic_slice.14
  137.8 0.1 broadcast_compare_fusion.2
  138.0 1.3 fusion.37
  139.3 0.3 pad_add_fusion.2
  139.6 0.2 constant_dynamic-slice_fusion.2
  139.8 2.4 fusion.38
  142.2 3.0 %convert_reduce_fusion.2 = f32[2,512]{1,0:T(2,128)S(1)} fusion(f32[2,512]{1,0:T(2,128)S(1)} %get-tuple-element.263, f32[2,512,2176]{2,1,0:T(8,128)S(1)} %get-tuple-element.264, pred[512,2176]{1,0:T(8,128)(4,1)S(1)} %pad_add_fusion.2), kind=kLoop, calls=%fused_computation.2.clone.1 | loop fusion | flops 15596544 | bytes 10035200 | tf_op jit(solution)/shard_map/while/body/eval_jaxpr/reduce_sum | solution.py:134
  145.3 4.2 %fusion.39 = f32[2,512,128]{1,2,0:T(8,128)S(1)} fusion(bf16[2176,2,128]{0,2,1:T(8,128)(2,1)} %get-tuple-element.304, f32[2,512,2176]{2,1,0:T(8,128)S(1)} %get-tuple-element.264, f32[2,512]{1,0:T(2,128)S(1)} %get-tuple-element.263, pred[512,2176]{1,0:T(8,128)(4,1)S(1)} %pad_add_fusion.2), kind=kOutput, calls=%fused_computation.20.clone.1 | convolution fusion | flops 581566464 | bytes 11669504 | tf_op jit(solution)/shard_map/while/body/eval_jaxpr/hqk,khd->qhd/dot_general | solution.py:135
  149.5 0.2 copy.98
  149.7 0.8 constant_dynamic-update-slice_fusion.2
  150.6 0.2 copy.75
  150.8 0.2 copy.74
  151.0 2.0 pad_maximum_fusion
  153.0 2.8 copy.76
  155.8 3.6 %all-to-all-start.4 = ((f32[1,1024,260]{2,0,1:T(1,128)}), f32[1,1024,260]{2,0,1:T(1,128)S(1)}, u32[]{:S(2)}, u32[]{:S(2)}) async-start(f32[1,1024,260]{2,0,1:T(1,128)} %copy.76), calls=%async_computation.4 | async-start | bytes 3145728 | tf_op jit(solution)/shard_map/all_to_all | solution.py:66
  159.4 36.6 %all-gather.8.cloned.1.call-done = bf16[256,4096]{0,1:T(8,128)(2,1)} async-done(((bf16[256,128]{0,1:T(8,128)(2,1)}), bf16[256,4096]{0,1:T(8,128)(2,1)}) %all-gather.8.cloned.1.call-update) | async-done | bytes 2097168 | tf_op jit(solution)/shard_map/all_gather | solution.py:162
  196.0 7.6 %all-to-all-done.4 = f32[1,1024,260]{2,0,1:T(1,128)S(1)} async-done(((f32[1,1024,260]{2,0,1:T(1,128)}), f32[1,1024,260]{2,0,1:T(1,128)S(1)}, u32[]{:S(2)}, u32[]{:S(2)}) %all-to-all-start.4) | async-done | bytes 1064992 | tf_op jit(solution)/shard_map/all_to_all | solution.py:66
  203.5 1.1 copy-done
  204.7 6.1 %all-to-all-start.5 = ((bf16[256,16,256]{0,2,1:T(8,128)(2,1)}), bf16[256,16,256]{0,2,1:T(8,128)(2,1)S(1)}, u32[]{:S(2)}, u32[]{:S(2)}) async-start(bf16[256,16,256]{0,2,1:T(8,128)(2,1)} %bitcast.90), calls=%async_computation.5 | async-start | bytes 4194304 | tf_op jit(solution)/shard_map/all_to_all | solution.py:163
  210.9 3.6 %copy.77 = f32[1,1024,260]{1,2,0:T(8,128)S(1)} copy(f32[1,1024,260]{2,0,1:T(1,128)} %copy-done) | data formatting | bytes 2129920 | tf_op jit(solution)/shard_map/all_to_all | solution.py:66
  214.4 0.2 copy.89
  214.8 0.4 fusion.11
  215.2 5.0 %all_gather.13 = bf16[128,512]{0,1:T(8,128)(2,1)} all-gather(bf16[128,256]{0,1:T(8,128)(2,1)S(1)} %fusion.16), channel_id=1, replica_groups=mesh['section'=4,'head_0'=8,'head_1'=2,'kv'=8] {'head_1'}, dimensions={1}, use_global_device_ids=true | all-gather | bytes 196608 | tf_op jit(solution)/shard_map/all_gather | solution.py:76
  220.3 47.1 %all-to-all-done.5 = bf16[256,16,256]{0,2,1:T(8,128)(2,1)S(1)} async-done(((bf16[256,16,256]{0,2,1:T(8,128)(2,1)}), bf16[256,16,256]{0,2,1:T(8,128)(2,1)S(1)}, u32[]{:S(2)}, u32[]{:S(2)}) %all-to-all-start.5) | async-done | bytes 2097184 | tf_op jit(solution)/shard_map/all_to_all | solution.py:163
  267.4 2.4 copy.79
  269.7 2.8 all-gather.6.cloned.1.call-done
  272.5 3.1 %fusion.10 = bf16[1,128,256]{2,1,0:T(8,128)(2,1)} fusion(bf16[128,4096]{0,1:T(8,128)(2,1)} %all-gather.6.cloned.1.call-done, bf16[4096,256]{1,0:T(8,128)(2,1)} %bitcast.81), kind=kOutput, calls=%fused_computation.27 | convolution fusion | flops 268468224 | bytes 3211264 | tf_op jit(solution)/shard_map/dot_general | solution.py:164
  (36 shorter events, 0.6 us)
Async XLA Ops:
  7.4 11.4 %copy-start.3 = (bf16[128,2,256]{2,1,0:T(2,128)(2,1)S(1)}, bf16[128,2,256]{2,1,0:T(2,128)(2,1)}, u32[]{:S(2)}) copy-start(bf16[128,2,256]{2,1,0:T(2,128)(2,1)} %param.12) | copy-start | bytes 393220
  7.4 11.4 %copy-start.5 = (bf16[128,256]{1,0:T(8,128)(2,1)S(1)}, bf16[128,256]{1,0:T(8,128)(2,1)}, u32[]{:S(2)}) copy-start(bf16[128,256]{1,0:T(8,128)(2,1)} %param.11) | copy-start | bytes 196612
  9.6 34.6 %all-to-all-start = ((bf16[16,1,128,256]{2,3,1,0:T(8,128)(2,1)}), bf16[16,1,128,256]{2,3,1,0:T(8,128)(2,1)S(1)}, u32[]{:S(2)}, u32[]{:S(2)}) async-start(bf16[16,1,128,256]{2,3,1,0:T(8,128)(2,1)} %broadcast_in_dim.57), calls=%async_computation | async-start | bytes 2097152 | tf_op jit(solution)/shard_map/all_to_all | solution.py:19
  18.7 49.0 %all-gather.4.cloned.1.call-start = ((), (), s32[]{:S(2)}) async-start(), calls=%async_computation.6 | async-start | bytes 1769472 | tf_op jit(solution)/shard_map/all_gather | solution.py:29
  96.9 7.7 %copy-start.4 = (bf16[256,128]{1,0:T(8,128)(2,1)S(1)}, bf16[256,128]{1,0:T(8,128)(2,1)}, u32[]{:S(2)}) copy-start(bf16[256,128]{1,0:T(8,128)(2,1)} %param.17) | copy-start | bytes 196612
  96.9 8.5 %copy-start.2 = (bf16[1,2048,256]{2,1,0:T(8,128)(2,1)S(1)}, bf16[1,2048,256]{2,1,0:T(8,128)(2,1)}, u32[]{:S(2)}) copy-start(bf16[1,2048,256]{2,1,0:T(8,128)(2,1)} %param.13) | copy-start | bytes 3145732
  98.0 23.7 %all-to-all-start.3 = ((bf16[8,128,256]{2,1,0:T(8,128)(2,1)}), bf16[8,128,256]{2,1,0:T(8,128)(2,1)}, u32[]{:S(2)}, u32[]{:S(2)}) async-start(bf16[8,128,256]{2,1,0:T(8,128)(2,1)} %broadcast_in_dim.58), calls=%async_computation.3 | async-start | bytes 1048576 | tf_op jit(solution)/shard_map/all_to_all | solution.py:19
  104.4 91.5 %all-gather.8.cloned.1.call-start = ((), (), s32[]{:S(2)}) async-start(), calls=%async_computation.8 | async-start | bytes 2162688 | tf_op jit(solution)/shard_map/all_gather | solution.py:162
  109.1 13.7 %copy-start.1 = (bf16[2176,2,128]{2,0,1:T(8,128)(2,1)S(1)}, bf16[2176,2,128]{2,0,1:T(8,128)(2,1)}, u32[]{:S(2)}) copy-start(bf16[2176,2,128]{2,0,1:T(8,128)(2,1)} %copy.72) | copy-start | bytes 3342340
  155.8 47.8 %all-to-all-start.4 = ((f32[1,1024,260]{2,0,1:T(1,128)}), f32[1,1024,260]{2,0,1:T(1,128)S(1)}, u32[]{:S(2)}, u32[]{:S(2)}) async-start(f32[1,1024,260]{2,0,1:T(1,128)} %copy.76), calls=%async_computation.4 | async-start | bytes 3145728 | tf_op jit(solution)/shard_map/all_to_all | solution.py:66
  203.5 1.1 copy-start
  204.7 62.7 %all-to-all-start.5 = ((bf16[256,16,256]{0,2,1:T(8,128)(2,1)}), bf16[256,16,256]{0,2,1:T(8,128)(2,1)S(1)}, u32[]{:S(2)}, u32[]{:S(2)}) async-start(bf16[256,16,256]{0,2,1:T(8,128)(2,1)} %bitcast.90), calls=%async_computation.5 | async-start | bytes 4194304 | tf_op jit(solution)/shard_map/all_to_all | solution.py:163
  210.8 61.7 %all-gather.6.cloned.1.call-start = ((), (), s32[]{:S(2)}) async-start(), calls=%async_computation.7 | async-start | bytes 1179648 | tf_op jit(solution)/shard_map/all_gather | solution.py:76
Sparse Core Ops, SparseCore 0:
  21.6 46.0 all-gather.3
  220.4 52.0 all-gather.5
Sparse Core Ops, SparseCore 1:
  108.3 87.6 all-gather.7
where the time goes:
time: 284 us; the launch traced here: 283 us
  waiting for transfers between devices  132 us (46%)
  blocking collectives  50.4 us (18%)
  starting transfers between devices  25.6 us (9%)
  local copies, waits for them, and re-layouts  23.3 us (8%)
  matrix products  19.9 us (7%)
  between operations  15.1 us (5%)
  other arithmetic  15 us (5%)
    all_to_all x1, waiting for transfers between devices, shards(): lax.all_to_all(row_block, HEAD, split_axis=1, concat_axis=0, tiled=True)  47.1 us
    all_gather x1, waiting for transfers between devices, shards(): row_block = lax.all_gather(w_out, ('section', 'kv'), axis=1, tiled=True)  36.6 us
    all_to_all x2, waiting for transfers between devices, sent_to_all(): return lax.all_to_all(copies, axis, split_axis=0, concat_axis=0, tiled=True)  36.1 us
    all_to_all x1, blocking collectives, sent_and_summed(): lax.all_to_all(tiles, axis, split_axis=0, concat_axis=0, tiled=True)  25.6 us
    all_to_all x1, blocking collectives, shards(): lax.all_to_all(normed, 'section', split_axis=1, concat_axis=0, tiled=True)  19.8 us
    all_to_all x2, starting transfers between devices, sent_to_all(): return lax.all_to_all(copies, axis, split_axis=0, concat_axis=0, tiled=True)  15.6 us
    dot_general x2, matrix products, attend(): jnp.einsum('hqk,khd->qhd', weights, values_all, preferred_element_type=jn...  8.45 us
    all_to_all x1, waiting for transfers between devices, side_by_side_2(): lax.all_to_all(both, axis, split_axis=split_dim, concat_axis=concat_dim,...  7.58 us
  transfers between devices with their start and end apart: 7, of which 7 were waited for; matrix products, arithmetic and copies ran while one was open for 17% of the time, Pallas kernels for 0%

commit v1 on v0

v1 whole, which is shorter than its diff:
```python
import jax
import jax.numpy as jnp
from jax import lax
from jax.experimental import pallas as pl
from jax.experimental.pallas import tpu as pltpu
from jax.sharding import Mesh
from jax.sharding import PartitionSpec as P

HD = 128
HEAD = ("y", "x_lo")
ROWS = ("x_hi", "kv")
STAT_ROWS = 16
QUERY_ROWS = 512
KEY_ROWS = 512
DEAD = -1e30
SCALE = HD**-0.5
EXPONENT = SCALE * 1.4426950408889634
VMEM = pltpu.CompilerParams(vmem_limit_bytes=48 * 1024 * 1024)
SCALAR = pl.BlockSpec(memory_space=pltpu.SMEM)
WHOLE = pl.BlockSpec(memory_space=pltpu.VMEM)


def dot(a, b):
    return jnp.dot(a, b, preferred_element_type=jnp.float32)


def shared(value, axes):
    copies = jnp.broadcast_to(value, (lax.axis_size(axes), *value.shape))
    return lax.all_to_all(copies, axes, split_axis=0, concat_axis=0, tiled=True)


def swapped(value):
    return lax.ppermute(value, "core", [(0, 1), (1, 0)])


def normalize_kernel(core_ref, x_ref, keep_ref, send_ref):
    core = core_ref[0]
    blocks = x_ref.shape[0]
    squares = None
    for b in range(blocks):
        x = x_ref[b].astype(jnp.float32)
        squares = x * x if squares is None else squares + x * x
    mean = jnp.sum(squares, axis=1, keepdims=True) / (blocks * x_ref.shape[2])
    factor = lax.rsqrt(mean + 1e-05)
    for half in range(2):
        for j in range(4):
            for out_ref, side in ((keep_ref, core), (send_ref, 1 - core)):
                x = x_ref[half * 8 + side * 4 + j].astype(jnp.float32)
                out_ref[half * 4 + j] = (x * factor).astype(jnp.bfloat16)


def project_kernel(own_ref, other_ref, w_ref, own_out, other_out):
    rows = own_ref.shape[1]
    total = None
    for b in range(own_ref.shape[0]):
        x = jnp.concatenate([own_ref[b], other_ref[b]], axis=0)
        part = dot(x, w_ref[b])
        total = part if total is None else total + part
    own_out[...] = total[:rows]
    other_out[...] = total[rows:]


def thirds(value):
    high = value.astype(jnp.bfloat16)
    rest = value - high.astype(jnp.float32)
    middle = rest.astype(jnp.bfloat16)
    low = (rest - middle.astype(jnp.float32)).astype(jnp.bfloat16)
    return [high.astype(jnp.float32), middle.astype(jnp.float32), low.astype(jnp.float32)]


def attend_kernel(kv_ref, bias_ref, q_ref, k_ref, v_ref, new_k_ref, new_v_ref, out_ref, s_ref):
    first = pl.program_id(1) * QUERY_ROWS
    q = q_ref[...]
    cache_rows = k_ref.shape[0]
    new_rows = new_k_ref.shape[0]

    def score(keys):
        return lax.dot_general(q, keys, (((1,), (1,)), ((), ())), preferred_element_type=jnp.float32)

    peak = None
    for at in range(0, cache_rows, KEY_ROWS):
        s = score(k_ref[at : at + KEY_ROWS]) + bias_ref[0:1, at : at + KEY_ROWS]
        s_ref[:, at : at + KEY_ROWS] = s
        for lane in range(0, KEY_ROWS, HD):
            piece = s[:, lane : lane + HD]
            peak = piece if peak is None else jnp.maximum(peak, piece)
    s = score(new_k_ref[...])
    row = first + lax.broadcasted_iota(jnp.int32, s.shape, 0)
    column = kv_ref[0] * new_rows + lax.broadcasted_iota(jnp.int32, s.shape, 1)
    s = jnp.where(column <= row, s, DEAD)
    s_ref[:, cache_rows:] = s
    peak = jnp.max(jnp.maximum(peak, s), axis=1, keepdims=True)

    def mixed(at, values):
        weights = jnp.exp2((s_ref[:, at : at + values.shape[0]] - peak) * EXPONENT)
        both = jnp.concatenate([values, jnp.ones_like(values)], axis=1)
        return dot(weights.astype(jnp.bfloat16), both)

    total = mixed(cache_rows, new_v_ref[...])
    for at in range(0, cache_rows, KEY_ROWS):
        total = total + mixed(at, v_ref[at : at + KEY_ROWS])

    lane = lax.broadcasted_iota(jnp.int32, (HD, HD), 1)
    blocks, rows, _ = out_ref.shape
    own = rows - STAT_ROWS
    for b in range(blocks):
        part = total[b * own : (b + 1) * own]
        out_ref[b, :own] = part[:, :HD].astype(jnp.bfloat16)
        turned = jnp.where(lane == 0, peak[b * own : (b + 1) * own], part[:, HD:]).T
        stats = thirds(turned[0:1]) + thirds(turned[1:2])
        stats = jnp.concatenate([*stats, jnp.zeros((STAT_ROWS - 6, HD), jnp.float32)], axis=0)
        out_ref[b, own:] = stats.astype(jnp.bfloat16)


def finish_kernel(core_ref, parts_ref, own_w_ref, other_w_ref, out_ref):
    core = core_ref[0]
    sources, rows, width = parts_ref.shape
    own = rows - STAT_ROWS
    heads = []
    for at in range(0, width, HD):
        stats = [parts_ref[z, own:, at : at + HD].astype(jnp.float32) for z in range(sources)]
        peaks = [s[0:1] + s[1:2] + s[2:3] for s in stats]
        totals = [s[3:4] + s[4:5] + s[5:6] for s in stats]
        highest = peaks[0]
        for p in peaks[1:]:
            highest = jnp.maximum(highest, p)
        factors = [jnp.exp2((p - highest) * EXPONENT) for p in peaks]
        total = sum(f * t for f, t in zip(factors, totals))
        shares = [f / total for f in factors]
        shares = jnp.concatenate([*shares, jnp.zeros((HD - sources, HD), jnp.float32)], axis=0).T
        mixture = None
        for z in range(sources):
            part = parts_ref[z, :own, at : at + HD].astype(jnp.float32) * shares[:, z : z + 1]
            mixture = part if mixture is None else mixture + part
        heads.append(mixture.astype(jnp.bfloat16))
    attended = jnp.concatenate(heads, axis=1)
    half = own_w_ref.shape[0] // 2
    for x_hi in range(2):
        for pair in range(half // 2):
            for w_ref, side in ((own_w_ref, core), (other_w_ref, 1 - core)):
                at = x_hi * half + pair * 2
                w = jnp.concatenate([w_ref[at], w_ref[at + 1]], axis=1)
                out_ref[x_hi * half + side * (half // 2) + pair] = dot(attended, w).astype(jnp.bfloat16)


def shards(tokens, w_query, w_keyvalue, cache_keys, cache_values, key_start, key_end, w_out):
    local_rows, width = tokens.shape[1:]
    cache_rows = cache_keys.shape[1]
    core = lax.axis_index("core").astype(jnp.int32).reshape(1)
    kv = lax.axis_index("kv").astype(jnp.int32)
    kv_count = lax.axis_size("kv")

    gathered = shared(tokens[0], HEAD)
    query_w = shared(w_query, ROWS).reshape(8, 256, width)
    pair_w = shared(w_keyvalue.reshape(-1, 2 * width), ROWS).reshape(8, 256, 2 * width)
    out_w = shared(w_out, ROWS)
    out_w_other = swapped(out_w)

    half_shape = jax.ShapeDtypeStruct((8, local_rows, width), jnp.bfloat16)
    keep, send = pl.pallas_call(
        normalize_kernel,
        out_shape=(half_shape, half_shape),
        in_specs=[SCALAR, WHOLE],
        out_specs=(WHOLE, WHOLE),
        compiler_params=VMEM,
        name="normalize",
    )(core, gathered)
    other = swapped(send)

    def project(w, name):
        shape = jax.ShapeDtypeStruct((local_rows, w.shape[2]), jnp.float32)
        mine, theirs = pl.pallas_call(
            project_kernel,
            out_shape=(shape, shape),
            in_specs=[WHOLE] * 3,
            out_specs=(WHOLE, WHOLE),
            compiler_params=VMEM,
            name=name,
        )(keep, other, w)
        return (mine + swapped(theirs)).astype(jnp.bfloat16)

    queries = shared(project(query_w, "project_queries"), "kv").reshape(-1, width)
    pair = project(pair_w, "project_pair")
    place = kv * cache_rows + lax.iota(jnp.int32, cache_rows)
    usable = (place >= key_start[0]) & (place < key_end[0])
    bias = jnp.broadcast_to(jnp.where(usable, 0.0, DEAD).astype(jnp.float32)[None], (8, cache_rows))

    blocks = QUERY_ROWS // local_rows
    padded = local_rows + STAT_ROWS
    parts = pl.pallas_call(
        attend_kernel,
        grid=(width // HD, queries.shape[0] // QUERY_ROWS),
        out_shape=jax.ShapeDtypeStruct((kv_count, padded, width), jnp.bfloat16),
        in_specs=[
            SCALAR,
            pl.BlockSpec((8, cache_rows), lambda h, i: (0, 0)),
            pl.BlockSpec((QUERY_ROWS, HD), lambda h, i: (i, h)),
            pl.BlockSpec((cache_rows, HD), lambda h, i: (0, h)),
            pl.BlockSpec((cache_rows, HD), lambda h, i: (0, h)),
            pl.BlockSpec((local_rows, HD), lambda h, i: (0, h)),
            pl.BlockSpec((local_rows, HD), lambda h, i: (0, h + width // HD)),
        ],
        out_specs=pl.BlockSpec((blocks, padded, HD), lambda h, i: (i, 0, h)),
        scratch_shapes=[pltpu.VMEM((QUERY_ROWS, cache_rows + local_rows), jnp.float32)],
        compiler_params=VMEM,
        name="attend",
    )(kv.reshape(1), bias, queries, cache_keys[0], cache_values[0], pair, pair)

    arrived = lax.all_to_all(parts, "kv", split_axis=0, concat_axis=0, tiled=True)
    columns = pl.pallas_call(
        finish_kernel,
        out_shape=jax.ShapeDtypeStruct((lax.axis_size(HEAD), local_rows, width), jnp.bfloat16),
        in_specs=[SCALAR, WHOLE, WHOLE, WHOLE],
        out_specs=WHOLE,
        compiler_params=VMEM,
        name="finish",
    )(core, arrived, out_w, out_w_other)
    columns = lax.all_to_all(columns, HEAD, split_axis=0, concat_axis=0, tiled=True)
    return columns.astype(jnp.float32).sum(axis=0).astype(jnp.bfloat16)[None]


def solution(mesh):
    section, head, kv = (mesh.shape[name] for name in ("section", "head", "kv"))
    torus = Mesh(
        mesh.devices.reshape(section // 2, 2, head // 2, 2, kv),
        ("x_hi", "core", "y", "x_lo", "kv"),
    )
    section = ("x_hi", "core")
    rows = ("x_hi", "core", "kv")
    return jax.shard_map(
        shards,
        mesh=torus,
        in_specs=(
            P(section, "kv", HEAD),
            P(rows, HEAD),
            P(rows, None, HEAD),
            P(section, "kv", HEAD),
            P(section, "kv", HEAD),
            P(section),
            P(section),
            P(HEAD, rows),
        ),
        out_specs=P(section, "kv", HEAD),
        check_vma=False,
    )
```

time: 284 us -> 265 us (0.933)
  the two profiles are of different devices: /device:TPU:16 before, /device:TPU:4 now
where the time goes in v1:
time: 265 us; the launch traced here: 264 us
  blocking collectives  109 us (41%)
  waiting for transfers between devices  94 us (35%)
  starting transfers between devices  31.2 us (12%)
  Pallas kernels  16.6 us (6%)
  local copies, waits for them, and re-layouts  10.5 us (4%)
    all_to_all x2, blocking collectives, shared(): return lax.all_to_all(copies, axes, split_axis=0, concat_axis=0, tiled=True)  73.3 us
    all_to_all x3, waiting for transfers between devices, shared(): return lax.all_to_all(copies, axes, split_axis=0, concat_axis=0, tiled=True)  71.7 us
    all_to_all x1, blocking collectives, shards(): lax.all_to_all(columns, HEAD, split_axis=0, concat_axis=0, tiled=True)  35.9 us
    all_to_all x3, starting transfers between devices, shared(): return lax.all_to_all(copies, axes, split_axis=0, concat_axis=0, tiled=True)  19.4 us
    all_to_all x1, waiting for transfers between devices, shards(): lax.all_to_all(parts, 'kv', split_axis=0, concat_axis=0, tiled=True)  19.3 us
    pallas_call x1, Pallas kernels, shards(): pl.pallas_call(attend_kernel, grid=(width // HD, queries.shape[0] // QUER...  13.4 us
    ppermute x4, starting transfers between devices, swapped(): return lax.ppermute(value, 'core', [(0, 1), (1, 0)])  8.28 us
    unnamed x25, local copies, waits for them, and re-layouts  5.79 us
  transfers between devices with their start and end apart: 8, of which 6 were waited for; matrix products, arithmetic and copies ran while one was open for 0% of the time, Pallas kernels for 6%

profile of v1, /device:TPU:4, one launch (start us, length us, event | category | flops | bytes accessed | tf_op | source)
XLA Modules:
  0.0 264.0 jit_solution(11617053239059574814)
XLA Ops:
  0.0 0.0 copy-start.10
  0.0 1.0 broadcast_in_dim.35
  1.0 36.3 %all_to_all.35.x_ref = bf16[16,128,256]{2,1,0:T(8,128)(2,1)} all-to-all(bf16[16,128,256]{2,1,0:T(8,128)(2,1)S(1)} %broadcast_in_dim.35), channel_id=1, replica_groups=mesh['x_hi'=2,'core'=2,'y'=8,'x_lo'=2,'kv'=8] {'y','x_lo'}, dimensions={0} | all-to-all | bytes 2097152 | tf_op jit(solution)/shard_map/all_to_all | solution.py:29
  37.3 0.0 copy-done.10
  37.3 0.0 copy-start.11
  37.3 0.1 broadcast_in_dim.36
  37.4 37.0 %all_to_all.36 = bf16[16,128,256]{2,1,0:T(8,128)(2,1)S(1)} all-to-all(bf16[16,128,256]{2,1,0:T(8,128)(2,1)S(1)} %broadcast_in_dim.36), channel_id=1, replica_groups=mesh['x_hi'=2,'core'=2,'y'=8,'x_lo'=2,'kv'=8] {'x_hi','kv'}, dimensions={0} | all-to-all | bytes 2097152 | tf_op jit(solution)/shard_map/all_to_all | solution.py:29
  74.4 0.0 copy-done.11
  74.4 0.0 copy-start.9
  74.4 1.2 broadcast_in_dim.39
  75.6 7.1 %all-to-all-start.5 = ((bf16[16,256,128]{2,1,0:T(8,128)(2,1)}), bf16[16,256,128]{2,1,0:T(8,128)(2,1)S(1)}, u32[]{:S(2)}, u32[]{:S(2)}) async-start(bf16[16,256,128]{2,1,0:T(8,128)(2,1)} %broadcast_in_dim.39), calls=%async_computation.5 | async-start | bytes 2097152 | tf_op jit(solution)/shard_map/all_to_all | solution.py:29
  82.7 0.0 copy-done.9
  82.8 24.6 %all-to-all-done.5.own_w_ref = bf16[16,256,128]{2,1,0:T(8,128)(2,1)S(1)} async-done(((bf16[16,256,128]{2,1,0:T(8,128)(2,1)}), bf16[16,256,128]{2,1,0:T(8,128)(2,1)S(1)}, u32[]{:S(2)}, u32[]{:S(2)}) %all-to-all-start.5) | async-done | bytes 1048608 | tf_op jit(solution)/shard_map/all_to_all | solution.py:29
  107.4 0.0 copy-start.1
  107.4 1.7 broadcast_in_dim.38
  109.0 0.0 copy-done.1
  109.0 7.2 %all-to-all-start.3 = ((bf16[16,128,512]{2,1,0:T(8,128)(2,1)}), bf16[16,128,512]{2,1,0:T(8,128)(2,1)S(1)}, u32[]{:S(2)}, u32[]{:S(2)}) async-start(bf16[16,128,512]{2,1,0:T(8,128)(2,1)} %broadcast_in_dim.38), calls=%async_computation.3 | async-start | bytes 4194304 | tf_op jit(solution)/shard_map/all_to_all | solution.py:29
  116.2 0.0 copy-start
  116.2 1.2 copy-done
  117.4 0.4 normalize.1
  117.8 0.0 copy-start.3
  117.8 1.9 collective-permute-start
  119.7 1.9 collective-permute-done.other_ref
  121.6 0.0 copy-start.5
  121.6 0.4 project_queries.1
  122.0 2.0 collective-permute-start.1
  124.1 1.2 collective-permute-done.1
  125.3 0.0 copy-done.3
  125.3 0.0 copy-done.5
  125.3 38.6 %all-to-all-done.3 = bf16[16,128,512]{2,1,0:T(8,128)(2,1)S(1)} async-done(((bf16[16,128,512]{2,1,0:T(8,128)(2,1)}), bf16[16,128,512]{2,1,0:T(8,128)(2,1)S(1)}, u32[]{:S(2)}, u32[]{:S(2)}) %all-to-all-start.3) | async-done | bytes 2097184 | tf_op jit(solution)/shard_map/all_to_all | solution.py:29
  164.0 0.8 broadcast_in_dim.37
  164.8 0.0 copy-start.2
  164.8 5.1 %all-to-all-start.2 = ((bf16[8,128,256]{2,1,0:T(8,128)(2,1)}), bf16[8,128,256]{2,1,0:T(8,128)(2,1)}, u32[]{:S(2)}, u32[]{:S(2)}) async-start(bf16[8,128,256]{2,1,0:T(8,128)(2,1)} %broadcast_in_dim.37), calls=%async_computation.2 | async-start | bytes 1048576 | tf_op jit(solution)/shard_map/all_to_all | solution.py:29
  169.9 0.0 copy-start.4
  169.9 1.0 copy-done.4
  171.0 0.0 copy-start.6
  171.0 1.0 copy-done.6
  172.0 1.4 project_pair.1
  173.4 1.9 collective-permute-start.2
  176.7 0.0 copy-done.2
  176.7 2.4 collective-permute-start.3
  179.1 0.0 collective-permute-done.2
  179.1 8.4 %all-to-all-done.2 = bf16[8,128,256]{2,1,0:T(8,128)(2,1)} async-done(((bf16[8,128,256]{2,1,0:T(8,128)(2,1)}), bf16[8,128,256]{2,1,0:T(8,128)(2,1)}, u32[]{:S(2)}, u32[]{:S(2)}) %all-to-all-start.2) | async-done | bytes 524320 | tf_op jit(solution)/shard_map/all_to_all | solution.py:29
  187.6 0.0 copy-start.7
  187.6 1.2 copy-done.7
  188.8 0.0 copy-start.8
  188.8 1.2 copy-done.8
  190.0 13.4 %attend.1 = bf16[8,144,256]{2,1,0:T(8,128)(2,1)} custom-call(s32[1]{0:T(128)} %bitcast.1.kv_ref, f32[8,2048]{1,0:T(8,128)S(1)} %broadcast_in_dim.34.bias_ref, bf16[1024,256]{1,0:T(8,128)(2,1)} %bitcast.6.q_ref, bf16[2048,256]{1,0:T(8,128)(2,1)S(1)} %bitcast.17, bf16[2048,256]{1,0:T(8,128)(2,1)S(1)} %bitcast.18, ...), custom_call_target="tpu_custom_call" | custom-call | tf_op jit(solution)/shard_map/attend/pallas_call | solution.py:190
  203.4 3.5 %all-to-all-start.4 = ((bf16[8,144,256]{2,1,0:T(8,128)(2,1)}), bf16[8,144,256]{2,1,0:T(8,128)(2,1)S(1)}, u32[]{:S(2)}, u32[]{:S(2)}) async-start(bf16[8,144,256]{2,1,0:T(8,128)(2,1)} %attend.1), calls=%async_computation.4 | async-start | bytes 1179648 | tf_op jit(solution)/shard_map/all_to_all | solution.py:209
  206.9 0.0 collective-permute-done.3.other_w_ref
  206.9 19.3 %all-to-all-done.4.parts_ref = bf16[8,144,256]{2,1,0:T(8,128)(2,1)S(1)} async-done(((bf16[8,144,256]{2,1,0:T(8,128)(2,1)}), bf16[8,144,256]{2,1,0:T(8,128)(2,1)S(1)}, u32[]{:S(2)}, u32[]{:S(2)}) %all-to-all-start.4) | async-done | bytes 589856 | tf_op jit(solution)/shard_map/all_to_all | solution.py:209
  226.2 1.1 finish.1
  227.3 35.9 %all_to_all.37 = bf16[16,128,256]{2,1,0:T(8,128)(2,1)S(1)} all-to-all(bf16[16,128,256]{2,1,0:T(8,128)(2,1)S(1)} %finish.1), channel_id=1, replica_groups=mesh['x_hi'=2,'core'=2,'y'=8,'x_lo'=2,'kv'=8] {'y','x_lo'}, dimensions={0} | all-to-all | bytes 2097152 | tf_op jit(solution)/shard_map/all_to_all | solution.py:218
  263.2 0.8 reduce_sum.12
  (5 shorter events, 0.1 us)
Async XLA Ops:
  0.0 37.3 %copy-start.10 = (bf16[128,256]{1,0:T(8,128)(2,1)S(1)}, bf16[128,256]{1,0:T(8,128)(2,1)}, u32[]{:S(2)}) copy-start(bf16[128,256]{1,0:T(8,128)(2,1)} %param.9) | copy-start | bytes 196612
  37.3 37.1 %copy-start.11 = (bf16[256,128]{1,0:T(8,128)(2,1)S(1)}, bf16[256,128]{1,0:T(8,128)(2,1)}, u32[]{:S(2)}) copy-start(bf16[256,128]{1,0:T(8,128)(2,1)} %param.15) | copy-start | bytes 196612
  74.4 8.3 %copy-start.9 = (bf16[128,2,256]{2,1,0:T(2,128)(2,1)S(1)}, bf16[128,2,256]{2,1,0:T(2,128)(2,1)}, u32[]{:S(2)}) copy-start(bf16[128,2,256]{2,1,0:T(2,128)(2,1)} %param.10) | copy-start | bytes 393220
  75.6 31.8 %all-to-all-start.5 = ((bf16[16,256,128]{2,1,0:T(8,128)(2,1)}), bf16[16,256,128]{2,1,0:T(8,128)(2,1)S(1)}, u32[]{:S(2)}, u32[]{:S(2)}) async-start(bf16[16,256,128]{2,1,0:T(8,128)(2,1)} %broadcast_in_dim.39), calls=%async_computation.5 | async-start | bytes 2097152 | tf_op jit(solution)/shard_map/all_to_all | solution.py:29
  107.4 1.7 copy-start.1
  109.0 54.9 %all-to-all-start.3 = ((bf16[16,128,512]{2,1,0:T(8,128)(2,1)}), bf16[16,128,512]{2,1,0:T(8,128)(2,1)S(1)}, u32[]{:S(2)}, u32[]{:S(2)}) async-start(bf16[16,128,512]{2,1,0:T(8,128)(2,1)} %broadcast_in_dim.38), calls=%async_computation.3 | async-start | bytes 4194304 | tf_op jit(solution)/shard_map/all_to_all | solution.py:29
  116.2 1.2 copy-start
  117.8 7.5 %copy-start.3 = (bf16[8,128,256]{2,1,0:T(8,128)(2,1)}, bf16[8,128,256]{2,1,0:T(8,128)(2,1)S(1)}, u32[]{:S(2)}) copy-start(bf16[8,128,256]{2,1,0:T(8,128)(2,1)S(1)} %get-tuple-element.11.own_ref) | copy-start | bytes 1572868
  117.8 3.8 %collective-permute-start = (bf16[8,128,256]{2,1,0:T(8,128)(2,1)S(1)}, bf16[8,128,256]{2,1,0:T(8,128)(2,1)S(1)}, u32[]{:S(2)}, u32[]{:S(2)}) collective-permute-start(bf16[8,128,256]{2,1,0:T(8,128)(2,1)S(1)} %get-tuple-element.12), channel_id=1, source_target_pairs={{0,128},{128,0},{1,129},{129,1},{2,130},{130,2},{3,131},{131,3},{4... | collective-permute-start | bytes 1572872 | tf_op jit(solution)/shard_map/ppermute | solution.py:33
  121.6 3.7 %copy-start.5 = (bf16[8,128,256]{2,1,0:T(8,128)(2,1)}, bf16[8,128,256]{2,1,0:T(8,128)(2,1)S(1)}, u32[]{:S(2)}) copy-start(bf16[8,128,256]{2,1,0:T(8,128)(2,1)S(1)} %collective-permute-done.other_ref) | copy-start | bytes 1572868
  122.0 3.2 %collective-permute-start.1 = (f32[128,256]{1,0:T(8,128)S(1)}, f32[128,256]{1,0:T(8,128)S(1)}, u32[]{:S(2)}, u32[]{:S(2)}) collective-permute-start(f32[128,256]{1,0:T(8,128)S(1)} %get-tuple-element.14), channel_id=1, source_target_pairs={{0,128},{128,0},{1,129},{129,1},{2,130},{130,2},{3,131},{131,3},{4... | collective-permute-start | bytes 393224 | tf_op jit(solution)/shard_map/ppermute | solution.py:33
  164.8 11.8 %copy-start.2 = (bf16[16,256,128]{2,1,0:T(8,128)(2,1)S(1)}, bf16[16,256,128]{2,1,0:T(8,128)(2,1)}, u32[]{:S(2)}) copy-start(bf16[16,256,128]{2,1,0:T(8,128)(2,1)} %copy-done.1) | copy-start | bytes 3145732
  164.8 22.8 %all-to-all-start.2 = ((bf16[8,128,256]{2,1,0:T(8,128)(2,1)}), bf16[8,128,256]{2,1,0:T(8,128)(2,1)}, u32[]{:S(2)}, u32[]{:S(2)}) async-start(bf16[8,128,256]{2,1,0:T(8,128)(2,1)} %broadcast_in_dim.37), calls=%async_computation.2 | async-start | bytes 1048576 | tf_op jit(solution)/shard_map/all_to_all | solution.py:29
  169.9 1.0 copy-start.4
  171.0 1.0 copy-start.6
  173.4 5.7 %collective-permute-start.2 = (f32[128,512]{1,0:T(8,128)}, f32[128,512]{1,0:T(8,128)S(1)}, u32[]{:S(2)}, u32[]{:S(2)}) collective-permute-start(f32[128,512]{1,0:T(8,128)} %get-tuple-element.16), channel_id=1, source_target_pairs={{0,128},{128,0},{1,129},{129,1},{2,130},{130,2},{3,131},{131,3},{4... | collective-permute-start | bytes 786440 | tf_op jit(solution)/shard_map/ppermute | solution.py:33
  176.7 30.3 %collective-permute-start.3 = (bf16[16,256,128]{2,1,0:T(8,128)(2,1)S(1)}, bf16[16,256,128]{2,1,0:T(8,128)(2,1)S(1)}, u32[]{:S(2)}, u32[]{:S(2)}) collective-permute-start(bf16[16,256,128]{2,1,0:T(8,128)(2,1)S(1)} %copy-done.2), channel_id=1, source_target_pairs={{0,128},{128,0},{1,129},{129,1},{2,130},{130,2},{3,131},{131,3},{4... | collective-permute-start | bytes 3145736 | tf_op jit(solution)/shard_map/ppermute | solution.py:33
  187.6 1.2 copy-start.7
  188.8 1.2 copy-start.8
  203.4 22.8 %all-to-all-start.4 = ((bf16[8,144,256]{2,1,0:T(8,128)(2,1)}), bf16[8,144,256]{2,1,0:T(8,128)(2,1)S(1)}, u32[]{:S(2)}, u32[]{:S(2)}) async-start(bf16[8,144,256]{2,1,0:T(8,128)(2,1)} %attend.1), calls=%async_computation.4 | async-start | bytes 1179648 | tf_op jit(solution)/shard_map/all_to_all | solution.py:209

commit v2 on v1

--- a/solution.py
+++ b/solution.py
@@ -8,7 +8,7 @@
 
 HD = 128
 HEAD = ("y", "x_lo")
-ROWS = ("x_hi", "kv")
+KV = ("z_4", "z_2", "z_1")
 STAT_ROWS = 16
 QUERY_ROWS = 512
 KEY_ROWS = 512
@@ -29,12 +29,12 @@
     return lax.all_to_all(copies, axes, split_axis=0, concat_axis=0, tiled=True)
 
 
-def swapped(value):
-    return lax.ppermute(value, "core", [(0, 1), (1, 0)])
-
-
-def normalize_kernel(core_ref, x_ref, keep_ref, send_ref):
-    core = core_ref[0]
+def swapped(value, axis):
+    return lax.ppermute(value, axis, [(0, 1), (1, 0)])
+
+
+def normalize_kernel(place_ref, x_ref, keep_ref, send_ref):
+    x_hi, core = place_ref[0], place_ref[1]
     blocks = x_ref.shape[0]
     squares = None
     for b in range(blocks):
@@ -42,22 +42,56 @@
         squares = x * x if squares is None else squares + x * x
     mean = jnp.sum(squares, axis=1, keepdims=True) / (blocks * x_ref.shape[2])
     factor = lax.rsqrt(mean + 1e-05)
-    for half in range(2):
+    for far in range(2):
+        half = 1 - x_hi if far else x_hi
         for j in range(4):
             for out_ref, side in ((keep_ref, core), (send_ref, 1 - core)):
                 x = x_ref[half * 8 + side * 4 + j].astype(jnp.float32)
-                out_ref[half * 4 + j] = (x * factor).astype(jnp.bfloat16)
-
-
-def project_kernel(own_ref, other_ref, w_ref, own_out, other_out):
-    rows = own_ref.shape[1]
+                out_ref[far, j] = (x * factor).astype(jnp.bfloat16)
+
+
+def project(place_ref, tiles, w_ref, far_w_ref, order):
+    kv = place_ref[2]
+    lanes = w_ref.shape[1]
+    near = pl.multiple_of((kv & 1) * lanes, lanes)
+    away = pl.multiple_of((1 - (kv & 1)) * lanes, lanes)
     total = None
-    for b in range(own_ref.shape[0]):
-        x = jnp.concatenate([own_ref[b], other_ref[b]], axis=0)
-        part = dot(x, w_ref[b])
-        total = part if total is None else total + part
-    own_out[...] = total[:rows]
-    other_out[...] = total[rows:]
+    for at in range(w_ref.shape[0]):
+        rows = order(at, kv)
+        for ref, lane in ((w_ref, near), (far_w_ref, away)):
+            x = jnp.concatenate([tile(rows, pl.ds(lane, lanes)) for tile in tiles], axis=0)
+            part = dot(x, ref[at])
+            total = part if total is None else total + part
+    return total
+
+
+def query_kernel(place_ref, keep_ref, other_ref, w_ref, far_w_ref, own_out, other_out):
+    def order(at, kv):
+        far, flip_4, flip_2 = at % 2, at // 2 % 2, at // 4
+        return far, (kv >> 1) ^ (2 * flip_4 + flip_2)
+
+    def tile(ref):
+        return lambda rows, lanes: ref[rows[0], rows[1], :, lanes]
+
+    total = project(place_ref, [tile(keep_ref), tile(other_ref)], w_ref, far_w_ref, order)
+    own_out[...] = total[: own_out.shape[0]]
+    other_out[...] = total[own_out.shape[0] :]
+
+
+def pair_kernel(place_ref, keep_ref, other_ref, far_ref, w_ref, far_w_ref, own_out, other_out):
+    def order(at, kv):
+        flip_4, flip_2 = at % 2, at // 2
+        return (kv >> 1) ^ (2 * flip_4 + flip_2)
+
+    def tile(ref, side):
+        return lambda rows, lanes: ref[side, rows, :, lanes]
+
+    tiles = [tile(keep_ref, 0), tile(far_ref, 0), tile(other_ref, 0), tile(far_ref, 1)]
+    total = project(place_ref, tiles, w_ref, far_w_ref, order)
+    rows = own_out.shape[1]
+    for n in range(2):
+        own_out[n] = total[n * rows : (n + 1) * rows]
+        other_out[n] = total[(n + 2) * rows : (n + 3) * rows]
 
 
 def thirds(value):
@@ -112,8 +146,8 @@
         out_ref[b, own:] = stats.astype(jnp.bfloat16)
 
 
-def finish_kernel(core_ref, parts_ref, own_w_ref, other_w_ref, out_ref):
-    core = core_ref[0]
+def finish_kernel(place_ref, parts_ref, w_ref, far_w_ref, swap_w_ref, swap_far_w_ref, out_ref):
+    x_hi, core, kv = place_ref[0], place_ref[1], place_ref[2]
     sources, rows, width = parts_ref.shape
     own = rows - STAT_ROWS
     heads = []
@@ -134,53 +168,61 @@
             mixture = part if mixture is None else mixture + part
         heads.append(mixture.astype(jnp.bfloat16))
     attended = jnp.concatenate(heads, axis=1)
-    half = own_w_ref.shape[0] // 2
-    for x_hi in range(2):
-        for pair in range(half // 2):
-            for w_ref, side in ((own_w_ref, core), (other_w_ref, 1 - core)):
-                at = x_hi * half + pair * 2
-                w = jnp.concatenate([w_ref[at], w_ref[at + 1]], axis=1)
-                out_ref[x_hi * half + side * (half // 2) + pair] = dot(attended, w).astype(jnp.bfloat16)
+    lanes = w_ref.shape[2]
+    near = pl.multiple_of((kv & 1) * lanes, lanes)
+    away = pl.multiple_of((1 - (kv & 1)) * lanes, lanes)
+    for at in range(w_ref.shape[0]):
+        far, flip_4, flip_2 = at % 2, at // 2 % 2, at // 4
+        section = 2 * (x_hi ^ far)
+        pair = (kv >> 1) ^ (2 * flip_4 + flip_2)
+        for near_ref, away_ref, side in ((w_ref, far_w_ref, core), (swap_w_ref, swap_far_w_ref, 1 - core)):
+            to = (section + side) * 4 + pair
+            for ref, lane in ((near_ref, near), (away_ref, away)):
+                out_ref[to, :, pl.ds(lane, lanes)] = dot(attended, ref[at]).astype(jnp.bfloat16)
+
+
+def doubled(value, axes):
+    for axis in axes[:-1]:
+        value = jnp.concatenate([value, swapped(value, axis)], axis=0)
+    return value, swapped(value, axes[-1])
 
 
 def shards(tokens, w_query, w_keyvalue, cache_keys, cache_values, key_start, key_end, w_out):
     local_rows, width = tokens.shape[1:]
     cache_rows = cache_keys.shape[1]
-    core = lax.axis_index("core").astype(jnp.int32).reshape(1)
-    kv = lax.axis_index("kv").astype(jnp.int32)
-    kv_count = lax.axis_size("kv")
-
-    gathered = shared(tokens[0], HEAD)
-    query_w = shared(w_query, ROWS).reshape(8, 256, width)
-    pair_w = shared(w_keyvalue.reshape(-1, 2 * width), ROWS).reshape(8, 256, 2 * width)
-    out_w = shared(w_out, ROWS)
-    out_w_other = swapped(out_w)
-
-    half_shape = jax.ShapeDtypeStruct((8, local_rows, width), jnp.bfloat16)
-    keep, send = pl.pallas_call(
-        normalize_kernel,
-        out_shape=(half_shape, half_shape),
-        in_specs=[SCALAR, WHOLE],
-        out_specs=(WHOLE, WHOLE),
-        compiler_params=VMEM,
-        name="normalize",
-    )(core, gathered)
-    other = swapped(send)
-
-    def project(w, name):
-        shape = jax.ShapeDtypeStruct((local_rows, w.shape[2]), jnp.float32)
-        mine, theirs = pl.pallas_call(
-            project_kernel,
-            out_shape=(shape, shape),
-            in_specs=[WHOLE] * 3,
-            out_specs=(WHOLE, WHOLE),
+    kv = lax.axis_index(KV).astype(jnp.int32)
+    kv_count = lax.axis_size(KV)
+    own = jnp.stack([lax.axis_index("x_hi"), lax.axis_index("core"), kv]).astype(jnp.int32)
+
+    def call(kernel, shapes, name, *operands):
+        return pl.pallas_call(
+            kernel,
+            out_shape=shapes,
+            in_specs=[SCALAR] + [WHOLE] * len(operands),
+            out_specs=jax.tree.map(lambda _: WHOLE, shapes),
             compiler_params=VMEM,
             name=name,
-        )(keep, other, w)
-        return (mine + swapped(theirs)).astype(jnp.bfloat16)
-
-    queries = shared(project(query_w, "project_queries"), "kv").reshape(-1, width)
-    pair = project(pair_w, "project_pair")
+        )(own, *operands)
+
+    gathered = shared(tokens[0], HEAD)
+    query_w = doubled(w_query[None], ("x_hi", *KV))
+    pair_w = doubled(w_keyvalue.reshape(1, -1, 2 * width), KV)
+    out_w = doubled(w_out[None], ("x_hi", *KV))
+    out_w = (*out_w, *(swapped(w, "core") for w in out_w))
+
+    half = jax.ShapeDtypeStruct((2, 4, local_rows, width), jnp.bfloat16)
+    keep, send = call(normalize_kernel, (half, half), "normalize", gathered)
+    other = swapped(send, "core")
+    partial = jax.ShapeDtypeStruct((local_rows, width), jnp.float32)
+    mine, theirs = call(query_kernel, (partial, partial), "project_queries", keep, other, *query_w)
+    queries = (mine + swapped(theirs, "core")).astype(jnp.bfloat16)
+    queries = shared(queries, KV).reshape(-1, width)
+
+    far = swapped(jnp.stack([keep[1], other[1]]), "x_hi")
+    partial = jax.ShapeDtypeStruct((2, local_rows, 2 * width), jnp.float32)
+    mine, theirs = call(pair_kernel, (partial, partial), "project_pair", keep, other, far, *pair_w)
+    mine = mine + swapped(theirs, "core")
+    pair = (mine[0] + swapped(mine[1], "x_hi")).astype(jnp.bfloat16)
     place = kv * cache_rows + lax.iota(jnp.int32, cache_rows)
     usable = (place >= key_start[0]) & (place < key_end[0])
     bias = jnp.broadcast_to(jnp.where(usable, 0.0, DEAD).astype(jnp.float32)[None], (8, cache_rows))
@@ -206,15 +248,9 @@
         name="attend",
     )(kv.reshape(1), bias, queries, cache_keys[0], cache_values[0], pair, pair)
 
-    arrived = lax.all_to_all(parts, "kv", split_axis=0, concat_axis=0, tiled=True)
-    columns = pl.pallas_call(
-        finish_kernel,
-        out_shape=jax.ShapeDtypeStruct((lax.axis_size(HEAD), local_rows, width), jnp.bfloat16),
-        in_specs=[SCALAR, WHOLE, WHOLE, WHOLE],
-        out_specs=WHOLE,
-        compiler_params=VMEM,
-        name="finish",
-    )(core, arrived, out_w, out_w_other)
+    arrived = lax.all_to_all(parts, KV, split_axis=0, concat_axis=0, tiled=True)
+    blocks = jax.ShapeDtypeStruct((lax.axis_size(HEAD), local_rows, width), jnp.bfloat16)
+    columns = call(finish_kernel, blocks, "finish", arrived, *out_w)
     columns = lax.all_to_all(columns, HEAD, split_axis=0, concat_axis=0, tiled=True)
     return columns.astype(jnp.float32).sum(axis=0).astype(jnp.bfloat16)[None]
 
@@ -222,24 +258,24 @@
 def solution(mesh):
     section, head, kv = (mesh.shape[name] for name in ("section", "head", "kv"))
     torus = Mesh(
-        mesh.devices.reshape(section // 2, 2, head // 2, 2, kv),
-        ("x_hi", "core", "y", "x_lo", "kv"),
+        mesh.devices.reshape(section // 2, 2, head // 2, 2, kv // 4, 2, 2),
+        ("x_hi", "core", "y", "x_lo", *KV),
     )
     section = ("x_hi", "core")
-    rows = ("x_hi", "core", "kv")
+    rows = (*section, *KV)
     return jax.shard_map(
         shards,
         mesh=torus,
         in_specs=(
-            P(section, "kv", HEAD),
+            P(section, KV, HEAD),
             P(rows, HEAD),
             P(rows, None, HEAD),
-            P(section, "kv", HEAD),
-            P(section, "kv", HEAD),
+            P(section, KV, HEAD),
+            P(section, KV, HEAD),
             P(section),
             P(section),
             P(HEAD, rows),
         ),
-        out_specs=P(section, "kv", HEAD),
+        out_specs=P(section, KV, HEAD),
         check_vma=False,
     )

time: 265 us -> 206 us (0.78)
  blocking collectives: 109 us -> 33.4 us
  starting transfers between devices: 31.2 us -> 91.3 us
  waiting for transfers between devices: 94 us -> 50.6 us
  local copies, waits for them, and re-layouts: 10.5 us -> 4.51 us
  other arithmetic: 0.83 us -> 3.96 us
    all_to_all x2 -> x0, blocking collectives: 73.3 us -> none  [shared(): return lax.all_to_all(copies, axes, split_axis=0, concat_axis=0, tiled=True)]
    all_to_all x3 -> x2, waiting for transfers between devices: 71.7 us -> 4.84 us  [shared(): return lax.all_to_all(copies, axes, split_axis=0, concat_axis=0, tiled=True)]
    ppermute x4 -> x18, starting transfers between devices: 8.28 us -> 73.5 us  [swapped(): return lax.ppermute(value, axis, [(0, 1), (1, 0)])]
    ppermute x4 -> x18, waiting for transfers between devices: 3.07 us -> 33.1 us  [swapped(): return lax.ppermute(value, axis, [(0, 1), (1, 0)])]
    all_to_all x3 -> x2, starting transfers between devices: 19.4 us -> 11.6 us  [shared(): return lax.all_to_all(copies, axes, split_axis=0, concat_axis=0, tiled=True)]
    all_to_all x1, waiting for transfers between devices: 19.3 us -> 12.7 us  [shards(): arrived = lax.all_to_all(parts, KV, split_axis=0, concat_axis=0, tiled=True)]
    unnamed x25 -> x14, local copies, waits for them, and re-layouts: 5.79 us -> 0.84 us
    pallas_call x4, Pallas kernels: 3.27 us -> 6.27 us  [call(): pl.pallas_call(kernel, out_shape=shapes, in_specs=[SCALAR] + [WHOLE] * le...]
  transfers between devices with their start and end apart: 8 -> 21, of which waited for: 6 -> 7; matrix products, arithmetic and copies ran while one was open for 0% -> 2% of each run, Pallas kernels for 6% -> 8%
where the time goes in v2:
time: 206 us; the launch traced here: 205 us
  starting transfers between devices  91.3 us (44%)
  waiting for transfers between devices  50.6 us (25%)
  blocking collectives  33.4 us (16%)
  Pallas kernels  19.1 us (9%)
  local copies, waits for them, and re-layouts  4.51 us (2%)
  other arithmetic  3.96 us (2%)
    ppermute x18, starting transfers between devices, swapped(): return lax.ppermute(value, axis, [(0, 1), (1, 0)])  73.5 us
    all_to_all x1, blocking collectives, shards(): lax.all_to_all(columns, HEAD, split_axis=0, concat_axis=0, tiled=True)  33.4 us
    ppermute x18, waiting for transfers between devices, swapped(): return lax.ppermute(value, axis, [(0, 1), (1, 0)])  33.1 us
    pallas_call x1, Pallas kernels, shards(): pl.pallas_call(attend_kernel, grid=(width // HD, queries.shape[0] // QUER...  12.9 us
    all_to_all x1, waiting for transfers between devices, shards(): arrived = lax.all_to_all(parts, KV, split_axis=0, concat_axis=0, tiled=True)  12.7 us
    all_to_all x2, starting transfers between devices, shared(): return lax.all_to_all(copies, axes, split_axis=0, concat_axis=0, tiled=True)  11.6 us
    pallas_call x4, Pallas kernels, call(): pl.pallas_call(kernel, out_shape=shapes, in_specs=[SCALAR] + [WHOLE] * le...  6.27 us
    all_to_all x1, starting transfers between devices, shards(): arrived = lax.all_to_all(parts, KV, split_axis=0, concat_axis=0, tiled=True)  6.17 us
  transfers between devices with their start and end apart: 21, of which 7 were waited for; matrix products, arithmetic and copies ran while one was open for 2% of the time, Pallas kernels for 8%

profile of v2, /device:TPU:4, one launch (start us, length us, event | category | flops | bytes accessed | tf_op | source)
XLA Modules:
  0.0 204.7 jit_solution(6239189588217798747)
XLA Ops:
  0.0 1.9 broadcast_in_dim.32
  1.9 8.0 %all-to-all-start = ((bf16[16,128,256]{2,1,0:T(8,128)(2,1)}), bf16[16,128,256]{2,1,0:T(8,128)(2,1)S(1)}, u32[]{:S(2)}, u32[]{:S(2)}) async-start(bf16[16,128,256]{2,1,0:T(8,128)(2,1)} %broadcast_in_dim.32), calls=%async_computation | async-start | bytes 2097152 | tf_op jit(solution)/shard_map/all_to_all | solution.py:29
  9.9 0.0 copy-done.3
  9.9 3.6 %collective-permute-start.1 = (bf16[1,128,256]{2,1,0:T(8,128)(2,1)S(1)}, bf16[1,128,256]{2,1,0:T(8,128)(2,1)S(1)}, u32[]{:S(2)}, u32[]{:S(2)}) collective-permute-start(bf16[1,128,256]{2,1,0:T(8,128)(2,1)S(1)} %bitcast.25), channel_id=1, source_target_pairs={{0,256},{256,0},{1,257},{257,1},{2,258},{258,2},{3,259},{259,3},{4... | collective-permute-start | bytes 196616 | tf_op jit(solution)/shard_map/ppermute | solution.py:33
  13.5 0.0 copy-done.5
  13.5 0.1 reshape.16
  13.6 10.1 %collective-permute-start.7 = (bf16[1,128,512]{2,1,0:T(8,128)(2,1)S(1)}, bf16[1,128,512]{2,1,0:T(8,128)(2,1)S(1)}, u32[]{:S(2)}, u32[]{:S(2)}) collective-permute-start(bf16[1,128,512]{2,1,0:T(8,128)(2,1)S(1)} %reshape.16), channel_id=1, source_target_pairs={{0,4},{4,0},{1,5},{5,1},{2,6},{6,2},{3,7},{7,3},{8,12},{12,8},{9,1... | collective-permute-start | bytes 393224 | tf_op jit(solution)/shard_map/ppermute | solution.py:33
  23.7 0.0 collective-permute-done.1
  23.7 4.9 %collective-permute-start.2 = (bf16[2,128,256]{2,1,0:T(8,128)(2,1)S(1)}, bf16[2,128,256]{2,1,0:T(8,128)(2,1)S(1)}, u32[]{:S(2)}, u32[]{:S(2)}) collective-permute-start(bf16[2,128,256]{2,1,0:T(8,128)(2,1)S(1)} %pad_maximum_fusion.6), channel_id=1, source_target_pairs={{0,4},{4,0},{1,5},{5,1},{2,6},{6,2},{3,7},{7,3},{8,12},{12,8},{9,1... | collective-permute-start | bytes 393224 | tf_op jit(solution)/shard_map/ppermute | solution.py:33
  28.6 0.1 pad_add_fusion.place_ref
  28.7 0.4 collective-permute-done.7
  29.1 4.7 %collective-permute-start.8 = (bf16[2,128,512]{2,1,0:T(8,128)(2,1)S(1)}, bf16[2,128,512]{2,1,0:T(8,128)(2,1)S(1)}, u32[]{:S(2)}, u32[]{:S(2)}) collective-permute-start(bf16[2,128,512]{2,1,0:T(8,128)(2,1)S(1)} %pad_maximum_fusion.4), channel_id=1, source_target_pairs={{0,2},{2,0},{1,3},{3,1},{4,6},{6,4},{5,7},{7,5},{8,10},{10,8},{9,1... | collective-permute-start | bytes 786440 | tf_op jit(solution)/shard_map/ppermute | solution.py:33
  33.8 4.8 %all-to-all-done.x_ref = bf16[16,128,256]{2,1,0:T(8,128)(2,1)S(1)} async-done(((bf16[16,128,256]{2,1,0:T(8,128)(2,1)}), bf16[16,128,256]{2,1,0:T(8,128)(2,1)S(1)}, u32[]{:S(2)}, u32[]{:S(2)}) %all-to-all-start) | async-done | bytes 1048608 | tf_op jit(solution)/shard_map/all_to_all | solution.py:29
  38.6 0.9 normalize.1
  39.6 1.9 collective-permute-start
  41.5 0.0 collective-permute-done.2
  41.5 6.1 %collective-permute-start.3 = (bf16[4,128,256]{2,1,0:T(8,128)(2,1)S(1)}, bf16[4,128,256]{2,1,0:T(8,128)(2,1)S(1)}, u32[]{:S(2)}, u32[]{:S(2)}) collective-permute-start(bf16[4,128,256]{2,1,0:T(8,128)(2,1)S(1)} %pad_maximum_fusion.3), channel_id=1, source_target_pairs={{0,2},{2,0},{1,3},{3,1},{4,6},{6,4},{5,7},{7,5},{8,10},{10,8},{9,1... | collective-permute-start | bytes 786440 | tf_op jit(solution)/shard_map/ppermute | solution.py:33
  47.7 0.0 collective-permute-done.8
  47.7 4.3 %collective-permute-start.9 = (bf16[4,128,512]{2,1,0:T(8,128)(2,1)S(1)}, bf16[4,128,512]{2,1,0:T(8,128)(2,1)S(1)}, u32[]{:S(2)}, u32[]{:S(2)}) collective-permute-start(bf16[4,128,512]{2,1,0:T(8,128)(2,1)S(1)} %constant_dynamic-update-slice_fusion.w_ref), channel_id=1, source_target_pairs={{0,1},{1,0},{2,3},{3,2},{4,5},{5,4},{6,7},{7,6},{8,9},{9,8},{10,11... | collective-permute-start | bytes 1572872 | tf_op jit(solution)/shard_map/ppermute | solution.py:33
  52.0 8.3 %collective-permute-done.3 = bf16[4,128,256]{2,1,0:T(8,128)(2,1)S(1)} collective-permute-done((bf16[4,128,256]{2,1,0:T(8,128)(2,1)S(1)}, bf16[4,128,256]{2,1,0:T(8,128)(2,1)S(1)}, u32[]{:S(2)}, u32[]{:S(2)}) %collective-permute-start.3) | collective-permute-done | bytes 262176 | tf_op jit(solution)/shard_map/ppermute | solution.py:33
  60.3 0.1 pad_maximum_fusion.w_ref
  60.4 2.6 %collective-permute-start.4 = (bf16[8,128,256]{2,1,0:T(8,128)(2,1)S(1)}, bf16[8,128,256]{2,1,0:T(8,128)(2,1)S(1)}, u32[]{:S(2)}, u32[]{:S(2)}) collective-permute-start(bf16[8,128,256]{2,1,0:T(8,128)(2,1)S(1)} %pad_maximum_fusion.w_ref), channel_id=1, source_target_pairs={{0,1},{1,0},{2,3},{3,2},{4,5},{5,4},{6,7},{7,6},{8,9},{9,8},{10,11... | collective-permute-start | bytes 1572872 | tf_op jit(solution)/shard_map/ppermute | solution.py:33
  63.0 0.0 collective-permute-done.other_ref
  63.0 0.0 copy-start.4
  63.0 0.1 pad_maximum_fusion.1
  63.1 2.7 %collective-permute-start.6 = (bf16[2,4,128,256]{3,2,1,0:T(8,128)(2,1)S(1)}, bf16[2,4,128,256]{3,2,1,0:T(8,128)(2,1)S(1)}, u32[]{:S(2)}, u32[]{:S(2)}) collective-permute-start(bf16[2,4,128,256]{3,2,1,0:T(8,128)(2,1)S(1)} %pad_maximum_fusion.1), channel_id=1, source_target_pairs={{0,256},{256,0},{1,257},{257,1},{2,258},{258,2},{3,259},{259,3},{4... | collective-permute-start | bytes 1572872 | tf_op jit(solution)/shard_map/ppermute | solution.py:33
  65.8 4.6 %collective-permute-start.12 = (bf16[1,256,128]{2,1,0:T(8,128)(2,1)S(1)}, bf16[1,256,128]{2,1,0:T(8,128)(2,1)S(1)}, u32[]{:S(2)}, u32[]{:S(2)}) collective-permute-start(bf16[1,256,128]{2,1,0:T(8,128)(2,1)S(1)} %bitcast.29), channel_id=1, source_target_pairs={{0,256},{256,0},{1,257},{257,1},{2,258},{258,2},{3,259},{259,3},{4... | collective-permute-start | bytes 196616 | tf_op jit(solution)/shard_map/ppermute | solution.py:33
  70.5 8.8 %collective-permute-done.4.far_w_ref = bf16[8,128,256]{2,1,0:T(8,128)(2,1)S(1)} collective-permute-done((bf16[8,128,256]{2,1,0:T(8,128)(2,1)S(1)}, bf16[8,128,256]{2,1,0:T(8,128)(2,1)S(1)}, u32[]{:S(2)}, u32[]{:S(2)}) %collective-permute-start.4) | collective-permute-done | bytes 524320 | tf_op jit(solution)/shard_map/ppermute | solution.py:33
  79.2 1.2 project_queries.1
  80.5 1.9 collective-permute-start.5
  82.4 0.0 collective-permute-done.9.far_w_ref
  82.4 0.0 collective-permute-done.6.far_ref
  82.4 1.8 project_pair.1
  84.2 2.4 %collective-permute-start.10 = (f32[2,128,512]{2,1,0:T(8,128)S(1)}, f32[2,128,512]{2,1,0:T(8,128)S(1)}, u32[]{:S(2)}, u32[]{:S(2)}) collective-permute-start(f32[2,128,512]{2,1,0:T(8,128)S(1)} %get-tuple-element.16), channel_id=1, source_target_pairs={{0,128},{128,0},{1,129},{129,1},{2,130},{130,2},{3,131},{131,3},{4... | collective-permute-start | bytes 1572872 | tf_op jit(solution)/shard_map/ppermute | solution.py:33
  86.6 0.0 collective-permute-done.12
  86.6 9.4 %collective-permute-start.13 = (bf16[2,256,128]{2,1,0:T(8,128)(2,1)S(1)}, bf16[2,256,128]{2,1,0:T(8,128)(2,1)S(1)}, u32[]{:S(2)}, u32[]{:S(2)}) collective-permute-start(bf16[2,256,128]{2,1,0:T(8,128)(2,1)S(1)} %pad_maximum_fusion.7), channel_id=1, source_target_pairs={{0,4},{4,0},{1,5},{5,1},{2,6},{6,2},{3,7},{7,3},{8,12},{12,8},{9,1... | collective-permute-start | bytes 393224 | tf_op jit(solution)/shard_map/ppermute | solution.py:33
  96.0 0.0 collective-permute-done.5
  96.0 0.9 broadcast_in_dim.34
  96.9 3.6 %all-to-all-start.1 = ((bf16[8,128,256]{2,1,0:T(8,128)(2,1)}), bf16[8,128,256]{2,1,0:T(8,128)(2,1)S(1)}, u32[]{:S(2)}, u32[]{:S(2)}) async-start(bf16[8,128,256]{2,1,0:T(8,128)(2,1)} %broadcast_in_dim.34), calls=%async_computation.1 | async-start | bytes 1048576 | tf_op jit(solution)/shard_map/all_to_all | solution.py:29
  100.5 0.0 collective-permute-done.13
  100.5 0.7 pad_maximum_fusion.5
  101.3 5.5 %collective-permute-start.14 = (bf16[4,256,128]{2,1,0:T(8,128)(2,1)}, bf16[4,256,128]{2,1,0:T(8,128)(2,1)}, u32[]{:S(2)}, u32[]{:S(2)}) collective-permute-start(bf16[4,256,128]{2,1,0:T(8,128)(2,1)} %pad_maximum_fusion.5), channel_id=1, source_target_pairs={{0,2},{2,0},{1,3},{3,1},{4,6},{6,4},{5,7},{7,5},{8,10},{10,8},{9,1... | collective-permute-start | bytes 786440 | tf_op jit(solution)/shard_map/ppermute | solution.py:33
  106.8 0.0 collective-permute-done.10
  106.8 0.1 add.30
  106.9 0.8 copy-done.2
  107.7 0.7 slice_bitcast_fusion
  108.4 2.7 %collective-permute-start.11 = (f32[128,512]{1,0:T(8,128)}, f32[128,512]{1,0:T(8,128)}, u32[]{:S(2)}, u32[]{:S(2)}) collective-permute-start(f32[128,512]{1,0:T(8,128)} %slice_bitcast_fusion), channel_id=1, source_target_pairs={{0,256},{256,0},{1,257},{257,1},{2,258},{258,2},{3,259},{259,3},{4... | collective-permute-start | bytes 786440 | tf_op jit(solution)/shard_map/ppermute | solution.py:33
  112.4 13.9 %collective-permute-done.14 = bf16[4,256,128]{2,1,0:T(8,128)(2,1)} collective-permute-done((bf16[4,256,128]{2,1,0:T(8,128)(2,1)}, bf16[4,256,128]{2,1,0:T(8,128)(2,1)}, u32[]{:S(2)}, u32[]{:S(2)}) %collective-permute-start.14) | collective-permute-done | bytes 262176 | tf_op jit(solution)/shard_map/ppermute | solution.py:33
  126.3 1.0 pad_maximum_fusion.2.w_ref
  127.3 1.9 collective-permute-start.15
  129.3 0.0 collective-permute-done.11
  129.3 1.1 fusion.1.new_k_ref.new_v_ref
  130.3 0.0 all-to-all-done.1
  130.4 12.9 %attend.1 = bf16[8,144,256]{2,1,0:T(8,128)(2,1)} custom-call(s32[1]{0:T(128)} %bitcast.2.kv_ref, f32[8,2048]{1,0:T(8,128)S(1)} %broadcast_in_dim.31.bias_ref, bf16[1024,256]{1,0:T(8,128)(2,1)S(1)} %bitcast.22, bf16[2048,256]{1,0:T(8,128)(2,1)S(1)} %bitcast.23, bf16[2048,256]{1,0:T(8,128)(2,1)S(1)} %bitcast.24, ...), custom_call_target="tpu_custom_call" | custom-call | tf_op jit(solution)/shard_map/attend/pallas_call | solution.py:232
  143.2 6.2 %all-to-all-start.2 = ((bf16[8,144,256]{2,1,0:T(8,128)(2,1)}), bf16[8,144,256]{2,1,0:T(8,128)(2,1)S(1)}, u32[]{:S(2)}, u32[]{:S(2)}) async-start(bf16[8,144,256]{2,1,0:T(8,128)(2,1)} %attend.1), calls=%async_computation.2 | async-start | bytes 1179648 | tf_op jit(solution)/shard_map/all_to_all | solution.py:251
  149.4 1.9 collective-permute-start.16
  151.3 0.0 collective-permute-done.15.far_w_ref
  151.3 2.4 %collective-permute-start.17 = (bf16[8,256,128]{2,1,0:T(8,128)(2,1)}, bf16[8,256,128]{2,1,0:T(8,128)(2,1)S(1)}, u32[]{:S(2)}, u32[]{:S(2)}) collective-permute-start(bf16[8,256,128]{2,1,0:T(8,128)(2,1)} %collective-permute-done.15.far_w_ref), channel_id=1, source_target_pairs={{0,128},{128,0},{1,129},{129,1},{2,130},{130,2},{3,131},{131,3},{4... | collective-permute-start | bytes 1572872 | tf_op jit(solution)/shard_map/ppermute | solution.py:33
  153.7 0.0 collective-permute-done.16.swap_w_ref
  153.8 1.7 collective-permute-done.17.swap_far_w_ref
  155.5 12.7 %all-to-all-done.2.parts_ref = bf16[8,144,256]{2,1,0:T(8,128)(2,1)S(1)} async-done(((bf16[8,144,256]{2,1,0:T(8,128)(2,1)}), bf16[8,144,256]{2,1,0:T(8,128)(2,1)S(1)}, u32[]{:S(2)}, u32[]{:S(2)}) %all-to-all-start.2) | async-done | bytes 589856 | tf_op jit(solution)/shard_map/all_to_all | solution.py:251
  168.1 2.4 %finish.1 = bf16[16,128,256]{2,1,0:T(8,128)(2,1)S(1)} custom-call(s32[3]{0:T(128)S(1)} %pad_add_fusion.place_ref, bf16[8,144,256]{2,1,0:T(8,128)(2,1)S(1)} %all-to-all-done.2.parts_ref, bf16[8,256,128]{2,1,0:T(8,128)(2,1)S(1)} %pad_maximum_fusion.2.w_ref, bf16[8,256,128]{2,1,0:T(8,128)(2,1)} %collective-permute-done.15.far_w_ref, ...), custom_call_target="tpu_custom_call" | custom-call | tf_op jit(solution)/shard_map/finish/pallas_call | solution.py:198
  170.5 33.4 %all_to_all.20 = bf16[16,128,256]{2,1,0:T(8,128)(2,1)S(1)} all-to-all(bf16[16,128,256]{2,1,0:T(8,128)(2,1)S(1)} %finish.1), channel_id=1, replica_groups=mesh['x_hi'=2,'core'=2,'y'=8,'x_lo'=2,'z_4'=2,'z_2'=2,'z_1'=2] {'y','x_lo'}, dimensions={0} | all-to-all | bytes 2097152 | tf_op jit(solution)/shard_map/all_to_all | solution.py:254
  203.9 0.8 reduce_sum.12
  (20 shorter events, 0.2 us)
Async XLA Ops:
  1.9 8.0 %copy-start.3 = (bf16[128,256]{1,0:T(8,128)(2,1)S(1)}, bf16[128,256]{1,0:T(8,128)(2,1)}, u32[]{:S(2)}) copy-start(bf16[128,256]{1,0:T(8,128)(2,1)} %param.9) | copy-start | bytes 196612
  1.9 11.6 %copy-start.5 = (bf16[128,2,256]{2,1,0:T(2,128)(2,1)S(1)}, bf16[128,2,256]{2,1,0:T(2,128)(2,1)}, u32[]{:S(2)}) copy-start(bf16[128,2,256]{2,1,0:T(2,128)(2,1)} %param.10) | copy-start | bytes 393220
  1.9 36.7 %all-to-all-start = ((bf16[16,128,256]{2,1,0:T(8,128)(2,1)}), bf16[16,128,256]{2,1,0:T(8,128)(2,1)S(1)}, u32[]{:S(2)}, u32[]{:S(2)}) async-start(bf16[16,128,256]{2,1,0:T(8,128)(2,1)} %broadcast_in_dim.32), calls=%async_computation | async-start | bytes 2097152 | tf_op jit(solution)/shard_map/all_to_all | solution.py:29
  9.9 13.8 %collective-permute-start.1 = (bf16[1,128,256]{2,1,0:T(8,128)(2,1)S(1)}, bf16[1,128,256]{2,1,0:T(8,128)(2,1)S(1)}, u32[]{:S(2)}, u32[]{:S(2)}) collective-permute-start(bf16[1,128,256]{2,1,0:T(8,128)(2,1)S(1)} %bitcast.25), channel_id=1, source_target_pairs={{0,256},{256,0},{1,257},{257,1},{2,258},{258,2},{3,259},{259,3},{4... | collective-permute-start | bytes 196616 | tf_op jit(solution)/shard_map/ppermute | solution.py:33
  13.6 15.5 %collective-permute-start.7 = (bf16[1,128,512]{2,1,0:T(8,128)(2,1)S(1)}, bf16[1,128,512]{2,1,0:T(8,128)(2,1)S(1)}, u32[]{:S(2)}, u32[]{:S(2)}) collective-permute-start(bf16[1,128,512]{2,1,0:T(8,128)(2,1)S(1)} %reshape.16), channel_id=1, source_target_pairs={{0,4},{4,0},{1,5},{5,1},{2,6},{6,2},{3,7},{7,3},{8,12},{12,8},{9,1... | collective-permute-start | bytes 393224 | tf_op jit(solution)/shard_map/ppermute | solution.py:33
  23.7 17.8 %collective-permute-start.2 = (bf16[2,128,256]{2,1,0:T(8,128)(2,1)S(1)}, bf16[2,128,256]{2,1,0:T(8,128)(2,1)S(1)}, u32[]{:S(2)}, u32[]{:S(2)}) collective-permute-start(bf16[2,128,256]{2,1,0:T(8,128)(2,1)S(1)} %pad_maximum_fusion.6), channel_id=1, source_target_pairs={{0,4},{4,0},{1,5},{5,1},{2,6},{6,2},{3,7},{7,3},{8,12},{12,8},{9,1... | collective-permute-start | bytes 393224 | tf_op jit(solution)/shard_map/ppermute | solution.py:33
  29.1 18.6 %collective-permute-start.8 = (bf16[2,128,512]{2,1,0:T(8,128)(2,1)S(1)}, bf16[2,128,512]{2,1,0:T(8,128)(2,1)S(1)}, u32[]{:S(2)}, u32[]{:S(2)}) collective-permute-start(bf16[2,128,512]{2,1,0:T(8,128)(2,1)S(1)} %pad_maximum_fusion.4), channel_id=1, source_target_pairs={{0,2},{2,0},{1,3},{3,1},{4,6},{6,4},{5,7},{7,5},{8,10},{10,8},{9,1... | collective-permute-start | bytes 786440 | tf_op jit(solution)/shard_map/ppermute | solution.py:33
  39.6 23.4 %collective-permute-start = (bf16[2,4,128,256]{3,2,1,0:T(8,128)(2,1)S(1)}, bf16[2,4,128,256]{3,2,1,0:T(8,128)(2,1)S(1)}, u32[]{:S(2)}, u32[]{:S(2)}) collective-permute-start(bf16[2,4,128,256]{3,2,1,0:T(8,128)(2,1)S(1)} %get-tuple-element.12), channel_id=1, source_target_pairs={{0,128},{128,0},{1,129},{129,1},{2,130},{130,2},{3,131},{131,3},{4... | collective-permute-start | bytes 1572872 | tf_op jit(solution)/shard_map/ppermute | solution.py:33
  41.5 18.8 %collective-permute-start.3 = (bf16[4,128,256]{2,1,0:T(8,128)(2,1)S(1)}, bf16[4,128,256]{2,1,0:T(8,128)(2,1)S(1)}, u32[]{:S(2)}, u32[]{:S(2)}) collective-permute-start(bf16[4,128,256]{2,1,0:T(8,128)(2,1)S(1)} %pad_maximum_fusion.3), channel_id=1, source_target_pairs={{0,2},{2,0},{1,3},{3,1},{4,6},{6,4},{5,7},{7,5},{8,10},{10,8},{9,1... | collective-permute-start | bytes 786440 | tf_op jit(solution)/shard_map/ppermute | solution.py:33
  47.7 34.7 %collective-permute-start.9 = (bf16[4,128,512]{2,1,0:T(8,128)(2,1)S(1)}, bf16[4,128,512]{2,1,0:T(8,128)(2,1)S(1)}, u32[]{:S(2)}, u32[]{:S(2)}) collective-permute-start(bf16[4,128,512]{2,1,0:T(8,128)(2,1)S(1)} %constant_dynamic-update-slice_fusion.w_ref), channel_id=1, source_target_pairs={{0,1},{1,0},{2,3},{3,2},{4,5},{5,4},{6,7},{7,6},{8,9},{9,8},{10,11... | collective-permute-start | bytes 1572872 | tf_op jit(solution)/shard_map/ppermute | solution.py:33
  60.4 18.9 %collective-permute-start.4 = (bf16[8,128,256]{2,1,0:T(8,128)(2,1)S(1)}, bf16[8,128,256]{2,1,0:T(8,128)(2,1)S(1)}, u32[]{:S(2)}, u32[]{:S(2)}) collective-permute-start(bf16[8,128,256]{2,1,0:T(8,128)(2,1)S(1)} %pad_maximum_fusion.w_ref), channel_id=1, source_target_pairs={{0,1},{1,0},{2,3},{3,2},{4,5},{5,4},{6,7},{7,6},{8,9},{9,8},{10,11... | collective-permute-start | bytes 1572872 | tf_op jit(solution)/shard_map/ppermute | solution.py:33
  63.0 2.8 %copy-start.4 = (bf16[256,128]{1,0:T(8,128)(2,1)S(1)}, bf16[256,128]{1,0:T(8,128)(2,1)}, u32[]{:S(2)}) copy-start(bf16[256,128]{1,0:T(8,128)(2,1)} %param.15) | copy-start | bytes 196612
  63.1 19.3 %collective-permute-start.6 = (bf16[2,4,128,256]{3,2,1,0:T(8,128)(2,1)S(1)}, bf16[2,4,128,256]{3,2,1,0:T(8,128)(2,1)S(1)}, u32[]{:S(2)}, u32[]{:S(2)}) collective-permute-start(bf16[2,4,128,256]{3,2,1,0:T(8,128)(2,1)S(1)} %pad_maximum_fusion.1), channel_id=1, source_target_pairs={{0,256},{256,0},{1,257},{257,1},{2,258},{258,2},{3,259},{259,3},{4... | collective-permute-start | bytes 1572872 | tf_op jit(solution)/shard_map/ppermute | solution.py:33
  65.8 20.8 %collective-permute-start.12 = (bf16[1,256,128]{2,1,0:T(8,128)(2,1)S(1)}, bf16[1,256,128]{2,1,0:T(8,128)(2,1)S(1)}, u32[]{:S(2)}, u32[]{:S(2)}) collective-permute-start(bf16[1,256,128]{2,1,0:T(8,128)(2,1)S(1)} %bitcast.29), channel_id=1, source_target_pairs={{0,256},{256,0},{1,257},{257,1},{2,258},{258,2},{3,259},{259,3},{4... | collective-permute-start | bytes 196616 | tf_op jit(solution)/shard_map/ppermute | solution.py:33
  80.5 15.6 %collective-permute-start.5 = (f32[128,256]{1,0:T(8,128)S(1)}, f32[128,256]{1,0:T(8,128)S(1)}, u32[]{:S(2)}, u32[]{:S(2)}) collective-permute-start(f32[128,256]{1,0:T(8,128)S(1)} %get-tuple-element.14), channel_id=1, source_target_pairs={{0,128},{128,0},{1,129},{129,1},{2,130},{130,2},{3,131},{131,3},{4... | collective-permute-start | bytes 393224 | tf_op jit(solution)/shard_map/ppermute | solution.py:33
  84.2 22.6 %collective-permute-start.10 = (f32[2,128,512]{2,1,0:T(8,128)S(1)}, f32[2,128,512]{2,1,0:T(8,128)S(1)}, u32[]{:S(2)}, u32[]{:S(2)}) collective-permute-start(f32[2,128,512]{2,1,0:T(8,128)S(1)} %get-tuple-element.16), channel_id=1, source_target_pairs={{0,128},{128,0},{1,129},{129,1},{2,130},{130,2},{3,131},{131,3},{4... | collective-permute-start | bytes 1572872 | tf_op jit(solution)/shard_map/ppermute | solution.py:33
  86.6 13.9 %collective-permute-start.13 = (bf16[2,256,128]{2,1,0:T(8,128)(2,1)S(1)}, bf16[2,256,128]{2,1,0:T(8,128)(2,1)S(1)}, u32[]{:S(2)}, u32[]{:S(2)}) collective-permute-start(bf16[2,256,128]{2,1,0:T(8,128)(2,1)S(1)} %pad_maximum_fusion.7), channel_id=1, source_target_pairs={{0,4},{4,0},{1,5},{5,1},{2,6},{6,2},{3,7},{7,3},{8,12},{12,8},{9,1... | collective-permute-start | bytes 393224 | tf_op jit(solution)/shard_map/ppermute | solution.py:33
  96.9 33.4 %all-to-all-start.1 = ((bf16[8,128,256]{2,1,0:T(8,128)(2,1)}), bf16[8,128,256]{2,1,0:T(8,128)(2,1)S(1)}, u32[]{:S(2)}, u32[]{:S(2)}) async-start(bf16[8,128,256]{2,1,0:T(8,128)(2,1)} %broadcast_in_dim.34), calls=%async_computation.1 | async-start | bytes 1048576 | tf_op jit(solution)/shard_map/all_to_all | solution.py:29
  101.3 25.0 %collective-permute-start.14 = (bf16[4,256,128]{2,1,0:T(8,128)(2,1)}, bf16[4,256,128]{2,1,0:T(8,128)(2,1)}, u32[]{:S(2)}, u32[]{:S(2)}) collective-permute-start(bf16[4,256,128]{2,1,0:T(8,128)(2,1)} %pad_maximum_fusion.5), channel_id=1, source_target_pairs={{0,2},{2,0},{1,3},{3,1},{4,6},{6,4},{5,7},{7,5},{8,10},{10,8},{9,1... | collective-permute-start | bytes 786440 | tf_op jit(solution)/shard_map/ppermute | solution.py:33
  106.9 0.8 copy-start.2
  107.7 22.7 %copy-start = (bf16[1,2048,256]{2,1,0:T(8,128)(2,1)S(1)}, bf16[1,2048,256]{2,1,0:T(8,128)(2,1)}, u32[]{:S(2)}) copy-start(bf16[1,2048,256]{2,1,0:T(8,128)(2,1)} %param.11) | copy-start | bytes 3145732
  107.7 22.7 %copy-start.1 = (bf16[1,2048,256]{2,1,0:T(8,128)(2,1)S(1)}, bf16[1,2048,256]{2,1,0:T(8,128)(2,1)}, u32[]{:S(2)}) copy-start(bf16[1,2048,256]{2,1,0:T(8,128)(2,1)} %param.12) | copy-start | bytes 3145732
  108.4 20.8 %collective-permute-start.11 = (f32[128,512]{1,0:T(8,128)}, f32[128,512]{1,0:T(8,128)}, u32[]{:S(2)}, u32[]{:S(2)}) collective-permute-start(f32[128,512]{1,0:T(8,128)} %slice_bitcast_fusion), channel_id=1, source_target_pairs={{0,256},{256,0},{1,257},{257,1},{2,258},{258,2},{3,259},{259,3},{4... | collective-permute-start | bytes 786440 | tf_op jit(solution)/shard_map/ppermute | solution.py:33
  127.3 24.0 %collective-permute-start.15 = (bf16[8,256,128]{2,1,0:T(8,128)(2,1)S(1)}, bf16[8,256,128]{2,1,0:T(8,128)(2,1)}, u32[]{:S(2)}, u32[]{:S(2)}) collective-permute-start(bf16[8,256,128]{2,1,0:T(8,128)(2,1)S(1)} %pad_maximum_fusion.2.w_ref), channel_id=1, source_target_pairs={{0,1},{1,0},{2,3},{3,2},{4,5},{5,4},{6,7},{7,6},{8,9},{9,8},{10,11... | collective-permute-start | bytes 1572872 | tf_op jit(solution)/shard_map/ppermute | solution.py:33
  143.2 24.9 %all-to-all-start.2 = ((bf16[8,144,256]{2,1,0:T(8,128)(2,1)}), bf16[8,144,256]{2,1,0:T(8,128)(2,1)S(1)}, u32[]{:S(2)}, u32[]{:S(2)}) async-start(bf16[8,144,256]{2,1,0:T(8,128)(2,1)} %attend.1), calls=%async_computation.2 | async-start | bytes 1179648 | tf_op jit(solution)/shard_map/all_to_all | solution.py:251
  149.4 4.3 %collective-permute-start.16 = (bf16[8,256,128]{2,1,0:T(8,128)(2,1)S(1)}, bf16[8,256,128]{2,1,0:T(8,128)(2,1)S(1)}, u32[]{:S(2)}, u32[]{:S(2)}) collective-permute-start(bf16[8,256,128]{2,1,0:T(8,128)(2,1)S(1)} %pad_maximum_fusion.2.w_ref), channel_id=1, source_target_pairs={{0,128},{128,0},{1,129},{129,1},{2,130},{130,2},{3,131},{131,3},{4... | collective-permute-start | bytes 1572872 | tf_op jit(solution)/shard_map/ppermute | solution.py:33
  151.3 4.1 %collective-permute-start.17 = (bf16[8,256,128]{2,1,0:T(8,128)(2,1)}, bf16[8,256,128]{2,1,0:T(8,128)(2,1)S(1)}, u32[]{:S(2)}, u32[]{:S(2)}) collective-permute-start(bf16[8,256,128]{2,1,0:T(8,128)(2,1)} %collective-permute-done.15.far_w_ref), channel_id=1, source_target_pairs={{0,128},{128,0},{1,129},{129,1},{2,130},{130,2},{3,131},{131,3},{4... | collective-permute-start | bytes 1572872 | tf_op jit(solution)/shard_map/ppermute | solution.py:33

commit v3 on v2

--- a/solution.py
+++ b/solution.py
@@ -5,6 +5,7 @@
 from jax.experimental.pallas import tpu as pltpu
 from jax.sharding import Mesh
 from jax.sharding import PartitionSpec as P
+
 
 HD = 128
 HEAD = ("y", "x_lo")
@@ -50,44 +51,29 @@
                 out_ref[far, j] = (x * factor).astype(jnp.bfloat16)
 
 
-def project(place_ref, tiles, w_ref, far_w_ref, order):
+def query_kernel(place_ref, keep_ref, other_ref, w_ref, far_w_ref, own_out, other_out):
     kv = place_ref[2]
     lanes = w_ref.shape[1]
     near = pl.multiple_of((kv & 1) * lanes, lanes)
     away = pl.multiple_of((1 - (kv & 1)) * lanes, lanes)
     total = None
     for at in range(w_ref.shape[0]):
-        rows = order(at, kv)
+        far, flip_4, flip_2 = at % 2, at // 2 % 2, at // 4
+        rows = (kv >> 1) ^ (2 * flip_4 + flip_2)
         for ref, lane in ((w_ref, near), (far_w_ref, away)):
-            x = jnp.concatenate([tile(rows, pl.ds(lane, lanes)) for tile in tiles], axis=0)
-            part = dot(x, ref[at])
+            x = [tile[far, rows, :, pl.ds(lane, lanes)] for tile in (keep_ref, other_ref)]
+            part = dot(jnp.concatenate(x, axis=0), ref[at])
             total = part if total is None else total + part
-    return total
-
-
-def query_kernel(place_ref, keep_ref, other_ref, w_ref, far_w_ref, own_out, other_out):
-    def order(at, kv):
-        far, flip_4, flip_2 = at % 2, at // 2 % 2, at // 4
-        return far, (kv >> 1) ^ (2 * flip_4 + flip_2)
-
-    def tile(ref):
-        return lambda rows, lanes: ref[rows[0], rows[1], :, lanes]
-
-    total = project(place_ref, [tile(keep_ref), tile(other_ref)], w_ref, far_w_ref, order)
     own_out[...] = total[: own_out.shape[0]]
     other_out[...] = total[own_out.shape[0] :]
 
 
-def pair_kernel(place_ref, keep_ref, other_ref, far_ref, w_ref, far_w_ref, own_out, other_out):
-    def order(at, kv):
-        flip_4, flip_2 = at % 2, at // 2
-        return (kv >> 1) ^ (2 * flip_4 + flip_2)
-
-    def tile(ref, side):
-        return lambda rows, lanes: ref[side, rows, :, lanes]
-
-    tiles = [tile(keep_ref, 0), tile(far_ref, 0), tile(other_ref, 0), tile(far_ref, 1)]
-    total = project(place_ref, tiles, w_ref, far_w_ref, order)
+def pair_kernel(place_ref, keep_ref, other_ref, far_ref, w_ref, own_out, other_out):
+    total = None
+    for at in range(w_ref.shape[0]):
+        x = [keep_ref[0, at], far_ref[0, at], other_ref[0, at], far_ref[1, at]]
+        part = dot(jnp.concatenate(x, axis=0), w_ref[at])
+        total = part if total is None else total + part
     rows = own_out.shape[1]
     for n in range(2):
         own_out[n] = total[n * rows : (n + 1) * rows]
@@ -146,8 +132,8 @@
         out_ref[b, own:] = stats.astype(jnp.bfloat16)
 
 
-def finish_kernel(place_ref, parts_ref, w_ref, far_w_ref, swap_w_ref, swap_far_w_ref, out_ref):
-    x_hi, core, kv = place_ref[0], place_ref[1], place_ref[2]
+def finish_kernel(place_ref, parts_ref, w_ref, swap_w_ref, out_ref):
+    x_hi, core = place_ref[0], place_ref[1]
     sources, rows, width = parts_ref.shape
     own = rows - STAT_ROWS
     heads = []
@@ -168,17 +154,14 @@
             mixture = part if mixture is None else mixture + part
         heads.append(mixture.astype(jnp.bfloat16))
     attended = jnp.concatenate(heads, axis=1)
-    lanes = w_ref.shape[2]
-    near = pl.multiple_of((kv & 1) * lanes, lanes)
-    away = pl.multiple_of((1 - (kv & 1)) * lanes, lanes)
+    lanes = w_ref.shape[3]
     for at in range(w_ref.shape[0]):
-        far, flip_4, flip_2 = at % 2, at // 2 % 2, at // 4
-        section = 2 * (x_hi ^ far)
-        pair = (kv >> 1) ^ (2 * flip_4 + flip_2)
-        for near_ref, away_ref, side in ((w_ref, far_w_ref, core), (swap_w_ref, swap_far_w_ref, 1 - core)):
-            to = (section + side) * 4 + pair
-            for ref, lane in ((near_ref, near), (away_ref, away)):
-                out_ref[to, :, pl.ds(lane, lanes)] = dot(attended, ref[at]).astype(jnp.bfloat16)
+        lane = slice(at % 2 * lanes, (at % 2 + 1) * lanes)
+        for far in range(2):
+            section = 2 * (1 - x_hi if far else x_hi)
+            for ref, side in ((w_ref, core), (swap_w_ref, 1 - core)):
+                to = (section + side) * 4 + at // 2
+                out_ref[to, :, lane] = dot(attended, ref[at, far]).astype(jnp.bfloat16)
 
 
 def doubled(value, axes):
@@ -194,33 +177,34 @@
     kv_count = lax.axis_size(KV)
     own = jnp.stack([lax.axis_index("x_hi"), lax.axis_index("core"), kv]).astype(jnp.int32)
 
-    def call(kernel, shapes, name, *operands):
+    def call(kernel, shapes, *operands):
         return pl.pallas_call(
             kernel,
             out_shape=shapes,
             in_specs=[SCALAR] + [WHOLE] * len(operands),
             out_specs=jax.tree.map(lambda _: WHOLE, shapes),
             compiler_params=VMEM,
-            name=name,
         )(own, *operands)
 
     gathered = shared(tokens[0], HEAD)
     query_w = doubled(w_query[None], ("x_hi", *KV))
-    pair_w = doubled(w_keyvalue.reshape(1, -1, 2 * width), KV)
-    out_w = doubled(w_out[None], ("x_hi", *KV))
-    out_w = (*out_w, *(swapped(w, "core") for w in out_w))
+    pair_w = lax.all_gather(w_keyvalue.reshape(-1, 2 * width), KV, axis=0, tiled=True)
+    pair_w = pair_w.reshape(4, -1, 2 * width)
+    out_w = jnp.stack([w_out, swapped(w_out, "x_hi")])
+    out_w = lax.all_gather(out_w, KV, axis=0, tiled=False)
+    out_w = (out_w, swapped(out_w, "core"))
 
     half = jax.ShapeDtypeStruct((2, 4, local_rows, width), jnp.bfloat16)
-    keep, send = call(normalize_kernel, (half, half), "normalize", gathered)
+    keep, send = call(normalize_kernel, (half, half), gathered)
     other = swapped(send, "core")
     partial = jax.ShapeDtypeStruct((local_rows, width), jnp.float32)
-    mine, theirs = call(query_kernel, (partial, partial), "project_queries", keep, other, *query_w)
+    mine, theirs = call(query_kernel, (partial, partial), keep, other, *query_w)
     queries = (mine + swapped(theirs, "core")).astype(jnp.bfloat16)
     queries = shared(queries, KV).reshape(-1, width)
 
     far = swapped(jnp.stack([keep[1], other[1]]), "x_hi")
     partial = jax.ShapeDtypeStruct((2, local_rows, 2 * width), jnp.float32)
-    mine, theirs = call(pair_kernel, (partial, partial), "project_pair", keep, other, far, *pair_w)
+    mine, theirs = call(pair_kernel, (partial, partial), keep, other, far, pair_w)
     mine = mine + swapped(theirs, "core")
     pair = (mine[0] + swapped(mine[1], "x_hi")).astype(jnp.bfloat16)
     place = kv * cache_rows + lax.iota(jnp.int32, cache_rows)
@@ -250,7 +234,7 @@
 
     arrived = lax.all_to_all(parts, KV, split_axis=0, concat_axis=0, tiled=True)
     blocks = jax.ShapeDtypeStruct((lax.axis_size(HEAD), local_rows, width), jnp.bfloat16)
-    columns = call(finish_kernel, blocks, "finish", arrived, *out_w)
+    columns = call(finish_kernel, blocks, arrived, *out_w)
     columns = lax.all_to_all(columns, HEAD, split_axis=0, concat_axis=0, tiled=True)
     return columns.astype(jnp.float32).sum(axis=0).astype(jnp.bfloat16)[None]
 

time: 206 us -> 206 us (level)
  starting transfers between devices: 91.3 us -> 57.8 us
  waiting for transfers between devices: 50.6 us -> 64.4 us
  between operations: 1.76 us -> 15 us
  blocking collectives: 33.4 us -> 38.3 us
  local copies, waits for them, and re-layouts: 4.51 us -> 7.08 us
    ppermute x18 -> x11, starting transfers between devices: 73.5 us -> 38.4 us  [swapped(): return lax.ppermute(value, axis, [(0, 1), (1, 0)])]
    all_gather x0 -> x2, waiting for transfers between devices: none -> 8.07 us  [the longest x1 8.05 us: shards(): out_w = lax.all_gather(out_w, KV, axis=0, tiled=False)]
    all_to_all x1, waiting for transfers between devices: 12.7 us -> 18.9 us  [shards(): arrived = lax.all_to_all(parts, KV, split_axis=0, concat_axis=0, tiled=True)]
    all_to_all x1, blocking collectives: 33.4 us -> 38.3 us  [shards(): lax.all_to_all(columns, HEAD, split_axis=0, concat_axis=0, tiled=True)]
    ppermute x18 -> x11, waiting for transfers between devices: 33.1 us -> 28.6 us  [swapped(): return lax.ppermute(value, axis, [(0, 1), (1, 0)])]
    all_to_all x2, waiting for transfers between devices: 4.84 us -> 8.87 us  [shared(): return lax.all_to_all(copies, axes, split_axis=0, concat_axis=0, tiled=True)]
    unnamed x14 -> x19, local copies, waits for them, and re-layouts: 0.84 us -> 4.26 us
    all_to_all x2, starting transfers between devices: 11.6 us -> 14.9 us  [shared(): return lax.all_to_all(copies, axes, split_axis=0, concat_axis=0, tiled=True)]
  transfers between devices with their start and end apart: 21 -> 16, of which waited for: 7 -> 9; matrix products, arithmetic and copies ran while one was open for 2% -> 2% of each run, Pallas kernels for 8% -> 8%
where the time goes in v3:
time: 206 us; the launch traced here: 205 us
  waiting for transfers between devices  64.4 us (31%)
  starting transfers between devices  57.8 us (28%)
  blocking collectives  38.3 us (19%)
  Pallas kernels  18.8 us (9%)
  between operations  15 us (7%)
  local copies, waits for them, and re-layouts  7.08 us (3%)
  other arithmetic  3.99 us (2%)
    ppermute x11, starting transfers between devices, swapped(): return lax.ppermute(value, axis, [(0, 1), (1, 0)])  38.4 us
    all_to_all x1, blocking collectives, shards(): lax.all_to_all(columns, HEAD, split_axis=0, concat_axis=0, tiled=True)  38.3 us
    ppermute x11, waiting for transfers between devices, swapped(): return lax.ppermute(value, axis, [(0, 1), (1, 0)])  28.6 us
    all_to_all x1, waiting for transfers between devices, shards(): arrived = lax.all_to_all(parts, KV, split_axis=0, concat_axis=0, tiled=True)  18.9 us
    all_to_all x2, starting transfers between devices, shared(): return lax.all_to_all(copies, axes, split_axis=0, concat_axis=0, tiled=True)  14.9 us
    pallas_call x1, Pallas kernels, shards(): pl.pallas_call(attend_kernel, grid=(width // HD, queries.shape[0] // QUER...  12.9 us
    all_to_all x2, waiting for transfers between devices, shared(): return lax.all_to_all(copies, axes, split_axis=0, concat_axis=0, tiled=True)  8.87 us
    all_gather x1, waiting for transfers between devices, shards(): out_w = lax.all_gather(out_w, KV, axis=0, tiled=False)  8.05 us
  transfers between devices with their start and end apart: 16, of which 9 were waited for; matrix products, arithmetic and copies ran while one was open for 2% of the time, Pallas kernels for 8%

profile of v3, /device:TPU:4, one launch (start us, length us, event | category | flops | bytes accessed | tf_op | source)
XLA Modules:
  0.0 205.4 jit_solution(17123335428018372313)
XLA Ops:
  6.5 1.9 broadcast_in_dim.29
  8.5 0.0 copy-start.7
  8.5 8.0 %all-to-all-start = ((bf16[16,128,256]{2,1,0:T(8,128)(2,1)}), bf16[16,128,256]{2,1,0:T(8,128)(2,1)S(1)}, u32[]{:S(2)}, u32[]{:S(2)}) async-start(bf16[16,128,256]{2,1,0:T(8,128)(2,1)} %broadcast_in_dim.29), calls=%async_computation | async-start | bytes 2097152 | tf_op jit(solution)/shard_map/all_to_all | solution.py:30
  16.4 0.0 all-gather.4.cloned.1.call-start
  16.5 0.0 copy-done.7
  16.5 0.7 copy.9
  17.2 0.0 copy-start.5
  17.2 0.0 all-gather.4.cloned.1.call-update
  17.2 0.0 all-gather.6.cloned.1.call-start
  17.2 0.8 copy-done.5
  18.0 3.6 %collective-permute-start.1 = (bf16[1,128,256]{2,1,0:T(8,128)(2,1)S(1)}, bf16[1,128,256]{2,1,0:T(8,128)(2,1)S(1)}, u32[]{:S(2)}, u32[]{:S(2)}) collective-permute-start(bf16[1,128,256]{2,1,0:T(8,128)(2,1)S(1)} %bitcast.33), channel_id=1, source_target_pairs={{0,256},{256,0},{1,257},{257,1},{2,258},{258,2},{3,259},{259,3},{4... | collective-permute-start | bytes 196616 | tf_op jit(solution)/shard_map/ppermute | solution.py:34
  21.6 4.2 %collective-permute-done.1 = bf16[1,128,256]{2,1,0:T(8,128)(2,1)S(1)} collective-permute-done((bf16[1,128,256]{2,1,0:T(8,128)(2,1)S(1)}, bf16[1,128,256]{2,1,0:T(8,128)(2,1)S(1)}, u32[]{:S(2)}, u32[]{:S(2)}) %collective-permute-start.1) | collective-permute-done | bytes 65568 | tf_op jit(solution)/shard_map/ppermute | solution.py:34
  25.8 10.9 %collective-permute-start.2 = (bf16[2,128,256]{2,1,0:T(8,128)(2,1)S(1)}, bf16[2,128,256]{2,1,0:T(8,128)(2,1)S(1)}, u32[]{:S(2)}, u32[]{:S(2)}) collective-permute-start(bf16[2,128,256]{2,1,0:T(8,128)(2,1)S(1)} %pad_maximum_fusion.3), channel_id=1, source_target_pairs={{0,4},{4,0},{1,5},{5,1},{2,6},{6,2},{3,7},{7,3},{8,12},{12,8},{9,1... | collective-permute-start | bytes 393224 | tf_op jit(solution)/shard_map/ppermute | solution.py:34
  36.7 0.1 pad_add_fusion.place_ref
  36.8 8.4 %all-to-all-done.x_ref = bf16[16,128,256]{2,1,0:T(8,128)(2,1)S(1)} async-done(((bf16[16,128,256]{2,1,0:T(8,128)(2,1)}), bf16[16,128,256]{2,1,0:T(8,128)(2,1)S(1)}, u32[]{:S(2)}, u32[]{:S(2)}) %all-to-all-start) | async-done | bytes 1048608 | tf_op jit(solution)/shard_map/all_to_all | solution.py:30
  45.2 0.9 shard_map.82
  46.1 0.0 copy-start.8
  46.1 2.1 collective-permute-start
  48.1 0.0 collective-permute-done.2
  48.2 6.1 %collective-permute-start.3 = (bf16[4,128,256]{2,1,0:T(8,128)(2,1)S(1)}, bf16[4,128,256]{2,1,0:T(8,128)(2,1)S(1)}, u32[]{:S(2)}, u32[]{:S(2)}) collective-permute-start(bf16[4,128,256]{2,1,0:T(8,128)(2,1)S(1)} %pad_maximum_fusion.2), channel_id=1, source_target_pairs={{0,2},{2,0},{1,3},{3,1},{4,6},{6,4},{5,7},{7,5},{8,10},{10,8},{9,1... | collective-permute-start | bytes 786440 | tf_op jit(solution)/shard_map/ppermute | solution.py:34
  54.3 0.0 copy-done.8
  54.3 2.7 %collective-permute-start.9 = (bf16[256,128]{1,0:T(8,128)(2,1)S(1)}, bf16[256,128]{1,0:T(8,128)(2,1)S(1)}, u32[]{:S(2)}, u32[]{:S(2)}) collective-permute-start(bf16[256,128]{1,0:T(8,128)(2,1)S(1)} %copy-done.8), channel_id=1, source_target_pairs={{0,256},{256,0},{1,257},{257,1},{2,258},{258,2},{3,259},{259,3},{4... | collective-permute-start | bytes 196616 | tf_op jit(solution)/shard_map/ppermute | solution.py:34
  57.0 4.9 %collective-permute-done.9 = bf16[256,128]{1,0:T(8,128)(2,1)S(1)} collective-permute-done((bf16[256,128]{1,0:T(8,128)(2,1)S(1)}, bf16[256,128]{1,0:T(8,128)(2,1)S(1)}, u32[]{:S(2)}, u32[]{:S(2)}) %collective-permute-start.9) | collective-permute-done | bytes 65568 | tf_op jit(solution)/shard_map/ppermute | solution.py:34
  62.0 0.7 pad_maximum_fusion.4
  62.6 0.0 all-gather.6.cloned.1.call-update
  62.7 7.8 %collective-permute-done.3 = bf16[4,128,256]{2,1,0:T(8,128)(2,1)S(1)} collective-permute-done((bf16[4,128,256]{2,1,0:T(8,128)(2,1)S(1)}, bf16[4,128,256]{2,1,0:T(8,128)(2,1)S(1)}, u32[]{:S(2)}, u32[]{:S(2)}) %collective-permute-start.3) | collective-permute-done | bytes 262176 | tf_op jit(solution)/shard_map/ppermute | solution.py:34
  70.5 0.1 pad_maximum_fusion.w_ref
  70.6 1.9 collective-permute-start.4
  72.5 0.0 collective-permute-done.other_ref
  72.6 0.1 pad_maximum_fusion.1
  72.6 2.6 %collective-permute-start.6 = (bf16[2,4,128,256]{3,2,1,0:T(8,128)(2,1)S(1)}, bf16[2,4,128,256]{3,2,1,0:T(8,128)(2,1)S(1)}, u32[]{:S(2)}, u32[]{:S(2)}) collective-permute-start(bf16[2,4,128,256]{3,2,1,0:T(8,128)(2,1)S(1)} %pad_maximum_fusion.1), channel_id=1, source_target_pairs={{0,256},{256,0},{1,257},{257,1},{2,258},{258,2},{3,259},{259,3},{4... | collective-permute-start | bytes 1572872 | tf_op jit(solution)/shard_map/ppermute | solution.py:34
  75.2 11.2 %collective-permute-done.4.far_w_ref = bf16[8,128,256]{2,1,0:T(8,128)(2,1)S(1)} collective-permute-done((bf16[8,128,256]{2,1,0:T(8,128)(2,1)S(1)}, bf16[8,128,256]{2,1,0:T(8,128)(2,1)S(1)}, u32[]{:S(2)}, u32[]{:S(2)}) %collective-permute-start.4) | collective-permute-done | bytes 524320 | tf_op jit(solution)/shard_map/ppermute | solution.py:34
  86.4 1.2 shard_map.83
  87.6 1.9 collective-permute-start.5
  89.5 0.0 all-gather.4.cloned.1.call-done
  89.6 0.4 collective-permute-done.6.far_ref
  89.9 1.2 copy-done
  91.2 1.2 shard_map.84
  92.4 2.1 collective-permute-start.7
  94.5 0.0 collective-permute-done.5
  94.5 0.8 broadcast_in_dim.31
  95.4 6.9 %all-to-all-start.1 = ((bf16[8,128,256]{2,1,0:T(8,128)(2,1)}), bf16[8,128,256]{2,1,0:T(8,128)(2,1)S(1)}, u32[]{:S(2)}, u32[]{:S(2)}) async-start(bf16[8,128,256]{2,1,0:T(8,128)(2,1)} %broadcast_in_dim.31), calls=%async_computation.1 | async-start | bytes 1048576 | tf_op jit(solution)/shard_map/all_to_all | solution.py:30
  102.3 0.0 collective-permute-done.7
  102.3 0.0 copy-start.6
  102.3 0.8 copy-done.6
  103.1 1.3 add.30
  104.4 0.0 copy-start.4
  104.4 0.8 copy-done.4
  105.2 2.7 %collective-permute-start.8 = (f32[128,512]{1,0:T(8,128)S(1)}, f32[128,512]{1,0:T(8,128)S(1)}, u32[]{:S(2)}, u32[]{:S(2)}) collective-permute-start(f32[128,512]{1,0:T(8,128)S(1)} %slice_bitcast_fusion), channel_id=1, source_target_pairs={{0,256},{256,0},{1,257},{257,1},{2,258},{258,2},{3,259},{259,3},{4... | collective-permute-start | bytes 786440 | tf_op jit(solution)/shard_map/ppermute | solution.py:34
  109.2 8.0 %all-gather.6.cloned.1.call-done = bf16[16,256,128]{2,1,0:T(8,128)(2,1)} async-done(((bf16[2,256,128]{2,1,0:T(8,128)(2,1)}), bf16[16,256,128]{2,1,0:T(8,128)(2,1)}) %all-gather.6.cloned.1.call-update) | async-done | bytes 1048592 | tf_op jit(solution)/shard_map/all_gather | solution.py:194
  117.2 1.9 collective-permute-start.10
  119.2 0.0 collective-permute-done.8
  119.2 1.0 fusion.1.new_k_ref.new_v_ref
  120.2 0.5 all-to-all-done.1
  120.7 0.0 copy-done.1
  120.7 0.0 copy-done.2
  120.7 12.9 %attend.1 = bf16[8,144,256]{2,1,0:T(8,128)(2,1)} custom-call(s32[1]{0:T(128)} %bitcast.2.kv_ref, f32[8,2048]{1,0:T(8,128)S(1)} %broadcast_in_dim.28.bias_ref, bf16[1024,256]{1,0:T(8,128)(2,1)S(1)} %bitcast.27, bf16[2048,256]{1,0:T(8,128)(2,1)S(1)} %bitcast.29, bf16[2048,256]{1,0:T(8,128)(2,1)S(1)} %bitcast.30, ...), custom_call_target="tpu_custom_call" | custom-call | tf_op jit(solution)/shard_map/attend/pallas_call | solution.py:216
  133.6 4.4 %all-to-all-start.2 = ((bf16[8,144,256]{2,1,0:T(8,128)(2,1)}), bf16[8,144,256]{2,1,0:T(8,128)(2,1)S(1)}, u32[]{:S(2)}, u32[]{:S(2)}) async-start(bf16[8,144,256]{2,1,0:T(8,128)(2,1)} %attend.1), calls=%async_computation.2 | async-start | bytes 1179648 | tf_op jit(solution)/shard_map/all_to_all | solution.py:235
  138.0 0.0 collective-permute-done.10.swap_w_ref
  138.0 18.9 %all-to-all-done.2.parts_ref = bf16[8,144,256]{2,1,0:T(8,128)(2,1)S(1)} async-done(((bf16[8,144,256]{2,1,0:T(8,128)(2,1)}), bf16[8,144,256]{2,1,0:T(8,128)(2,1)S(1)}, u32[]{:S(2)}, u32[]{:S(2)}) %all-to-all-start.2) | async-done | bytes 589856 | tf_op jit(solution)/shard_map/all_to_all | solution.py:235
  156.9 0.0 copy-done.3
  156.9 2.6 %shard_map.85 = bf16[16,128,256]{2,1,0:T(8,128)(2,1)S(1)} custom-call(s32[3]{0:T(128)S(1)} %pad_add_fusion.place_ref, bf16[8,144,256]{2,1,0:T(8,128)(2,1)S(1)} %all-to-all-done.2.parts_ref, bf16[8,2,256,128]{3,2,1,0:T(8,128)(2,1)S(1)} %bitcast.32, bf16[8,2,256,128]{3,2,1,0:T(8,128)(2,1)} %collective-permute-done.10.swap_w_ref), custom_call_target="tpu_custom_call" | custom-call | tf_op jit(solution)/shard_map/pallas_call | solution.py:181
  159.5 38.3 %all_to_all.20 = bf16[16,128,256]{2,1,0:T(8,128)(2,1)S(1)} all-to-all(bf16[16,128,256]{2,1,0:T(8,128)(2,1)S(1)} %shard_map.85), channel_id=1, replica_groups=mesh['x_hi'=2,'core'=2,'y'=8,'x_lo'=2,'z_4'=2,'z_2'=2,'z_1'=2] {'y','x_lo'}, dimensions={0} | all-to-all | bytes 2097152 | tf_op jit(solution)/shard_map/all_to_all | solution.py:238
  197.8 0.8 reduce_sum.12
  (12 shorter events, 0.1 us)
Async XLA Ops:
  8.5 8.0 %copy-start.7 = (bf16[128,2,256]{2,1,0:T(2,128)(2,1)S(1)}, bf16[128,2,256]{2,1,0:T(2,128)(2,1)}, u32[]{:S(2)}) copy-start(bf16[128,2,256]{2,1,0:T(2,128)(2,1)} %param.10) | copy-start | bytes 393220
  8.5 36.7 %all-to-all-start = ((bf16[16,128,256]{2,1,0:T(8,128)(2,1)}), bf16[16,128,256]{2,1,0:T(8,128)(2,1)S(1)}, u32[]{:S(2)}, u32[]{:S(2)}) async-start(bf16[16,128,256]{2,1,0:T(8,128)(2,1)} %broadcast_in_dim.29), calls=%async_computation | async-start | bytes 2097152 | tf_op jit(solution)/shard_map/all_to_all | solution.py:30
  16.4 73.1 %all-gather.4.cloned.1.call-start = ((), (), s32[]{:S(2)}) async-start(), calls=%async_computation.4 | async-start | bytes 1179648 | tf_op jit(solution)/shard_map/all_gather | solution.py:191
  17.2 0.8 copy-start.5
  17.2 100.1 %all-gather.6.cloned.1.call-start = ((), (), s32[]{:S(2)}) async-start(), calls=%async_computation.5 | async-start | bytes 1179648 | tf_op jit(solution)/shard_map/all_gather | solution.py:194
  18.0 7.8 %collective-permute-start.1 = (bf16[1,128,256]{2,1,0:T(8,128)(2,1)S(1)}, bf16[1,128,256]{2,1,0:T(8,128)(2,1)S(1)}, u32[]{:S(2)}, u32[]{:S(2)}) collective-permute-start(bf16[1,128,256]{2,1,0:T(8,128)(2,1)S(1)} %bitcast.33), channel_id=1, source_target_pairs={{0,256},{256,0},{1,257},{257,1},{2,258},{258,2},{3,259},{259,3},{4... | collective-permute-start | bytes 196616 | tf_op jit(solution)/shard_map/ppermute | solution.py:34
  25.8 22.3 %collective-permute-start.2 = (bf16[2,128,256]{2,1,0:T(8,128)(2,1)S(1)}, bf16[2,128,256]{2,1,0:T(8,128)(2,1)S(1)}, u32[]{:S(2)}, u32[]{:S(2)}) collective-permute-start(bf16[2,128,256]{2,1,0:T(8,128)(2,1)S(1)} %pad_maximum_fusion.3), channel_id=1, source_target_pairs={{0,4},{4,0},{1,5},{5,1},{2,6},{6,2},{3,7},{7,3},{8,12},{12,8},{9,1... | collective-permute-start | bytes 393224 | tf_op jit(solution)/shard_map/ppermute | solution.py:34
  46.1 8.2 %copy-start.8 = (bf16[256,128]{1,0:T(8,128)(2,1)S(1)}, bf16[256,128]{1,0:T(8,128)(2,1)}, u32[]{:S(2)}) copy-start(bf16[256,128]{1,0:T(8,128)(2,1)} %param.15) | copy-start | bytes 196612
  46.1 26.4 %collective-permute-start = (bf16[2,4,128,256]{3,2,1,0:T(8,128)(2,1)S(1)}, bf16[2,4,128,256]{3,2,1,0:T(8,128)(2,1)S(1)}, u32[]{:S(2)}, u32[]{:S(2)}) collective-permute-start(bf16[2,4,128,256]{3,2,1,0:T(8,128)(2,1)S(1)} %get-tuple-element.12), channel_id=1, source_target_pairs={{0,128},{128,0},{1,129},{129,1},{2,130},{130,2},{3,131},{131,3},{4... | collective-permute-start | bytes 1572872 | tf_op jit(solution)/shard_map/ppermute | solution.py:34
  48.2 22.3 %collective-permute-start.3 = (bf16[4,128,256]{2,1,0:T(8,128)(2,1)S(1)}, bf16[4,128,256]{2,1,0:T(8,128)(2,1)S(1)}, u32[]{:S(2)}, u32[]{:S(2)}) collective-permute-start(bf16[4,128,256]{2,1,0:T(8,128)(2,1)S(1)} %pad_maximum_fusion.2), channel_id=1, source_target_pairs={{0,2},{2,0},{1,3},{3,1},{4,6},{6,4},{5,7},{7,5},{8,10},{10,8},{9,1... | collective-permute-start | bytes 786440 | tf_op jit(solution)/shard_map/ppermute | solution.py:34
  54.3 7.7 %collective-permute-start.9 = (bf16[256,128]{1,0:T(8,128)(2,1)S(1)}, bf16[256,128]{1,0:T(8,128)(2,1)S(1)}, u32[]{:S(2)}, u32[]{:S(2)}) collective-permute-start(bf16[256,128]{1,0:T(8,128)(2,1)S(1)} %copy-done.8), channel_id=1, source_target_pairs={{0,256},{256,0},{1,257},{257,1},{2,258},{258,2},{3,259},{259,3},{4... | collective-permute-start | bytes 196616 | tf_op jit(solution)/shard_map/ppermute | solution.py:34
  70.6 15.8 %collective-permute-start.4 = (bf16[8,128,256]{2,1,0:T(8,128)(2,1)S(1)}, bf16[8,128,256]{2,1,0:T(8,128)(2,1)S(1)}, u32[]{:S(2)}, u32[]{:S(2)}) collective-permute-start(bf16[8,128,256]{2,1,0:T(8,128)(2,1)S(1)} %pad_maximum_fusion.w_ref), channel_id=1, source_target_pairs={{0,1},{1,0},{2,3},{3,2},{4,5},{5,4},{6,7},{7,6},{8,9},{9,8},{10,11... | collective-permute-start | bytes 1572872 | tf_op jit(solution)/shard_map/ppermute | solution.py:34
  72.6 17.3 %collective-permute-start.6 = (bf16[2,4,128,256]{3,2,1,0:T(8,128)(2,1)S(1)}, bf16[2,4,128,256]{3,2,1,0:T(8,128)(2,1)S(1)}, u32[]{:S(2)}, u32[]{:S(2)}) collective-permute-start(bf16[2,4,128,256]{3,2,1,0:T(8,128)(2,1)S(1)} %pad_maximum_fusion.1), channel_id=1, source_target_pairs={{0,256},{256,0},{1,257},{257,1},{2,258},{258,2},{3,259},{259,3},{4... | collective-permute-start | bytes 1572872 | tf_op jit(solution)/shard_map/ppermute | solution.py:34
  87.6 6.9 %collective-permute-start.5 = (f32[128,256]{1,0:T(8,128)S(1)}, f32[128,256]{1,0:T(8,128)S(1)}, u32[]{:S(2)}, u32[]{:S(2)}) collective-permute-start(f32[128,256]{1,0:T(8,128)S(1)} %get-tuple-element.14), channel_id=1, source_target_pairs={{0,128},{128,0},{1,129},{129,1},{2,130},{130,2},{3,131},{131,3},{4... | collective-permute-start | bytes 393224 | tf_op jit(solution)/shard_map/ppermute | solution.py:34
  89.9 1.2 copy-start
  92.4 9.9 %collective-permute-start.7 = (f32[2,128,512]{2,1,0:T(8,128)S(1)}, f32[2,128,512]{2,1,0:T(8,128)S(1)}, u32[]{:S(2)}, u32[]{:S(2)}) collective-permute-start(f32[2,128,512]{2,1,0:T(8,128)S(1)} %get-tuple-element.16), channel_id=1, source_target_pairs={{0,128},{128,0},{1,129},{129,1},{2,130},{130,2},{3,131},{131,3},{4... | collective-permute-start | bytes 1572872 | tf_op jit(solution)/shard_map/ppermute | solution.py:34
  95.4 25.3 %all-to-all-start.1 = ((bf16[8,128,256]{2,1,0:T(8,128)(2,1)}), bf16[8,128,256]{2,1,0:T(8,128)(2,1)S(1)}, u32[]{:S(2)}, u32[]{:S(2)}) async-start(bf16[8,128,256]{2,1,0:T(8,128)(2,1)} %broadcast_in_dim.31), calls=%async_computation.1 | async-start | bytes 1048576 | tf_op jit(solution)/shard_map/all_to_all | solution.py:30
  102.3 0.8 copy-start.6
  103.1 17.6 %copy-start.1 = (bf16[1,2048,256]{2,1,0:T(8,128)(2,1)S(1)}, bf16[1,2048,256]{2,1,0:T(8,128)(2,1)}, u32[]{:S(2)}) copy-start(bf16[1,2048,256]{2,1,0:T(8,128)(2,1)} %param.11) | copy-start | bytes 3145732
  103.1 17.6 %copy-start.2 = (bf16[1,2048,256]{2,1,0:T(8,128)(2,1)S(1)}, bf16[1,2048,256]{2,1,0:T(8,128)(2,1)}, u32[]{:S(2)}) copy-start(bf16[1,2048,256]{2,1,0:T(8,128)(2,1)} %param.12) | copy-start | bytes 3145732
  104.4 0.8 copy-start.4
  105.2 14.0 %collective-permute-start.8 = (f32[128,512]{1,0:T(8,128)S(1)}, f32[128,512]{1,0:T(8,128)S(1)}, u32[]{:S(2)}, u32[]{:S(2)}) collective-permute-start(f32[128,512]{1,0:T(8,128)S(1)} %slice_bitcast_fusion), channel_id=1, source_target_pairs={{0,256},{256,0},{1,257},{257,1},{2,258},{258,2},{3,259},{259,3},{4... | collective-permute-start | bytes 786440 | tf_op jit(solution)/shard_map/ppermute | solution.py:34
  117.2 20.8 %collective-permute-start.10 = (bf16[8,2,256,128]{3,2,1,0:T(8,128)(2,1)}, bf16[8,2,256,128]{3,2,1,0:T(8,128)(2,1)}, u32[]{:S(2)}, u32[]{:S(2)}) collective-permute-start(bf16[8,2,256,128]{3,2,1,0:T(8,128)(2,1)} %bitcast.31), channel_id=1, source_target_pairs={{0,128},{128,0},{1,129},{129,1},{2,130},{130,2},{3,131},{131,3},{4... | collective-permute-start | bytes 3145736 | tf_op jit(solution)/shard_map/ppermute | solution.py:34
  133.6 23.3 %copy-start.3 = (bf16[16,256,128]{2,1,0:T(8,128)(2,1)S(1)}, bf16[16,256,128]{2,1,0:T(8,128)(2,1)}, u32[]{:S(2)}) copy-start(bf16[16,256,128]{2,1,0:T(8,128)(2,1)} %all-gather.6.cloned.1.call-done) | copy-start | bytes 3145732
  133.6 23.3 %all-to-all-start.2 = ((bf16[8,144,256]{2,1,0:T(8,128)(2,1)}), bf16[8,144,256]{2,1,0:T(8,128)(2,1)S(1)}, u32[]{:S(2)}, u32[]{:S(2)}) async-start(bf16[8,144,256]{2,1,0:T(8,128)(2,1)} %attend.1), calls=%async_computation.2 | async-start | bytes 1179648 | tf_op jit(solution)/shard_map/all_to_all | solution.py:235
Sparse Core Ops, SparseCore 0:
  19.3 51.8 all-gather.3
  73.3 43.8 all-gather.5

commit v4 on v3

--- a/solution.py
+++ b/solution.py
@@ -51,19 +51,22 @@
                 out_ref[far, j] = (x * factor).astype(jnp.bfloat16)
 
 
-def query_kernel(place_ref, keep_ref, other_ref, w_ref, far_w_ref, own_out, other_out):
+def query_kernel(place_ref, keep_ref, other_ref, w_ref, far_w_ref, away_w_ref, own_out, other_out):
     kv = place_ref[2]
-    lanes = w_ref.shape[1]
+    lanes = far_w_ref.shape[1]
     near = pl.multiple_of((kv & 1) * lanes, lanes)
     away = pl.multiple_of((1 - (kv & 1)) * lanes, lanes)
     total = None
     for at in range(w_ref.shape[0]):
-        far, flip_4, flip_2 = at % 2, at // 2 % 2, at // 4
+        x = jnp.concatenate([keep_ref[0, at], other_ref[0, at]], axis=0)
+        part = dot(x, w_ref[at])
+        total = part if total is None else total + part
+    for at in range(far_w_ref.shape[0]):
+        flip_4, flip_2 = at % 2, at // 2
         rows = (kv >> 1) ^ (2 * flip_4 + flip_2)
-        for ref, lane in ((w_ref, near), (far_w_ref, away)):
-            x = [tile[far, rows, :, pl.ds(lane, lanes)] for tile in (keep_ref, other_ref)]
-            part = dot(jnp.concatenate(x, axis=0), ref[at])
-            total = part if total is None else total + part
+        for ref, lane in ((far_w_ref, near), (away_w_ref, away)):
+            x = [tile[1, rows, :, pl.ds(lane, lanes)] for tile in (keep_ref, other_ref)]
+            total = total + dot(jnp.concatenate(x, axis=0), ref[at])
     own_out[...] = total[: own_out.shape[0]]
     other_out[...] = total[own_out.shape[0] :]
 
@@ -88,45 +91,53 @@
     return [high.astype(jnp.float32), middle.astype(jnp.float32), low.astype(jnp.float32)]
 
 
-def attend_kernel(kv_ref, bias_ref, q_ref, k_ref, v_ref, new_k_ref, new_v_ref, out_ref, s_ref):
-    first = pl.program_id(1) * QUERY_ROWS
+def score(q, keys):
+    return lax.dot_general(q, keys, (((1,), (1,)), ((), ())), preferred_element_type=jnp.float32)
+
+
+def mixed(scores, peak, values):
+    weights = jnp.exp2((scores - peak) * EXPONENT).astype(jnp.bfloat16)
+    return dot(weights, jnp.concatenate([values, jnp.ones_like(values)], axis=1))
+
+
+def cache_kernel(bias_ref, q_ref, k_ref, v_ref, peak_ref, total_ref, s_ref):
     q = q_ref[...]
     cache_rows = k_ref.shape[0]
-    new_rows = new_k_ref.shape[0]
-
-    def score(keys):
-        return lax.dot_general(q, keys, (((1,), (1,)), ((), ())), preferred_element_type=jnp.float32)
-
     peak = None
     for at in range(0, cache_rows, KEY_ROWS):
-        s = score(k_ref[at : at + KEY_ROWS]) + bias_ref[0:1, at : at + KEY_ROWS]
+        s = score(q, k_ref[at : at + KEY_ROWS]) + bias_ref[0:1, at : at + KEY_ROWS]
         s_ref[:, at : at + KEY_ROWS] = s
         for lane in range(0, KEY_ROWS, HD):
             piece = s[:, lane : lane + HD]
             peak = piece if peak is None else jnp.maximum(peak, piece)
-    s = score(new_k_ref[...])
-    row = first + lax.broadcasted_iota(jnp.int32, s.shape, 0)
-    column = kv_ref[0] * new_rows + lax.broadcasted_iota(jnp.int32, s.shape, 1)
+    peak = jnp.max(peak, axis=1, keepdims=True)
+    total = None
+    for at in range(0, cache_rows, KEY_ROWS):
+        part = mixed(s_ref[:, at : at + KEY_ROWS], peak, v_ref[at : at + KEY_ROWS])
+        total = part if total is None else total + part
+    peak_ref[0] = jnp.broadcast_to(peak, peak_ref.shape[1:])
+    total_ref[0] = total
+
+
+def new_kernel(place_ref, q_ref, k_ref, v_ref, peak_ref, total_ref, out_ref):
+    s = score(q_ref[...], k_ref[...])
+    row = pl.program_id(1) * QUERY_ROWS + lax.broadcasted_iota(jnp.int32, s.shape, 0)
+    column = place_ref[2] * k_ref.shape[0] + lax.broadcasted_iota(jnp.int32, s.shape, 1)
     s = jnp.where(column <= row, s, DEAD)
-    s_ref[:, cache_rows:] = s
-    peak = jnp.max(jnp.maximum(peak, s), axis=1, keepdims=True)
-
-    def mixed(at, values):
-        weights = jnp.exp2((s_ref[:, at : at + values.shape[0]] - peak) * EXPONENT)
-        both = jnp.concatenate([values, jnp.ones_like(values)], axis=1)
-        return dot(weights.astype(jnp.bfloat16), both)
-
-    total = mixed(cache_rows, new_v_ref[...])
-    for at in range(0, cache_rows, KEY_ROWS):
-        total = total + mixed(at, v_ref[at : at + KEY_ROWS])
+    cache_peak = peak_ref[0]
+    peak = jnp.maximum(cache_peak, jnp.max(s, axis=1, keepdims=True))
+    fresh = mixed(s, peak, v_ref[...])
+    kept = jnp.exp2((cache_peak - peak) * EXPONENT)
+    mixture = total_ref[0, :, :HD] * kept + fresh[:, :HD]
+    total = total_ref[0, :, HD:] * kept + fresh[:, HD:]
 
     lane = lax.broadcasted_iota(jnp.int32, (HD, HD), 1)
     blocks, rows, _ = out_ref.shape
     own = rows - STAT_ROWS
     for b in range(blocks):
-        part = total[b * own : (b + 1) * own]
-        out_ref[b, :own] = part[:, :HD].astype(jnp.bfloat16)
-        turned = jnp.where(lane == 0, peak[b * own : (b + 1) * own], part[:, HD:]).T
+        part = slice(b * own, (b + 1) * own)
+        out_ref[b, :own] = mixture[part].astype(jnp.bfloat16)
+        turned = jnp.where(lane == 0, peak[part], total[part]).T
         stats = thirds(turned[0:1]) + thirds(turned[1:2])
         stats = jnp.concatenate([*stats, jnp.zeros((STAT_ROWS - 6, HD), jnp.float32)], axis=0)
         out_ref[b, own:] = stats.astype(jnp.bfloat16)
@@ -187,10 +198,12 @@
         )(own, *operands)
 
     gathered = shared(tokens[0], HEAD)
-    query_w = doubled(w_query[None], ("x_hi", *KV))
+    query_w_far = swapped(w_query[None], "x_hi")
+    out_w = jnp.stack([w_out, swapped(w_out, "x_hi")])
+    query_w_far = doubled(query_w_far, KV)
+    query_w = shared(w_query, KV).reshape(4, -1, width)
     pair_w = lax.all_gather(w_keyvalue.reshape(-1, 2 * width), KV, axis=0, tiled=True)
     pair_w = pair_w.reshape(4, -1, 2 * width)
-    out_w = jnp.stack([w_out, swapped(w_out, "x_hi")])
     out_w = lax.all_gather(out_w, KV, axis=0, tiled=False)
     out_w = (out_w, swapped(out_w, "core"))
 
@@ -198,7 +211,7 @@
     keep, send = call(normalize_kernel, (half, half), gathered)
     other = swapped(send, "core")
     partial = jax.ShapeDtypeStruct((local_rows, width), jnp.float32)
-    mine, theirs = call(query_kernel, (partial, partial), keep, other, *query_w)
+    mine, theirs = call(query_kernel, (partial, partial), keep, other, query_w, *query_w_far)
     queries = (mine + swapped(theirs, "core")).astype(jnp.bfloat16)
     queries = shared(queries, KV).reshape(-1, width)
 
@@ -211,26 +224,43 @@
     usable = (place >= key_start[0]) & (place < key_end[0])
     bias = jnp.broadcast_to(jnp.where(usable, 0.0, DEAD).astype(jnp.float32)[None], (8, cache_rows))
 
-    blocks = QUERY_ROWS // local_rows
+    heads = width // HD
+    rows = queries.shape[0]
+    grid = (heads, rows // QUERY_ROWS)
+    query_spec = pl.BlockSpec((QUERY_ROWS, HD), lambda h, i: (i, h))
+    cache_spec = pl.BlockSpec((cache_rows, HD), lambda h, i: (0, h))
+    peak_spec = pl.BlockSpec((1, QUERY_ROWS, HD), lambda h, i: (h, i, 0))
+    total_spec = pl.BlockSpec((1, QUERY_ROWS, 2 * HD), lambda h, i: (h, i, 0))
+    peaks, totals = pl.pallas_call(
+        cache_kernel,
+        grid=grid,
+        out_shape=(
+            jax.ShapeDtypeStruct((heads, rows, HD), jnp.float32),
+            jax.ShapeDtypeStruct((heads, rows, 2 * HD), jnp.float32),
+        ),
+        in_specs=[pl.BlockSpec((8, cache_rows), lambda h, i: (0, 0)), query_spec, cache_spec, cache_spec],
+        out_specs=(peak_spec, total_spec),
+        scratch_shapes=[pltpu.VMEM((QUERY_ROWS, cache_rows), jnp.float32)],
+        compiler_params=VMEM,
+        name="attend_cache",
+    )(bias, queries, cache_keys[0], cache_values[0])
     padded = local_rows + STAT_ROWS
     parts = pl.pallas_call(
-        attend_kernel,
-        grid=(width // HD, queries.shape[0] // QUERY_ROWS),
+        new_kernel,
+        grid=grid,
         out_shape=jax.ShapeDtypeStruct((kv_count, padded, width), jnp.bfloat16),
         in_specs=[
             SCALAR,
-            pl.BlockSpec((8, cache_rows), lambda h, i: (0, 0)),
-            pl.BlockSpec((QUERY_ROWS, HD), lambda h, i: (i, h)),
-            pl.BlockSpec((cache_rows, HD), lambda h, i: (0, h)),
-            pl.BlockSpec((cache_rows, HD), lambda h, i: (0, h)),
+            query_spec,
             pl.BlockSpec((local_rows, HD), lambda h, i: (0, h)),
-            pl.BlockSpec((local_rows, HD), lambda h, i: (0, h + width // HD)),
+            pl.BlockSpec((local_rows, HD), lambda h, i: (0, h + heads)),
+            peak_spec,
+            total_spec,
         ],
-        out_specs=pl.BlockSpec((blocks, padded, HD), lambda h, i: (i, 0, h)),
-        scratch_shapes=[pltpu.VMEM((QUERY_ROWS, cache_rows + local_rows), jnp.float32)],
+        out_specs=pl.BlockSpec((QUERY_ROWS // local_rows, padded, HD), lambda h, i: (i, 0, h)),
         compiler_params=VMEM,
-        name="attend",
-    )(kv.reshape(1), bias, queries, cache_keys[0], cache_values[0], pair, pair)
+        name="attend_new",
+    )(own, queries, pair, pair, peaks, totals)
 
     arrived = lax.all_to_all(parts, KV, split_axis=0, concat_axis=0, tiled=True)
     blocks = jax.ShapeDtypeStruct((lax.axis_size(HEAD), local_rows, width), jnp.bfloat16)

time: 206 us -> 223 us (1.083)
  waiting for transfers between devices: 64.4 us -> 85.2 us
  blocking collectives: 38.3 us -> 32.7 us
    all_to_all x2 -> x3, waiting for transfers between devices: 8.87 us -> 37.1 us  [shared(): return lax.all_to_all(copies, axes, split_axis=0, concat_axis=0, tiled=True)]
    all_gather x1, waiting for transfers between devices: 8.05 us -> 0.02 us  [shards(): out_w = lax.all_gather(out_w, KV, axis=0, tiled=False)]
    all_to_all x2 -> x3, starting transfers between devices: 14.9 us -> 21.6 us  [shared(): return lax.all_to_all(copies, axes, split_axis=0, concat_axis=0, tiled=True)]
    all_to_all x1, blocking collectives: 38.3 us -> 32.7 us  [shards(): lax.all_to_all(columns, HEAD, split_axis=0, concat_axis=0, tiled=True)]
    ppermute x11, starting transfers between devices: 38.4 us -> 33.1 us  [swapped(): return lax.ppermute(value, axis, [(0, 1), (1, 0)])]
    pallas_call x1 -> x2, Pallas kernels: 12.9 us -> 14.4 us  [the longest x1 10.7 us: shards(): pl.pallas_call(cache_kernel, grid=grid, out_shape=(jax.ShapeDtypeStruct((...]
  transfers between devices with their start and end apart: 16 -> 17, of which waited for: 9 -> 6; matrix products, arithmetic and copies ran while one was open for 2% -> 2% of each run, Pallas kernels for 8% -> 8%
where the time goes in v4:
time: 223 us; the launch traced here: 222 us
  waiting for transfers between devices  85.2 us (38%)
  starting transfers between devices  58.3 us (26%)
  blocking collectives  32.7 us (15%)
  Pallas kernels  21 us (9%)
  between operations  15.1 us (7%)
  local copies, waits for them, and re-layouts  7.12 us (3%)
  other arithmetic  2.8 us (1%)
    all_to_all x3, waiting for transfers between devices, shared(): return lax.all_to_all(copies, axes, split_axis=0, concat_axis=0, tiled=True)  37.1 us
    ppermute x11, starting transfers between devices, swapped(): return lax.ppermute(value, axis, [(0, 1), (1, 0)])  33.1 us
    all_to_all x1, blocking collectives, shards(): lax.all_to_all(columns, HEAD, split_axis=0, concat_axis=0, tiled=True)  32.7 us
    ppermute x11, waiting for transfers between devices, swapped(): return lax.ppermute(value, axis, [(0, 1), (1, 0)])  28.7 us
    all_to_all x3, starting transfers between devices, shared(): return lax.all_to_all(copies, axes, split_axis=0, concat_axis=0, tiled=True)  21.6 us
    all_to_all x1, waiting for transfers between devices, shards(): arrived = lax.all_to_all(parts, KV, split_axis=0, concat_axis=0, tiled=True)  19.3 us
    pallas_call x1, Pallas kernels, shards(): pl.pallas_call(cache_kernel, grid=grid, out_shape=(jax.ShapeDtypeStruct((...  10.7 us
    pallas_call x4, Pallas kernels, call(): pl.pallas_call(kernel, out_shape=shapes, in_specs=[SCALAR] + [WHOLE] * le...  6.62 us
  transfers between devices with their start and end apart: 17, of which 6 were waited for; matrix products, arithmetic and copies ran while one was open for 2% of the time, Pallas kernels for 8%

profile of v4, /device:TPU:4, one launch (start us, length us, event | category | flops | bytes accessed | tf_op | source)
XLA Modules:
  0.0 222.2 jit_solution(6255320994883639978)
XLA Ops:
  6.5 2.0 broadcast_in_dim.29
  8.5 7.8 %all-to-all-start = ((bf16[16,128,256]{2,1,0:T(8,128)(2,1)}), bf16[16,128,256]{2,1,0:T(8,128)(2,1)S(1)}, u32[]{:S(2)}, u32[]{:S(2)}) async-start(bf16[16,128,256]{2,1,0:T(8,128)(2,1)} %broadcast_in_dim.29), calls=%async_computation | async-start | bytes 2097152 | tf_op jit(solution)/shard_map/all_to_all | solution.py:30
  16.4 0.0 all-gather.4.cloned.1.call-start
  16.4 0.0 copy-done.6
  16.4 0.7 copy.9
  17.1 0.0 all-gather.4.cloned.1.call-update
  17.1 0.1 pad_add_fusion.place_ref
  17.2 27.9 %all-to-all-done.x_ref = bf16[16,128,256]{2,1,0:T(8,128)(2,1)S(1)} async-done(((bf16[16,128,256]{2,1,0:T(8,128)(2,1)}), bf16[16,128,256]{2,1,0:T(8,128)(2,1)S(1)}, u32[]{:S(2)}, u32[]{:S(2)}) %all-to-all-start) | async-done | bytes 1048608 | tf_op jit(solution)/shard_map/all_to_all | solution.py:30
  45.1 0.9 shard_map.82
  46.0 1.9 collective-permute-start
  47.9 0.0 copy-done.8
  47.9 2.5 %collective-permute-start.9 = (bf16[256,128]{1,0:T(8,128)(2,1)S(1)}, bf16[256,128]{1,0:T(8,128)(2,1)S(1)}, u32[]{:S(2)}, u32[]{:S(2)}) collective-permute-start(bf16[256,128]{1,0:T(8,128)(2,1)S(1)} %copy-done.8), channel_id=1, source_target_pairs={{0,256},{256,0},{1,257},{257,1},{2,258},{258,2},{3,259},{259,3},{4... | collective-permute-start | bytes 196616 | tf_op jit(solution)/shard_map/ppermute | solution.py:34
  50.5 0.0 copy-done.7
  50.5 4.8 %collective-permute-start.1 = (bf16[1,128,256]{2,1,0:T(8,128)(2,1)S(1)}, bf16[1,128,256]{2,1,0:T(8,128)(2,1)S(1)}, u32[]{:S(2)}, u32[]{:S(2)}) collective-permute-start(bf16[1,128,256]{2,1,0:T(8,128)(2,1)S(1)} %bitcast.39), channel_id=1, source_target_pairs={{0,256},{256,0},{1,257},{257,1},{2,258},{258,2},{3,259},{259,3},{4... | collective-permute-start | bytes 196616 | tf_op jit(solution)/shard_map/ppermute | solution.py:34
  55.3 0.8 broadcast_in_dim.30
  56.2 10.3 %all-to-all-start.1 = ((bf16[8,128,256]{2,1,0:T(8,128)(2,1)}), bf16[8,128,256]{2,1,0:T(8,128)(2,1)S(1)}, u32[]{:S(2)}, u32[]{:S(2)}) async-start(bf16[8,128,256]{2,1,0:T(8,128)(2,1)} %broadcast_in_dim.30), calls=%async_computation.1 | async-start | bytes 1048576 | tf_op jit(solution)/shard_map/all_to_all | solution.py:30
  66.5 0.0 all-gather.6.cloned.1.call-start
  66.5 0.0 collective-permute-done.9
  66.5 0.7 pad_maximum_fusion.2
  67.2 0.0 all-gather.6.cloned.1.call-update
  67.2 0.0 collective-permute-done.1
  67.2 7.8 %collective-permute-start.2 = (bf16[1,128,256]{2,1,0:T(8,128)(2,1)S(1)}, bf16[1,128,256]{2,1,0:T(8,128)(2,1)S(1)}, u32[]{:S(2)}, u32[]{:S(2)}) collective-permute-start(bf16[1,128,256]{2,1,0:T(8,128)(2,1)S(1)} %collective-permute-done.1), channel_id=1, source_target_pairs={{0,4},{4,0},{1,5},{5,1},{2,6},{6,2},{3,7},{7,3},{8,12},{12,8},{9,1... | collective-permute-start | bytes 196616 | tf_op jit(solution)/shard_map/ppermute | solution.py:34
  75.1 11.9 %collective-permute-done.2 = bf16[1,128,256]{2,1,0:T(8,128)(2,1)S(1)} collective-permute-done((bf16[1,128,256]{2,1,0:T(8,128)(2,1)S(1)}, bf16[1,128,256]{2,1,0:T(8,128)(2,1)S(1)}, u32[]{:S(2)}, u32[]{:S(2)}) %collective-permute-start.2) | collective-permute-done | bytes 65568 | tf_op jit(solution)/shard_map/ppermute | solution.py:34
  87.0 2.3 %collective-permute-start.3 = (bf16[2,128,256]{2,1,0:T(8,128)(2,1)S(1)}, bf16[2,128,256]{2,1,0:T(8,128)(2,1)S(1)}, u32[]{:S(2)}, u32[]{:S(2)}) collective-permute-start(bf16[2,128,256]{2,1,0:T(8,128)(2,1)S(1)} %pad_maximum_fusion.1), channel_id=1, source_target_pairs={{0,2},{2,0},{1,3},{3,1},{4,6},{6,4},{5,7},{7,5},{8,10},{10,8},{9,1... | collective-permute-start | bytes 393224 | tf_op jit(solution)/shard_map/ppermute | solution.py:34
  89.3 0.0 collective-permute-done.other_ref
  89.4 0.1 pad_maximum_fusion
  89.4 2.7 %collective-permute-start.6 = (bf16[2,4,128,256]{3,2,1,0:T(8,128)(2,1)S(1)}, bf16[2,4,128,256]{3,2,1,0:T(8,128)(2,1)S(1)}, u32[]{:S(2)}, u32[]{:S(2)}) collective-permute-start(bf16[2,4,128,256]{3,2,1,0:T(8,128)(2,1)S(1)} %pad_maximum_fusion), channel_id=1, source_target_pairs={{0,256},{256,0},{1,257},{257,1},{2,258},{258,2},{3,259},{259,3},{4... | collective-permute-start | bytes 1572872 | tf_op jit(solution)/shard_map/ppermute | solution.py:34
  92.1 7.6 %collective-permute-done.3 = bf16[2,128,256]{2,1,0:T(8,128)(2,1)S(1)} collective-permute-done((bf16[2,128,256]{2,1,0:T(8,128)(2,1)S(1)}, bf16[2,128,256]{2,1,0:T(8,128)(2,1)S(1)}, u32[]{:S(2)}, u32[]{:S(2)}) %collective-permute-start.3) | collective-permute-done | bytes 131104 | tf_op jit(solution)/shard_map/ppermute | solution.py:34
  99.8 1.9 collective-permute-start.4
  101.7 9.2 %collective-permute-done.4.away_w_ref = bf16[4,128,256]{2,1,0:T(8,128)(2,1)S(1)} collective-permute-done((bf16[4,128,256]{2,1,0:T(8,128)(2,1)S(1)}, bf16[4,128,256]{2,1,0:T(8,128)(2,1)S(1)}, u32[]{:S(2)}, u32[]{:S(2)}) %collective-permute-start.4) | collective-permute-done | bytes 262176 | tf_op jit(solution)/shard_map/ppermute | solution.py:34
  110.9 0.0 all-to-all-done.1
  110.9 1.1 shard_map.83
  112.0 1.9 collective-permute-start.5
  113.9 0.0 all-gather.4.cloned.1.call-done
  113.9 0.0 collective-permute-done.6.far_ref
  113.9 0.0 copy-start
  113.9 1.2 copy-done
  115.2 2.0 shard_map.84
  117.2 2.5 %collective-permute-start.7 = (f32[2,128,512]{2,1,0:T(8,128)}, f32[2,128,512]{2,1,0:T(8,128)}, u32[]{:S(2)}, u32[]{:S(2)}) collective-permute-start(f32[2,128,512]{2,1,0:T(8,128)} %get-tuple-element.18), channel_id=1, source_target_pairs={{0,128},{128,0},{1,129},{129,1},{2,130},{130,2},{3,131},{131,3},{4... | collective-permute-start | bytes 1572872 | tf_op jit(solution)/shard_map/ppermute | solution.py:34
  119.7 0.0 collective-permute-done.5
  119.8 0.8 broadcast_in_dim.32
  120.6 3.5 %all-to-all-start.2 = ((bf16[8,128,256]{2,1,0:T(8,128)(2,1)}), bf16[8,128,256]{2,1,0:T(8,128)(2,1)S(1)}, u32[]{:S(2)}, u32[]{:S(2)}) async-start(bf16[8,128,256]{2,1,0:T(8,128)(2,1)} %broadcast_in_dim.32), calls=%async_computation.2 | async-start | bytes 1048576 | tf_op jit(solution)/shard_map/all_to_all | solution.py:30
  124.1 0.0 collective-permute-done.7
  124.1 1.2 add.28
  125.3 0.0 copy-start.4
  125.3 0.8 copy-done.4
  126.1 0.7 slice_bitcast_fusion
  126.8 2.7 %collective-permute-start.8 = (f32[128,512]{1,0:T(8,128)}, f32[128,512]{1,0:T(8,128)S(1)}, u32[]{:S(2)}, u32[]{:S(2)}) collective-permute-start(f32[128,512]{1,0:T(8,128)} %slice_bitcast_fusion), channel_id=1, source_target_pairs={{0,256},{256,0},{1,257},{257,1},{2,258},{258,2},{3,259},{259,3},{4... | collective-permute-start | bytes 786440 | tf_op jit(solution)/shard_map/ppermute | solution.py:34
  130.8 0.0 all-gather.6.cloned.1.call-done
  130.9 1.9 collective-permute-start.10
  132.8 9.2 %all-to-all-done.2 = bf16[8,128,256]{2,1,0:T(8,128)(2,1)S(1)} async-done(((bf16[8,128,256]{2,1,0:T(8,128)(2,1)}), bf16[8,128,256]{2,1,0:T(8,128)(2,1)S(1)}, u32[]{:S(2)}, u32[]{:S(2)}) %all-to-all-start.2) | async-done | bytes 524320 | tf_op jit(solution)/shard_map/all_to_all | solution.py:30
  142.0 0.0 copy-done.1
  142.0 0.0 copy-done.2
  142.0 10.7 %attend_cache.1 = (f32[2,1024,128]{2,1,0:T(8,128)S(1)}, f32[2,1024,256]{2,1,0:T(8,128)S(1)}) custom-call(f32[8,2048]{1,0:T(8,128)S(1)} %broadcast_in_dim.35.bias_ref, bf16[1024,256]{1,0:T(8,128)(2,1)S(1)} %bitcast.28, bf16[2048,256]{1,0:T(8,128)(2,1)S(1)} %bitcast.32, bf16[2048,256]{1,0:T(8,128)(2,1)S(1)} %bitcast.33), custom_call_target="tpu_custom_call" | custom-call | tf_op jit(solution)/shard_map/attend_cache/pallas_call | solution.py:234
  152.7 0.0 collective-permute-done.8
  152.7 0.0 copy-done.5
  152.8 0.0 copy-start.3
  152.8 3.7 %attend_new.1 = bf16[8,144,256]{2,1,0:T(8,128)(2,1)} custom-call(s32[3]{0:T(128)S(1)} %pad_add_fusion.place_ref, bf16[1024,256]{1,0:T(8,128)(2,1)S(1)} %bitcast.29, bf16[128,512]{1,0:T(8,128)(2,1)S(1)} %fusion.1.k_ref.v_ref, bf16[128,512]{1,0:T(8,128)(2,1)S(1)} %fusion.1.k_ref.v_ref, f32[2,1024,128]{2,1,0:T(8,128)S(1)} %get-tuple-element.19.peak_ref, ...), custom_call_target="tpu_custom_call" | custom-call | tf_op jit(solution)/shard_map/attend_new/pallas_call | solution.py:248
  156.5 3.5 %all-to-all-start.3 = ((bf16[8,144,256]{2,1,0:T(8,128)(2,1)}), bf16[8,144,256]{2,1,0:T(8,128)(2,1)S(1)}, u32[]{:S(2)}, u32[]{:S(2)}) async-start(bf16[8,144,256]{2,1,0:T(8,128)(2,1)} %attend_new.1), calls=%async_computation.3 | async-start | bytes 1179648 | tf_op jit(solution)/shard_map/all_to_all | solution.py:265
  160.0 0.0 collective-permute-done.10.swap_w_ref
  160.0 19.3 %all-to-all-done.3.parts_ref = bf16[8,144,256]{2,1,0:T(8,128)(2,1)S(1)} async-done(((bf16[8,144,256]{2,1,0:T(8,128)(2,1)}), bf16[8,144,256]{2,1,0:T(8,128)(2,1)S(1)}, u32[]{:S(2)}, u32[]{:S(2)}) %all-to-all-start.3) | async-done | bytes 589856 | tf_op jit(solution)/shard_map/all_to_all | solution.py:265
  179.3 2.6 %shard_map.85 = bf16[16,128,256]{2,1,0:T(8,128)(2,1)S(1)} custom-call(s32[3]{0:T(128)S(1)} %pad_add_fusion.place_ref, bf16[8,144,256]{2,1,0:T(8,128)(2,1)S(1)} %all-to-all-done.3.parts_ref, bf16[8,2,256,128]{3,2,1,0:T(8,128)(2,1)S(1)} %bitcast.35, bf16[8,2,256,128]{3,2,1,0:T(8,128)(2,1)} %collective-permute-done.10.swap_w_ref), custom_call_target="tpu_custom_call" | custom-call | tf_op jit(solution)/shard_map/pallas_call | solution.py:192
  181.9 32.7 %all_to_all.25 = bf16[16,128,256]{2,1,0:T(8,128)(2,1)S(1)} all-to-all(bf16[16,128,256]{2,1,0:T(8,128)(2,1)S(1)} %shard_map.85), channel_id=1, replica_groups=mesh['x_hi'=2,'core'=2,'y'=8,'x_lo'=2,'z_4'=2,'z_2'=2,'z_1'=2] {'y','x_lo'}, dimensions={0} | all-to-all | bytes 2097152 | tf_op jit(solution)/shard_map/all_to_all | solution.py:268
  214.6 0.8 reduce_sum.12
  (17 shorter events, 0.2 us)
Async XLA Ops:
  6.5 9.9 %copy-start.6 = (bf16[128,2,256]{2,1,0:T(2,128)(2,1)S(1)}, bf16[128,2,256]{2,1,0:T(2,128)(2,1)}, u32[]{:S(2)}) copy-start(bf16[128,2,256]{2,1,0:T(2,128)(2,1)} %param.10) | copy-start | bytes 393220
  6.5 41.4 %copy-start.8 = (bf16[256,128]{1,0:T(8,128)(2,1)S(1)}, bf16[256,128]{1,0:T(8,128)(2,1)}, u32[]{:S(2)}) copy-start(bf16[256,128]{1,0:T(8,128)(2,1)} %param.15) | copy-start | bytes 196612
  6.5 43.9 %copy-start.7 = (bf16[128,256]{1,0:T(8,128)(2,1)S(1)}, bf16[128,256]{1,0:T(8,128)(2,1)}, u32[]{:S(2)}) copy-start(bf16[128,256]{1,0:T(8,128)(2,1)} %param.9) | copy-start | bytes 196612
  8.5 36.6 %all-to-all-start = ((bf16[16,128,256]{2,1,0:T(8,128)(2,1)}), bf16[16,128,256]{2,1,0:T(8,128)(2,1)S(1)}, u32[]{:S(2)}, u32[]{:S(2)}) async-start(bf16[16,128,256]{2,1,0:T(8,128)(2,1)} %broadcast_in_dim.29), calls=%async_computation | async-start | bytes 2097152 | tf_op jit(solution)/shard_map/all_to_all | solution.py:30
  16.4 97.6 %all-gather.4.cloned.1.call-start = ((), (), s32[]{:S(2)}) async-start(), calls=%async_computation.5 | async-start | bytes 1179648 | tf_op jit(solution)/shard_map/all_gather | solution.py:205
  46.0 43.3 %collective-permute-start = (bf16[2,4,128,256]{3,2,1,0:T(8,128)(2,1)S(1)}, bf16[2,4,128,256]{3,2,1,0:T(8,128)(2,1)S(1)}, u32[]{:S(2)}, u32[]{:S(2)}) collective-permute-start(bf16[2,4,128,256]{3,2,1,0:T(8,128)(2,1)S(1)} %get-tuple-element.14), channel_id=1, source_target_pairs={{0,128},{128,0},{1,129},{129,1},{2,130},{130,2},{3,131},{131,3},{4... | collective-permute-start | bytes 1572872 | tf_op jit(solution)/shard_map/ppermute | solution.py:34
  47.9 18.6 %collective-permute-start.9 = (bf16[256,128]{1,0:T(8,128)(2,1)S(1)}, bf16[256,128]{1,0:T(8,128)(2,1)S(1)}, u32[]{:S(2)}, u32[]{:S(2)}) collective-permute-start(bf16[256,128]{1,0:T(8,128)(2,1)S(1)} %copy-done.8), channel_id=1, source_target_pairs={{0,256},{256,0},{1,257},{257,1},{2,258},{258,2},{3,259},{259,3},{4... | collective-permute-start | bytes 196616 | tf_op jit(solution)/shard_map/ppermute | solution.py:34
  50.5 16.8 %collective-permute-start.1 = (bf16[1,128,256]{2,1,0:T(8,128)(2,1)S(1)}, bf16[1,128,256]{2,1,0:T(8,128)(2,1)S(1)}, u32[]{:S(2)}, u32[]{:S(2)}) collective-permute-start(bf16[1,128,256]{2,1,0:T(8,128)(2,1)S(1)} %bitcast.39), channel_id=1, source_target_pairs={{0,256},{256,0},{1,257},{257,1},{2,258},{258,2},{3,259},{259,3},{4... | collective-permute-start | bytes 196616 | tf_op jit(solution)/shard_map/ppermute | solution.py:34
  56.2 54.7 %all-to-all-start.1 = ((bf16[8,128,256]{2,1,0:T(8,128)(2,1)}), bf16[8,128,256]{2,1,0:T(8,128)(2,1)S(1)}, u32[]{:S(2)}, u32[]{:S(2)}) async-start(bf16[8,128,256]{2,1,0:T(8,128)(2,1)} %broadcast_in_dim.30), calls=%async_computation.1 | async-start | bytes 1048576 | tf_op jit(solution)/shard_map/all_to_all | solution.py:30
  66.5 64.4 %all-gather.6.cloned.1.call-start = ((), (), s32[]{:S(2)}) async-start(), calls=%async_computation.6 | async-start | bytes 1179648 | tf_op jit(solution)/shard_map/all_gather | solution.py:207
  67.2 19.8 %collective-permute-start.2 = (bf16[1,128,256]{2,1,0:T(8,128)(2,1)S(1)}, bf16[1,128,256]{2,1,0:T(8,128)(2,1)S(1)}, u32[]{:S(2)}, u32[]{:S(2)}) collective-permute-start(bf16[1,128,256]{2,1,0:T(8,128)(2,1)S(1)} %collective-permute-done.1), channel_id=1, source_target_pairs={{0,4},{4,0},{1,5},{5,1},{2,6},{6,2},{3,7},{7,3},{8,12},{12,8},{9,1... | collective-permute-start | bytes 196616 | tf_op jit(solution)/shard_map/ppermute | solution.py:34
  87.0 12.7 %collective-permute-start.3 = (bf16[2,128,256]{2,1,0:T(8,128)(2,1)S(1)}, bf16[2,128,256]{2,1,0:T(8,128)(2,1)S(1)}, u32[]{:S(2)}, u32[]{:S(2)}) collective-permute-start(bf16[2,128,256]{2,1,0:T(8,128)(2,1)S(1)} %pad_maximum_fusion.1), channel_id=1, source_target_pairs={{0,2},{2,0},{1,3},{3,1},{4,6},{6,4},{5,7},{7,5},{8,10},{10,8},{9,1... | collective-permute-start | bytes 393224 | tf_op jit(solution)/shard_map/ppermute | solution.py:34
  89.4 24.5 %collective-permute-start.6 = (bf16[2,4,128,256]{3,2,1,0:T(8,128)(2,1)S(1)}, bf16[2,4,128,256]{3,2,1,0:T(8,128)(2,1)S(1)}, u32[]{:S(2)}, u32[]{:S(2)}) collective-permute-start(bf16[2,4,128,256]{3,2,1,0:T(8,128)(2,1)S(1)} %pad_maximum_fusion), channel_id=1, source_target_pairs={{0,256},{256,0},{1,257},{257,1},{2,258},{258,2},{3,259},{259,3},{4... | collective-permute-start | bytes 1572872 | tf_op jit(solution)/shard_map/ppermute | solution.py:34
  99.8 11.1 %collective-permute-start.4 = (bf16[4,128,256]{2,1,0:T(8,128)(2,1)S(1)}, bf16[4,128,256]{2,1,0:T(8,128)(2,1)S(1)}, u32[]{:S(2)}, u32[]{:S(2)}) collective-permute-start(bf16[4,128,256]{2,1,0:T(8,128)(2,1)S(1)} %constant_dynamic-update-slice_fusion.far_w_ref), channel_id=1, source_target_pairs={{0,1},{1,0},{2,3},{3,2},{4,5},{5,4},{6,7},{7,6},{8,9},{9,8},{10,11... | collective-permute-start | bytes 786440 | tf_op jit(solution)/shard_map/ppermute | solution.py:34
  112.0 7.8 %collective-permute-start.5 = (f32[128,256]{1,0:T(8,128)S(1)}, f32[128,256]{1,0:T(8,128)S(1)}, u32[]{:S(2)}, u32[]{:S(2)}) collective-permute-start(f32[128,256]{1,0:T(8,128)S(1)} %get-tuple-element.16), channel_id=1, source_target_pairs={{0,128},{128,0},{1,129},{129,1},{2,130},{130,2},{3,131},{131,3},{4... | collective-permute-start | bytes 393224 | tf_op jit(solution)/shard_map/ppermute | solution.py:34
  113.9 1.2 copy-start
  117.2 24.8 %copy-start.1 = (bf16[1,2048,256]{2,1,0:T(8,128)(2,1)S(1)}, bf16[1,2048,256]{2,1,0:T(8,128)(2,1)}, u32[]{:S(2)}) copy-start(bf16[1,2048,256]{2,1,0:T(8,128)(2,1)} %param.11) | copy-start | bytes 3145732
  117.2 24.8 %copy-start.2 = (bf16[1,2048,256]{2,1,0:T(8,128)(2,1)S(1)}, bf16[1,2048,256]{2,1,0:T(8,128)(2,1)}, u32[]{:S(2)}) copy-start(bf16[1,2048,256]{2,1,0:T(8,128)(2,1)} %param.12) | copy-start | bytes 3145732
  117.2 6.9 %collective-permute-start.7 = (f32[2,128,512]{2,1,0:T(8,128)}, f32[2,128,512]{2,1,0:T(8,128)}, u32[]{:S(2)}, u32[]{:S(2)}) collective-permute-start(f32[2,128,512]{2,1,0:T(8,128)} %get-tuple-element.18), channel_id=1, source_target_pairs={{0,128},{128,0},{1,129},{129,1},{2,130},{130,2},{3,131},{131,3},{4... | collective-permute-start | bytes 1572872 | tf_op jit(solution)/shard_map/ppermute | solution.py:34
  120.6 21.4 %all-to-all-start.2 = ((bf16[8,128,256]{2,1,0:T(8,128)(2,1)}), bf16[8,128,256]{2,1,0:T(8,128)(2,1)S(1)}, u32[]{:S(2)}, u32[]{:S(2)}) async-start(bf16[8,128,256]{2,1,0:T(8,128)(2,1)} %broadcast_in_dim.32), calls=%async_computation.2 | async-start | bytes 1048576 | tf_op jit(solution)/shard_map/all_to_all | solution.py:30
  125.3 0.8 copy-start.4
  126.8 25.9 %copy-start.5 = (f32[2,128,512]{2,1,0:T(8,128)S(1)}, f32[2,128,512]{2,1,0:T(8,128)}, u32[]{:S(2)}) copy-start(f32[2,128,512]{2,1,0:T(8,128)} %copy-done.4) | copy-start | bytes 1572868
  126.8 25.9 %collective-permute-start.8 = (f32[128,512]{1,0:T(8,128)}, f32[128,512]{1,0:T(8,128)S(1)}, u32[]{:S(2)}, u32[]{:S(2)}) collective-permute-start(f32[128,512]{1,0:T(8,128)} %slice_bitcast_fusion), channel_id=1, source_target_pairs={{0,256},{256,0},{1,257},{257,1},{2,258},{258,2},{3,259},{259,3},{4... | collective-permute-start | bytes 786440 | tf_op jit(solution)/shard_map/ppermute | solution.py:34
  130.9 29.1 %collective-permute-start.10 = (bf16[8,2,256,128]{3,2,1,0:T(8,128)(2,1)}, bf16[8,2,256,128]{3,2,1,0:T(8,128)(2,1)}, u32[]{:S(2)}, u32[]{:S(2)}) collective-permute-start(bf16[8,2,256,128]{3,2,1,0:T(8,128)(2,1)} %bitcast.34), channel_id=1, source_target_pairs={{0,128},{128,0},{1,129},{129,1},{2,130},{130,2},{3,131},{131,3},{4... | collective-permute-start | bytes 3145736 | tf_op jit(solution)/shard_map/ppermute | solution.py:34
  152.8 26.5 %copy-start.3 = (bf16[16,256,128]{2,1,0:T(8,128)(2,1)S(1)}, bf16[16,256,128]{2,1,0:T(8,128)(2,1)}, u32[]{:S(2)}) copy-start(bf16[16,256,128]{2,1,0:T(8,128)(2,1)} %all-gather.6.cloned.1.call-done) | copy-start | bytes 3145732
  156.5 22.9 %all-to-all-start.3 = ((bf16[8,144,256]{2,1,0:T(8,128)(2,1)}), bf16[8,144,256]{2,1,0:T(8,128)(2,1)S(1)}, u32[]{:S(2)}, u32[]{:S(2)}) async-start(bf16[8,144,256]{2,1,0:T(8,128)(2,1)} %attend_new.1), calls=%async_computation.3 | async-start | bytes 1179648 | tf_op jit(solution)/shard_map/all_to_all | solution.py:265
Sparse Core Ops, SparseCore 0:
  19.2 46.4 all-gather.3
  69.4 40.7 all-gather.5

commit v5 on v4

--- a/solution.py
+++ b/solution.py
@@ -51,15 +51,19 @@
                 out_ref[far, j] = (x * factor).astype(jnp.bfloat16)
 
 
+def both_rows(w_ref, at):
+    return jnp.concatenate([w_ref[2 * at], w_ref[2 * at + 1]], axis=0)
+
+
 def query_kernel(place_ref, keep_ref, other_ref, w_ref, far_w_ref, away_w_ref, own_out, other_out):
     kv = place_ref[2]
     lanes = far_w_ref.shape[1]
     near = pl.multiple_of((kv & 1) * lanes, lanes)
     away = pl.multiple_of((1 - (kv & 1)) * lanes, lanes)
     total = None
-    for at in range(w_ref.shape[0]):
+    for at in range(w_ref.shape[0] // 2):
         x = jnp.concatenate([keep_ref[0, at], other_ref[0, at]], axis=0)
-        part = dot(x, w_ref[at])
+        part = dot(x, both_rows(w_ref, at))
         total = part if total is None else total + part
     for at in range(far_w_ref.shape[0]):
         flip_4, flip_2 = at % 2, at // 2
@@ -71,16 +75,17 @@
     other_out[...] = total[own_out.shape[0] :]
 
 
-def pair_kernel(place_ref, keep_ref, other_ref, far_ref, w_ref, own_out, other_out):
-    total = None
-    for at in range(w_ref.shape[0]):
-        x = [keep_ref[0, at], far_ref[0, at], other_ref[0, at], far_ref[1, at]]
-        part = dot(jnp.concatenate(x, axis=0), w_ref[at])
-        total = part if total is None else total + part
-    rows = own_out.shape[1]
-    for n in range(2):
-        own_out[n] = total[n * rows : (n + 1) * rows]
-        other_out[n] = total[(n + 2) * rows : (n + 3) * rows]
+def pair_kernel(place_ref, keep_ref, other_ref, far_ref, key_w_ref, value_w_ref, own_out, other_out):
+    rows, width = own_out.shape[1], key_w_ref.shape[2]
+    for lane, w_ref in ((0, key_w_ref), (width, value_w_ref)):
+        total = None
+        for at in range(w_ref.shape[0] // 2):
+            x = [keep_ref[0, at], far_ref[0, at], other_ref[0, at], far_ref[1, at]]
+            part = dot(jnp.concatenate(x, axis=0), both_rows(w_ref, at))
+            total = part if total is None else total + part
+        for n in range(2):
+            own_out[n, :, lane : lane + width] = total[n * rows : (n + 1) * rows]
+            other_out[n, :, lane : lane + width] = total[(n + 2) * rows : (n + 3) * rows]
 
 
 def thirds(value):
@@ -143,7 +148,7 @@
         out_ref[b, own:] = stats.astype(jnp.bfloat16)
 
 
-def finish_kernel(place_ref, parts_ref, w_ref, swap_w_ref, out_ref):
+def finish_kernel(place_ref, parts_ref, w_ref, far_w_ref, swap_w_ref, swap_far_w_ref, out_ref):
     x_hi, core = place_ref[0], place_ref[1]
     sources, rows, width = parts_ref.shape
     own = rows - STAT_ROWS
@@ -165,14 +170,15 @@
             mixture = part if mixture is None else mixture + part
         heads.append(mixture.astype(jnp.bfloat16))
     attended = jnp.concatenate(heads, axis=1)
-    lanes = w_ref.shape[3]
+    lanes = w_ref.shape[1]
+    sides = ((w_ref, x_hi, core), (far_w_ref, 1 - x_hi, core))
+    sides += ((swap_w_ref, x_hi, 1 - core), (swap_far_w_ref, 1 - x_hi, 1 - core))
     for at in range(w_ref.shape[0]):
         lane = slice(at % 2 * lanes, (at % 2 + 1) * lanes)
-        for far in range(2):
-            section = 2 * (1 - x_hi if far else x_hi)
-            for ref, side in ((w_ref, core), (swap_w_ref, 1 - core)):
-                to = (section + side) * 4 + at // 2
-                out_ref[to, :, lane] = dot(attended, ref[at, far]).astype(jnp.bfloat16)
+        for ref, half, side in sides:
+            w = jnp.concatenate([ref[at, :, :lanes], ref[at, :, lanes:]], axis=0)
+            to = (2 * half + side) * 4 + at // 2
+            out_ref[to, :, lane] = dot(attended, w).astype(jnp.bfloat16)
 
 
 def doubled(value, axes):
@@ -188,36 +194,44 @@
     kv_count = lax.axis_size(KV)
     own = jnp.stack([lax.axis_index("x_hi"), lax.axis_index("core"), kv]).astype(jnp.int32)
 
+    def part_of_weights(index):
+        block = (kv_count, local_rows, width)
+        operand = pltpu.with_memory_space_constraint(weights, pltpu.HBM)
+        return pl.BlockSpec(block, lambda i: (0, index, 0)), operand
+
     def call(kernel, shapes, *operands):
+        pairs = [o if isinstance(o, tuple) else (WHOLE, o) for o in operands]
         return pl.pallas_call(
             kernel,
+            grid=(1,),
             out_shape=shapes,
-            in_specs=[SCALAR] + [WHOLE] * len(operands),
+            in_specs=[SCALAR] + [spec for spec, _ in pairs],
             out_specs=jax.tree.map(lambda _: WHOLE, shapes),
             compiler_params=VMEM,
-        )(own, *operands)
+        )(own, *(operand for _, operand in pairs))
 
     gathered = shared(tokens[0], HEAD)
     query_w_far = swapped(w_query[None], "x_hi")
-    out_w = jnp.stack([w_out, swapped(w_out, "x_hi")])
     query_w_far = doubled(query_w_far, KV)
-    query_w = shared(w_query, KV).reshape(4, -1, width)
-    pair_w = lax.all_gather(w_keyvalue.reshape(-1, 2 * width), KV, axis=0, tiled=True)
-    pair_w = pair_w.reshape(4, -1, 2 * width)
-    out_w = lax.all_gather(out_w, KV, axis=0, tiled=False)
-    out_w = (out_w, swapped(out_w, "core"))
+    out_w = jnp.concatenate([w_out[:local_rows], w_out[local_rows:]], axis=1)
+    weights = jnp.concatenate([w_query, w_keyvalue[:, 0], w_keyvalue[:, 1], out_w], axis=0)
+    weights = lax.all_gather(weights, KV, axis=0, tiled=False)
+    out_w = weights[:, 3 * local_rows :]
+    out_w_far = swapped(out_w, "x_hi")
+    out_w_core = swapped(out_w, "core")
+    out_w_both = swapped(out_w_far, "core")
 
     half = jax.ShapeDtypeStruct((2, 4, local_rows, width), jnp.bfloat16)
     keep, send = call(normalize_kernel, (half, half), gathered)
     other = swapped(send, "core")
     partial = jax.ShapeDtypeStruct((local_rows, width), jnp.float32)
-    mine, theirs = call(query_kernel, (partial, partial), keep, other, query_w, *query_w_far)
+    mine, theirs = call(query_kernel, (partial, partial), keep, other, part_of_weights(0), *query_w_far)
     queries = (mine + swapped(theirs, "core")).astype(jnp.bfloat16)
     queries = shared(queries, KV).reshape(-1, width)
 
     far = swapped(jnp.stack([keep[1], other[1]]), "x_hi")
     partial = jax.ShapeDtypeStruct((2, local_rows, 2 * width), jnp.float32)
-    mine, theirs = call(pair_kernel, (partial, partial), keep, other, far, pair_w)
+    mine, theirs = call(pair_kernel, (partial, partial), keep, other, far, part_of_weights(1), part_of_weights(2))
     mine = mine + swapped(theirs, "core")
     pair = (mine[0] + swapped(mine[1], "x_hi")).astype(jnp.bfloat16)
     place = kv * cache_rows + lax.iota(jnp.int32, cache_rows)
@@ -264,7 +278,7 @@
 
     arrived = lax.all_to_all(parts, KV, split_axis=0, concat_axis=0, tiled=True)
     blocks = jax.ShapeDtypeStruct((lax.axis_size(HEAD), local_rows, width), jnp.bfloat16)
-    columns = call(finish_kernel, blocks, arrived, *out_w)
+    columns = call(finish_kernel, blocks, arrived, out_w, out_w_far, out_w_core, out_w_both)
     columns = lax.all_to_all(columns, HEAD, split_axis=0, concat_axis=0, tiled=True)
     return columns.astype(jnp.float32).sum(axis=0).astype(jnp.bfloat16)[None]
 

time: 223 us -> 205 us (0.919)
  the two profiles are of different devices: /device:TPU:4 before, /device:TPU:2 now
where the time goes in v5:
time: 205 us; the launch traced here: 204 us
  starting transfers between devices  63.1 us (31%)
  waiting for transfers between devices  59.9 us (29%)
  blocking collectives  30.9 us (15%)
  Pallas kernels  22 us (11%)
  between operations  15 us (7%)
  local copies, waits for them, and re-layouts  8.3 us (4%)
  other arithmetic  4.79 us (2%)
    ppermute x12, starting transfers between devices, swapped(): return lax.ppermute(value, axis, [(0, 1), (1, 0)])  43.7 us
    all_to_all x1, blocking collectives, shards(): lax.all_to_all(columns, HEAD, split_axis=0, concat_axis=0, tiled=True)  30.9 us
    all_to_all x2, waiting for transfers between devices, shared(): return lax.all_to_all(copies, axes, split_axis=0, concat_axis=0, tiled=True)  28.8 us
    ppermute x12, waiting for transfers between devices, swapped(): return lax.ppermute(value, axis, [(0, 1), (1, 0)])  19 us
    all_to_all x2, starting transfers between devices, shared(): return lax.all_to_all(copies, axes, split_axis=0, concat_axis=0, tiled=True)  14.8 us
    all_to_all x1, waiting for transfers between devices, shards(): arrived = lax.all_to_all(parts, KV, split_axis=0, concat_axis=0, tiled=True)  12.1 us
    pallas_call x1, Pallas kernels, shards(): pl.pallas_call(cache_kernel, grid=grid, out_shape=(jax.ShapeDtypeStruct((...  10.7 us
    pallas_call x4, Pallas kernels, call(): pl.pallas_call(kernel, grid=(1,), out_shape=shapes, in_specs=[SCALAR] + [...  7.59 us
  transfers between devices with their start and end apart: 16, of which 9 were waited for; matrix products, arithmetic and copies ran while one was open for 3% of the time, Pallas kernels for 10%

profile of v5, /device:TPU:2, one launch (start us, length us, event | category | flops | bytes accessed | tf_op | source)
XLA Modules:
  0.0 204.0 jit_solution(4450260895089895517)
XLA Ops:
  6.5 0.0 all-gather.3.cloned.1.call-start
  6.5 1.2 fusion.6
  7.8 0.8 fusion.7
  8.6 1.6 maximum_maximum_fusion
  10.1 0.0 all-gather.3.cloned.1.call-update
  10.1 0.0 copy-start.5
  10.2 2.0 broadcast_in_dim.26
  12.1 9.3 %all-to-all-start = ((bf16[16,128,256]{2,1,0:T(8,128)(2,1)}), bf16[16,128,256]{2,1,0:T(8,128)(2,1)S(1)}, u32[]{:S(2)}, u32[]{:S(2)}) async-start(bf16[16,128,256]{2,1,0:T(8,128)(2,1)} %broadcast_in_dim.26), calls=%async_computation | async-start | bytes 2097152 | tf_op jit(solution)/shard_map/all_to_all | solution.py:30
  21.4 0.1 pad_add_fusion.place_ref
  21.5 26.5 %all-to-all-done.x_ref = bf16[16,128,256]{2,1,0:T(8,128)(2,1)S(1)} async-done(((bf16[16,128,256]{2,1,0:T(8,128)(2,1)}), bf16[16,128,256]{2,1,0:T(8,128)(2,1)S(1)}, u32[]{:S(2)}, u32[]{:S(2)}) %all-to-all-start) | async-done | bytes 1048608 | tf_op jit(solution)/shard_map/all_to_all | solution.py:30
  48.0 0.9 shard_map.82
  48.9 1.9 collective-permute-start
  50.8 0.0 copy-done.5
  50.8 3.9 %collective-permute-start.1 = (bf16[1,128,256]{2,1,0:T(8,128)(2,1)S(1)}, bf16[1,128,256]{2,1,0:T(8,128)(2,1)S(1)}, u32[]{:S(2)}, u32[]{:S(2)}) collective-permute-start(bf16[1,128,256]{2,1,0:T(8,128)(2,1)S(1)} %bitcast.35), channel_id=1, source_target_pairs={{0,256},{256,0},{1,257},{257,1},{2,258},{258,2},{3,259},{259,3},{4... | collective-permute-start | bytes 196616 | tf_op jit(solution)/shard_map/ppermute | solution.py:34
  54.8 4.0 %collective-permute-done.1 = bf16[1,128,256]{2,1,0:T(8,128)(2,1)S(1)} collective-permute-done((bf16[1,128,256]{2,1,0:T(8,128)(2,1)S(1)}, bf16[1,128,256]{2,1,0:T(8,128)(2,1)S(1)}, u32[]{:S(2)}, u32[]{:S(2)}) %collective-permute-start.1) | collective-permute-done | bytes 65568 | tf_op jit(solution)/shard_map/ppermute | solution.py:34
  58.7 10.8 %collective-permute-start.2 = (bf16[1,128,256]{2,1,0:T(8,128)(2,1)S(1)}, bf16[1,128,256]{2,1,0:T(8,128)(2,1)S(1)}, u32[]{:S(2)}, u32[]{:S(2)}) collective-permute-start(bf16[1,128,256]{2,1,0:T(8,128)(2,1)S(1)} %collective-permute-done.1), channel_id=1, source_target_pairs={{0,4},{4,0},{1,5},{5,1},{2,6},{6,2},{3,7},{7,3},{8,12},{12,8},{9,1... | collective-permute-start | bytes 196616 | tf_op jit(solution)/shard_map/ppermute | solution.py:34
  69.5 2.8 %collective-permute-done.2 = bf16[1,128,256]{2,1,0:T(8,128)(2,1)S(1)} collective-permute-done((bf16[1,128,256]{2,1,0:T(8,128)(2,1)S(1)}, bf16[1,128,256]{2,1,0:T(8,128)(2,1)S(1)}, u32[]{:S(2)}, u32[]{:S(2)}) %collective-permute-start.2) | collective-permute-done | bytes 65568 | tf_op jit(solution)/shard_map/ppermute | solution.py:34
  72.4 4.8 %collective-permute-start.3 = (bf16[2,128,256]{2,1,0:T(8,128)(2,1)S(1)}, bf16[2,128,256]{2,1,0:T(8,128)(2,1)S(1)}, u32[]{:S(2)}, u32[]{:S(2)}) collective-permute-start(bf16[2,128,256]{2,1,0:T(8,128)(2,1)S(1)} %pad_maximum_fusion.1), channel_id=1, source_target_pairs={{0,2},{2,0},{1,3},{3,1},{4,6},{6,4},{5,7},{7,5},{8,10},{10,8},{9,1... | collective-permute-start | bytes 393224 | tf_op jit(solution)/shard_map/ppermute | solution.py:34
  77.3 0.0 collective-permute-done.other_ref
  77.3 0.1 pad_maximum_fusion
  77.3 4.0 %collective-permute-start.6 = (bf16[2,4,128,256]{3,2,1,0:T(8,128)(2,1)S(1)}, bf16[2,4,128,256]{3,2,1,0:T(8,128)(2,1)S(1)}, u32[]{:S(2)}, u32[]{:S(2)}) collective-permute-start(bf16[2,4,128,256]{3,2,1,0:T(8,128)(2,1)S(1)} %pad_maximum_fusion), channel_id=1, source_target_pairs={{0,256},{256,0},{1,257},{257,1},{2,258},{258,2},{3,259},{259,3},{4... | collective-permute-start | bytes 1572872 | tf_op jit(solution)/shard_map/ppermute | solution.py:34
  81.4 1.1 collective-permute-done.3
  82.5 2.1 %collective-permute-start.4 = (bf16[4,128,256]{2,1,0:T(8,128)(2,1)S(1)}, bf16[4,128,256]{2,1,0:T(8,128)(2,1)S(1)}, u32[]{:S(2)}, u32[]{:S(2)}) collective-permute-start(bf16[4,128,256]{2,1,0:T(8,128)(2,1)S(1)} %constant_dynamic-update-slice_fusion.far_w_ref), channel_id=1, source_target_pairs={{0,1},{1,0},{2,3},{3,2},{4,5},{5,4},{6,7},{7,6},{8,9},{9,8},{10,11... | collective-permute-start | bytes 786440 | tf_op jit(solution)/shard_map/ppermute | solution.py:34
  84.6 7.6 %collective-permute-done.4.away_w_ref = bf16[4,128,256]{2,1,0:T(8,128)(2,1)S(1)} collective-permute-done((bf16[4,128,256]{2,1,0:T(8,128)(2,1)S(1)}, bf16[4,128,256]{2,1,0:T(8,128)(2,1)S(1)}, u32[]{:S(2)}, u32[]{:S(2)}) %collective-permute-start.4) | collective-permute-done | bytes 262176 | tf_op jit(solution)/shard_map/ppermute | solution.py:34
  92.2 0.0 all-gather.3.cloned.1.call-done
  92.2 1.6 shard_map.83
  93.8 1.9 collective-permute-start.5
  95.7 0.0 collective-permute-done.6.far_ref
  95.8 2.7 %shard_map.84 = (f32[2,128,512]{2,1,0:T(8,128)S(1)}, f32[2,128,512]{2,1,0:T(8,128)}) custom-call(s32[3]{0:T(128)S(1)} %pad_add_fusion.place_ref, bf16[2,4,128,256]{3,2,1,0:T(8,128)(2,1)S(1)} %get-tuple-element.13.keep_ref, bf16[2,4,128,256]{3,2,1,0:T(8,128)(2,1)S(1)} %collective-permute-done.other_ref, ...), custom_call_target="tpu_custom_call" | custom-call | tf_op jit(solution)/shard_map/pallas_call | solution.py:204
  98.5 0.0 copy-start.2
  98.5 0.8 copy-done.2
  99.3 0.0 copy-start.3
  99.3 2.5 %collective-permute-start.7 = (f32[2,128,512]{2,1,0:T(8,128)}, f32[2,128,512]{2,1,0:T(8,128)}, u32[]{:S(2)}, u32[]{:S(2)}) collective-permute-start(f32[2,128,512]{2,1,0:T(8,128)} %get-tuple-element.18), channel_id=1, source_target_pairs={{0,128},{128,0},{1,129},{129,1},{2,130},{130,2},{3,131},{131,3},{4... | collective-permute-start | bytes 1572872 | tf_op jit(solution)/shard_map/ppermute | solution.py:34
  101.8 0.0 collective-permute-done.5
  101.8 0.8 broadcast_in_dim.28
  102.7 5.5 %all-to-all-start.1 = ((bf16[8,128,256]{2,1,0:T(8,128)(2,1)}), bf16[8,128,256]{2,1,0:T(8,128)(2,1)S(1)}, u32[]{:S(2)}, u32[]{:S(2)}) async-start(bf16[8,128,256]{2,1,0:T(8,128)(2,1)} %broadcast_in_dim.28), calls=%async_computation.1 | async-start | bytes 1048576 | tf_op jit(solution)/shard_map/all_to_all | solution.py:30
  108.2 0.0 copy-start
  108.2 0.0 copy-start.1
  108.2 0.0 collective-permute-done.7
  108.2 0.0 copy-done.3
  108.2 1.3 add.28
  109.5 0.0 copy-start.4
  109.5 0.8 copy-done.4
  110.3 0.7 slice_bitcast_fusion
  111.0 4.0 %collective-permute-start.8 = (f32[128,512]{1,0:T(8,128)}, f32[128,512]{1,0:T(8,128)S(1)}, u32[]{:S(2)}, u32[]{:S(2)}) collective-permute-start(f32[128,512]{1,0:T(8,128)} %slice_bitcast_fusion), channel_id=1, source_target_pairs={{0,256},{256,0},{1,257},{257,1},{2,258},{258,2},{3,259},{259,3},{4... | collective-permute-start | bytes 786440 | tf_op jit(solution)/shard_map/ppermute | solution.py:34
  116.4 1.1 slice.39.w_ref
  117.4 3.3 %collective-permute-start.9 = (bf16[8,128,256]{2,1,0:T(8,128)(2,1)S(1)}, bf16[8,128,256]{2,1,0:T(8,128)(2,1)}, u32[]{:S(2)}, u32[]{:S(2)}) collective-permute-start(bf16[8,128,256]{2,1,0:T(8,128)(2,1)S(1)} %slice.39.w_ref), channel_id=1, source_target_pairs={{0,256},{256,0},{1,257},{257,1},{2,258},{258,2},{3,259},{259,3},{4... | collective-permute-start | bytes 1572872 | tf_op jit(solution)/shard_map/ppermute | solution.py:34
  120.8 1.8 collective-permute-done.8
  122.6 1.0 fusion.1.k_ref.v_ref
  123.6 2.3 %all-to-all-done.1 = bf16[8,128,256]{2,1,0:T(8,128)(2,1)S(1)} async-done(((bf16[8,128,256]{2,1,0:T(8,128)(2,1)}), bf16[8,128,256]{2,1,0:T(8,128)(2,1)S(1)}, u32[]{:S(2)}, u32[]{:S(2)}) %all-to-all-start.1) | async-done | bytes 524320 | tf_op jit(solution)/shard_map/all_to_all | solution.py:30
  125.8 0.0 copy-done
  125.9 0.0 copy-done.1
  125.9 10.7 %attend_cache.1 = (f32[2,1024,128]{2,1,0:T(8,128)S(1)}, f32[2,1024,256]{2,1,0:T(8,128)S(1)}) custom-call(f32[8,2048]{1,0:T(8,128)S(1)} %broadcast_in_dim.31.bias_ref, bf16[1024,256]{1,0:T(8,128)(2,1)S(1)} %bitcast.26, bf16[2048,256]{1,0:T(8,128)(2,1)S(1)} %bitcast.28, bf16[2048,256]{1,0:T(8,128)(2,1)S(1)} %bitcast.29), custom_call_target="tpu_custom_call" | custom-call | tf_op jit(solution)/shard_map/attend_cache/pallas_call | solution.py:248
  136.6 3.7 %attend_new.1 = bf16[8,144,256]{2,1,0:T(8,128)(2,1)} custom-call(s32[3]{0:T(128)S(1)} %pad_add_fusion.place_ref, bf16[1024,256]{1,0:T(8,128)(2,1)S(1)} %bitcast.27, bf16[128,512]{1,0:T(8,128)(2,1)S(1)} %fusion.1.k_ref.v_ref, bf16[128,512]{1,0:T(8,128)(2,1)S(1)} %fusion.1.k_ref.v_ref, f32[2,1024,128]{2,1,0:T(8,128)S(1)} %get-tuple-element.19.peak_ref, ...), custom_call_target="tpu_custom_call" | custom-call | tf_op jit(solution)/shard_map/attend_new/pallas_call | solution.py:262
  140.2 4.6 %all-to-all-start.2 = ((bf16[8,144,256]{2,1,0:T(8,128)(2,1)}), bf16[8,144,256]{2,1,0:T(8,128)(2,1)S(1)}, u32[]{:S(2)}, u32[]{:S(2)}) async-start(bf16[8,144,256]{2,1,0:T(8,128)(2,1)} %attend_new.1), calls=%async_computation.2 | async-start | bytes 1179648 | tf_op jit(solution)/shard_map/all_to_all | solution.py:279
  144.9 1.9 collective-permute-start.10
  146.8 0.0 collective-permute-done.9.far_w_ref
  146.8 2.4 %collective-permute-start.11 = (bf16[8,128,256]{2,1,0:T(8,128)(2,1)}, bf16[8,128,256]{2,1,0:T(8,128)(2,1)S(1)}, u32[]{:S(2)}, u32[]{:S(2)}) collective-permute-start(bf16[8,128,256]{2,1,0:T(8,128)(2,1)} %collective-permute-done.9.far_w_ref), channel_id=1, source_target_pairs={{0,128},{128,0},{1,129},{129,1},{2,130},{130,2},{3,131},{131,3},{4... | collective-permute-start | bytes 1572872 | tf_op jit(solution)/shard_map/ppermute | solution.py:34
  149.2 0.0 collective-permute-done.10.swap_w_ref
  149.2 1.7 collective-permute-done.11.swap_far_w_ref
  150.9 12.1 %all-to-all-done.2.parts_ref = bf16[8,144,256]{2,1,0:T(8,128)(2,1)S(1)} async-done(((bf16[8,144,256]{2,1,0:T(8,128)(2,1)}), bf16[8,144,256]{2,1,0:T(8,128)(2,1)S(1)}, u32[]{:S(2)}, u32[]{:S(2)}) %all-to-all-start.2) | async-done | bytes 589856 | tf_op jit(solution)/shard_map/all_to_all | solution.py:279
  163.1 2.4 %shard_map.85 = bf16[16,128,256]{2,1,0:T(8,128)(2,1)S(1)} custom-call(s32[3]{0:T(128)S(1)} %pad_add_fusion.place_ref, bf16[8,144,256]{2,1,0:T(8,128)(2,1)S(1)} %all-to-all-done.2.parts_ref, bf16[8,128,256]{2,1,0:T(8,128)(2,1)S(1)} %slice.39.w_ref, bf16[8,128,256]{2,1,0:T(8,128)(2,1)} %collective-permute-done.9.far_w_ref, ...), custom_call_target="tpu_custom_call" | custom-call | tf_op jit(solution)/shard_map/pallas_call | solution.py:204
  165.4 30.9 %all_to_all.20 = bf16[16,128,256]{2,1,0:T(8,128)(2,1)S(1)} all-to-all(bf16[16,128,256]{2,1,0:T(8,128)(2,1)S(1)} %shard_map.85), channel_id=1, replica_groups=mesh['x_hi'=2,'core'=2,'y'=8,'x_lo'=2,'z_4'=2,'z_2'=2,'z_1'=2] {'y','x_lo'}, dimensions={0} | all-to-all | bytes 2097152 | tf_op jit(solution)/shard_map/all_to_all | solution.py:282
  196.3 0.8 reduce_sum.12
  (10 shorter events, 0.1 us)
Async XLA Ops:
  6.5 85.7 %all-gather.3.cloned.1.call-start = ((), (), s32[]{:S(2)}) async-start(), calls=%async_computation.4 | async-start | bytes 2359296 | tf_op jit(solution)/shard_map/all_gather | solution.py:218
  10.1 40.7 %copy-start.5 = (bf16[128,256]{1,0:T(8,128)(2,1)S(1)}, bf16[128,256]{1,0:T(8,128)(2,1)}, u32[]{:S(2)}) copy-start(bf16[128,256]{1,0:T(8,128)(2,1)} %param.9) | copy-start | bytes 196612
  12.1 35.9 %all-to-all-start = ((bf16[16,128,256]{2,1,0:T(8,128)(2,1)}), bf16[16,128,256]{2,1,0:T(8,128)(2,1)S(1)}, u32[]{:S(2)}, u32[]{:S(2)}) async-start(bf16[16,128,256]{2,1,0:T(8,128)(2,1)} %broadcast_in_dim.26), calls=%async_computation | async-start | bytes 2097152 | tf_op jit(solution)/shard_map/all_to_all | solution.py:30
  48.9 28.4 %collective-permute-start = (bf16[2,4,128,256]{3,2,1,0:T(8,128)(2,1)S(1)}, bf16[2,4,128,256]{3,2,1,0:T(8,128)(2,1)S(1)}, u32[]{:S(2)}, u32[]{:S(2)}) collective-permute-start(bf16[2,4,128,256]{3,2,1,0:T(8,128)(2,1)S(1)} %get-tuple-element.14), channel_id=1, source_target_pairs={{0,128},{128,0},{1,129},{129,1},{2,130},{130,2},{3,131},{131,3},{4... | collective-permute-start | bytes 1572872 | tf_op jit(solution)/shard_map/ppermute | solution.py:34
  50.8 7.9 %collective-permute-start.1 = (bf16[1,128,256]{2,1,0:T(8,128)(2,1)S(1)}, bf16[1,128,256]{2,1,0:T(8,128)(2,1)S(1)}, u32[]{:S(2)}, u32[]{:S(2)}) collective-permute-start(bf16[1,128,256]{2,1,0:T(8,128)(2,1)S(1)} %bitcast.35), channel_id=1, source_target_pairs={{0,256},{256,0},{1,257},{257,1},{2,258},{258,2},{3,259},{259,3},{4... | collective-permute-start | bytes 196616 | tf_op jit(solution)/shard_map/ppermute | solution.py:34
  58.7 13.7 %collective-permute-start.2 = (bf16[1,128,256]{2,1,0:T(8,128)(2,1)S(1)}, bf16[1,128,256]{2,1,0:T(8,128)(2,1)S(1)}, u32[]{:S(2)}, u32[]{:S(2)}) collective-permute-start(bf16[1,128,256]{2,1,0:T(8,128)(2,1)S(1)} %collective-permute-done.1), channel_id=1, source_target_pairs={{0,4},{4,0},{1,5},{5,1},{2,6},{6,2},{3,7},{7,3},{8,12},{12,8},{9,1... | collective-permute-start | bytes 196616 | tf_op jit(solution)/shard_map/ppermute | solution.py:34
  72.4 10.1 %collective-permute-start.3 = (bf16[2,128,256]{2,1,0:T(8,128)(2,1)S(1)}, bf16[2,128,256]{2,1,0:T(8,128)(2,1)S(1)}, u32[]{:S(2)}, u32[]{:S(2)}) collective-permute-start(bf16[2,128,256]{2,1,0:T(8,128)(2,1)S(1)} %pad_maximum_fusion.1), channel_id=1, source_target_pairs={{0,2},{2,0},{1,3},{3,1},{4,6},{6,4},{5,7},{7,5},{8,10},{10,8},{9,1... | collective-permute-start | bytes 393224 | tf_op jit(solution)/shard_map/ppermute | solution.py:34
  77.3 18.4 %collective-permute-start.6 = (bf16[2,4,128,256]{3,2,1,0:T(8,128)(2,1)S(1)}, bf16[2,4,128,256]{3,2,1,0:T(8,128)(2,1)S(1)}, u32[]{:S(2)}, u32[]{:S(2)}) collective-permute-start(bf16[2,4,128,256]{3,2,1,0:T(8,128)(2,1)S(1)} %pad_maximum_fusion), channel_id=1, source_target_pairs={{0,256},{256,0},{1,257},{257,1},{2,258},{258,2},{3,259},{259,3},{4... | collective-permute-start | bytes 1572872 | tf_op jit(solution)/shard_map/ppermute | solution.py:34
  82.5 9.7 %collective-permute-start.4 = (bf16[4,128,256]{2,1,0:T(8,128)(2,1)S(1)}, bf16[4,128,256]{2,1,0:T(8,128)(2,1)S(1)}, u32[]{:S(2)}, u32[]{:S(2)}) collective-permute-start(bf16[4,128,256]{2,1,0:T(8,128)(2,1)S(1)} %constant_dynamic-update-slice_fusion.far_w_ref), channel_id=1, source_target_pairs={{0,1},{1,0},{2,3},{3,2},{4,5},{5,4},{6,7},{7,6},{8,9},{9,8},{10,11... | collective-permute-start | bytes 786440 | tf_op jit(solution)/shard_map/ppermute | solution.py:34
  93.8 8.0 %collective-permute-start.5 = (f32[128,256]{1,0:T(8,128)S(1)}, f32[128,256]{1,0:T(8,128)S(1)}, u32[]{:S(2)}, u32[]{:S(2)}) collective-permute-start(f32[128,256]{1,0:T(8,128)S(1)} %get-tuple-element.16), channel_id=1, source_target_pairs={{0,128},{128,0},{1,129},{129,1},{2,130},{130,2},{3,131},{131,3},{4... | collective-permute-start | bytes 393224 | tf_op jit(solution)/shard_map/ppermute | solution.py:34
  98.5 0.8 copy-start.2
  99.3 8.9 %copy-start.3 = (f32[2,128,512]{2,1,0:T(8,128)S(1)}, f32[2,128,512]{2,1,0:T(8,128)}, u32[]{:S(2)}) copy-start(f32[2,128,512]{2,1,0:T(8,128)} %copy-done.2) | copy-start | bytes 1572868
  99.3 8.9 %collective-permute-start.7 = (f32[2,128,512]{2,1,0:T(8,128)}, f32[2,128,512]{2,1,0:T(8,128)}, u32[]{:S(2)}, u32[]{:S(2)}) collective-permute-start(f32[2,128,512]{2,1,0:T(8,128)} %get-tuple-element.18), channel_id=1, source_target_pairs={{0,128},{128,0},{1,129},{129,1},{2,130},{130,2},{3,131},{131,3},{4... | collective-permute-start | bytes 1572872 | tf_op jit(solution)/shard_map/ppermute | solution.py:34
  102.7 23.1 %all-to-all-start.1 = ((bf16[8,128,256]{2,1,0:T(8,128)(2,1)}), bf16[8,128,256]{2,1,0:T(8,128)(2,1)S(1)}, u32[]{:S(2)}, u32[]{:S(2)}) async-start(bf16[8,128,256]{2,1,0:T(8,128)(2,1)} %broadcast_in_dim.28), calls=%async_computation.1 | async-start | bytes 1048576 | tf_op jit(solution)/shard_map/all_to_all | solution.py:30
  108.2 17.7 %copy-start = (bf16[1,2048,256]{2,1,0:T(8,128)(2,1)S(1)}, bf16[1,2048,256]{2,1,0:T(8,128)(2,1)}, u32[]{:S(2)}) copy-start(bf16[1,2048,256]{2,1,0:T(8,128)(2,1)} %param.11) | copy-start | bytes 3145732
  108.2 17.7 %copy-start.1 = (bf16[1,2048,256]{2,1,0:T(8,128)(2,1)S(1)}, bf16[1,2048,256]{2,1,0:T(8,128)(2,1)}, u32[]{:S(2)}) copy-start(bf16[1,2048,256]{2,1,0:T(8,128)(2,1)} %param.12) | copy-start | bytes 3145732
  109.5 0.8 copy-start.4
  111.0 11.5 %collective-permute-start.8 = (f32[128,512]{1,0:T(8,128)}, f32[128,512]{1,0:T(8,128)S(1)}, u32[]{:S(2)}, u32[]{:S(2)}) collective-permute-start(f32[128,512]{1,0:T(8,128)} %slice_bitcast_fusion), channel_id=1, source_target_pairs={{0,256},{256,0},{1,257},{257,1},{2,258},{258,2},{3,259},{259,3},{4... | collective-permute-start | bytes 786440 | tf_op jit(solution)/shard_map/ppermute | solution.py:34
  117.4 29.4 %collective-permute-start.9 = (bf16[8,128,256]{2,1,0:T(8,128)(2,1)S(1)}, bf16[8,128,256]{2,1,0:T(8,128)(2,1)}, u32[]{:S(2)}, u32[]{:S(2)}) collective-permute-start(bf16[8,128,256]{2,1,0:T(8,128)(2,1)S(1)} %slice.39.w_ref), channel_id=1, source_target_pairs={{0,256},{256,0},{1,257},{257,1},{2,258},{258,2},{3,259},{259,3},{4... | collective-permute-start | bytes 1572872 | tf_op jit(solution)/shard_map/ppermute | solution.py:34
  140.2 22.8 %all-to-all-start.2 = ((bf16[8,144,256]{2,1,0:T(8,128)(2,1)}), bf16[8,144,256]{2,1,0:T(8,128)(2,1)S(1)}, u32[]{:S(2)}, u32[]{:S(2)}) async-start(bf16[8,144,256]{2,1,0:T(8,128)(2,1)} %attend_new.1), calls=%async_computation.2 | async-start | bytes 1179648 | tf_op jit(solution)/shard_map/all_to_all | solution.py:279
  144.9 4.3 %collective-permute-start.10 = (bf16[8,128,256]{2,1,0:T(8,128)(2,1)S(1)}, bf16[8,128,256]{2,1,0:T(8,128)(2,1)S(1)}, u32[]{:S(2)}, u32[]{:S(2)}) collective-permute-start(bf16[8,128,256]{2,1,0:T(8,128)(2,1)S(1)} %slice.39.w_ref), channel_id=1, source_target_pairs={{0,128},{128,0},{1,129},{129,1},{2,130},{130,2},{3,131},{131,3},{4... | collective-permute-start | bytes 1572872 | tf_op jit(solution)/shard_map/ppermute | solution.py:34
  146.8 4.1 %collective-permute-start.11 = (bf16[8,128,256]{2,1,0:T(8,128)(2,1)}, bf16[8,128,256]{2,1,0:T(8,128)(2,1)S(1)}, u32[]{:S(2)}, u32[]{:S(2)}) collective-permute-start(bf16[8,128,256]{2,1,0:T(8,128)(2,1)} %collective-permute-done.9.far_w_ref), channel_id=1, source_target_pairs={{0,128},{128,0},{1,129},{129,1},{2,130},{130,2},{3,131},{131,3},{4... | collective-permute-start | bytes 1572872 | tf_op jit(solution)/shard_map/ppermute | solution.py:34
Sparse Core Ops, SparseCore 0:
  10.3 48.7 all-gather.2

commit v6 on v5

--- a/solution.py
+++ b/solution.py
@@ -75,17 +75,31 @@
     other_out[...] = total[own_out.shape[0] :]
 
 
-def pair_kernel(place_ref, keep_ref, other_ref, far_ref, key_w_ref, value_w_ref, own_out, other_out):
-    rows, width = own_out.shape[1], key_w_ref.shape[2]
+def pair_kernel(place_ref, keep_ref, other_ref, far_ref, key_w_ref, value_w_ref, near_out, far_out, other_out):
+    rows, width = near_out.shape[0], key_w_ref.shape[2]
+    outs = (near_out, far_out, other_out.at[0], other_out.at[1])
     for lane, w_ref in ((0, key_w_ref), (width, value_w_ref)):
         total = None
         for at in range(w_ref.shape[0] // 2):
             x = [keep_ref[0, at], far_ref[0, at], other_ref[0, at], far_ref[1, at]]
             part = dot(jnp.concatenate(x, axis=0), both_rows(w_ref, at))
             total = part if total is None else total + part
-        for n in range(2):
-            own_out[n, :, lane : lane + width] = total[n * rows : (n + 1) * rows]
-            other_out[n, :, lane : lane + width] = total[(n + 2) * rows : (n + 3) * rows]
+        for n, out_ref in enumerate(outs):
+            out_ref[:, lane : lane + width] = total[n * rows : (n + 1) * rows]
+
+
+def copies_kernel(place_ref, own_ref, other_ref, out_ref):
+    total = (own_ref[...] + other_ref[...]).astype(jnp.bfloat16)
+    for n in range(out_ref.shape[0]):
+        out_ref[n] = total
+
+
+def pack_kernel(place_ref, query_ref, pair_ref, out_w_ref, out_ref):
+    rows = query_ref.shape[0]
+    out_ref[:rows] = query_ref[...]
+    out_ref[rows : 2 * rows] = pair_ref[:, 0]
+    out_ref[2 * rows : 3 * rows] = pair_ref[:, 1]
+    out_ref[3 * rows :] = jnp.concatenate([out_w_ref[:rows], out_w_ref[rows:]], axis=1)
 
 
 def thirds(value):
@@ -124,14 +138,18 @@
     total_ref[0] = total
 
 
-def new_kernel(place_ref, q_ref, k_ref, v_ref, peak_ref, total_ref, out_ref):
-    s = score(q_ref[...], k_ref[...])
+def new_kernel(place_ref, q_ref, *refs):
+    *pair_refs, peak_ref, total_ref, out_ref = refs
+    keys, values = [
+        (near[...] + core[0] + far[...]).astype(jnp.bfloat16) for near, core, far in (pair_refs[:3], pair_refs[3:])
+    ]
+    s = score(q_ref[...], keys)
     row = pl.program_id(1) * QUERY_ROWS + lax.broadcasted_iota(jnp.int32, s.shape, 0)
-    column = place_ref[2] * k_ref.shape[0] + lax.broadcasted_iota(jnp.int32, s.shape, 1)
+    column = place_ref[2] * keys.shape[0] + lax.broadcasted_iota(jnp.int32, s.shape, 1)
     s = jnp.where(column <= row, s, DEAD)
     cache_peak = peak_ref[0]
     peak = jnp.maximum(cache_peak, jnp.max(s, axis=1, keepdims=True))
-    fresh = mixed(s, peak, v_ref[...])
+    fresh = mixed(s, peak, values)
     kept = jnp.exp2((cache_peak - peak) * EXPONENT)
     mixture = total_ref[0, :, :HD] * kept + fresh[:, :HD]
     total = total_ref[0, :, HD:] * kept + fresh[:, HD:]
@@ -213,8 +231,8 @@
     gathered = shared(tokens[0], HEAD)
     query_w_far = swapped(w_query[None], "x_hi")
     query_w_far = doubled(query_w_far, KV)
-    out_w = jnp.concatenate([w_out[:local_rows], w_out[local_rows:]], axis=1)
-    weights = jnp.concatenate([w_query, w_keyvalue[:, 0], w_keyvalue[:, 1], out_w], axis=0)
+    packed = jax.ShapeDtypeStruct((4 * local_rows, width), jnp.bfloat16)
+    weights = call(pack_kernel, packed, w_query, w_keyvalue, w_out)
     weights = lax.all_gather(weights, KV, axis=0, tiled=False)
     out_w = weights[:, 3 * local_rows :]
     out_w_far = swapped(out_w, "x_hi")
@@ -226,14 +244,25 @@
     other = swapped(send, "core")
     partial = jax.ShapeDtypeStruct((local_rows, width), jnp.float32)
     mine, theirs = call(query_kernel, (partial, partial), keep, other, part_of_weights(0), *query_w_far)
-    queries = (mine + swapped(theirs, "core")).astype(jnp.bfloat16)
-    queries = shared(queries, KV).reshape(-1, width)
+    copies = jax.ShapeDtypeStruct((kv_count, local_rows, width), jnp.bfloat16)
+    copies = call(copies_kernel, copies, mine, swapped(theirs, "core"))
+    queries = lax.all_to_all(copies, KV, split_axis=0, concat_axis=0, tiled=True)
+    queries = queries.reshape(-1, width)
 
     far = swapped(jnp.stack([keep[1], other[1]]), "x_hi")
-    partial = jax.ShapeDtypeStruct((2, local_rows, 2 * width), jnp.float32)
-    mine, theirs = call(pair_kernel, (partial, partial), keep, other, far, part_of_weights(1), part_of_weights(2))
-    mine = mine + swapped(theirs, "core")
-    pair = (mine[0] + swapped(mine[1], "x_hi")).astype(jnp.bfloat16)
+    partial = jax.ShapeDtypeStruct((local_rows, 2 * width), jnp.float32)
+    both = jax.ShapeDtypeStruct((2, local_rows, 2 * width), jnp.float32)
+    pair_near, pair_far, theirs = call(
+        pair_kernel,
+        (partial, partial, both),
+        keep,
+        other,
+        far,
+        part_of_weights(1),
+        part_of_weights(2),
+    )
+    pair_core = swapped(theirs, "core")
+    pair_far = swapped(pair_far + pair_core[1], "x_hi")
     place = kv * cache_rows + lax.iota(jnp.int32, cache_rows)
     usable = (place >= key_start[0]) & (place < key_end[0])
     bias = jnp.broadcast_to(jnp.where(usable, 0.0, DEAD).astype(jnp.float32)[None], (8, cache_rows))
@@ -258,6 +287,11 @@
         compiler_params=VMEM,
         name="attend_cache",
     )(bias, queries, cache_keys[0], cache_values[0])
+
+    def pair_specs(first):
+        flat = pl.BlockSpec((local_rows, HD), lambda h, i: (0, h + first))
+        return flat, pl.BlockSpec((1, local_rows, HD), lambda h, i: (0, 0, h + first)), flat
+
     padded = local_rows + STAT_ROWS
     parts = pl.pallas_call(
         new_kernel,
@@ -266,15 +300,15 @@
         in_specs=[
             SCALAR,
             query_spec,
-            pl.BlockSpec((local_rows, HD), lambda h, i: (0, h)),
-            pl.BlockSpec((local_rows, HD), lambda h, i: (0, h + heads)),
+            *pair_specs(0),
+            *pair_specs(heads),
             peak_spec,
             total_spec,
         ],
         out_specs=pl.BlockSpec((QUERY_ROWS // local_rows, padded, HD), lambda h, i: (i, 0, h)),
         compiler_params=VMEM,
         name="attend_new",
-    )(own, queries, pair, pair, peaks, totals)
+    )(own, queries, *(pair_near, pair_core, pair_far) * 2, peaks, totals)
 
     arrived = lax.all_to_all(parts, KV, split_axis=0, concat_axis=0, tiled=True)
     blocks = jax.ShapeDtypeStruct((lax.axis_size(HEAD), local_rows, width), jnp.bfloat16)

time: 205 us -> 207 us (level)
  the two profiles are of different devices: /device:TPU:2 before, /device:TPU:4 now
where the time goes in v6:
time: 207 us; the launch traced here: 206 us
  blocking collectives  68.4 us (33%)
  starting transfers between devices  50.3 us (24%)
  waiting for transfers between devices  40.9 us (20%)
  Pallas kernels  24.9 us (12%)
  between operations  15 us (7%)
  local copies, waits for them, and re-layouts  5.93 us (3%)
    ppermute x12, starting transfers between devices, swapped(): return lax.ppermute(value, axis, [(0, 1), (1, 0)])  41.3 us
    all_to_all x1, blocking collectives, shared(): return lax.all_to_all(copies, axes, split_axis=0, concat_axis=0, tiled=True)  36.2 us
    all_to_all x1, blocking collectives, shards(): lax.all_to_all(columns, HEAD, split_axis=0, concat_axis=0, tiled=True)  32.2 us
    ppermute x12, waiting for transfers between devices, swapped(): return lax.ppermute(value, axis, [(0, 1), (1, 0)])  19.8 us
    all_to_all x1, waiting for transfers between devices, shards(): arrived = lax.all_to_all(parts, KV, split_axis=0, concat_axis=0, tiled=True)  13.2 us
    pallas_call x1, Pallas kernels, shards(): pl.pallas_call(cache_kernel, grid=grid, out_shape=(jax.ShapeDtypeStruct((...  10.6 us
    pallas_call x6, Pallas kernels, call(): pl.pallas_call(kernel, grid=(1,), out_shape=shapes, in_specs=[SCALAR] + [...  10.5 us
    all_to_all x1, waiting for transfers between devices, shards(): lax.all_to_all(copies, KV, split_axis=0, concat_axis=0, tiled=True)  7.86 us
  transfers between devices with their start and end apart: 15, of which 7 were waited for; matrix products, arithmetic and copies ran while one was open for 1% of the time, Pallas kernels for 10%

profile of v6, /device:TPU:4, one launch (start us, length us, event | category | flops | bytes accessed | tf_op | source)
XLA Modules:
  0.0 206.3 jit_solution(11725172470880581663)
XLA Ops:
  6.5 0.0 all-gather.3.cloned.1.call-start
  6.5 0.1 pad_add_fusion.place_ref
  6.6 0.0 copy-start.2
  6.6 0.9 copy-done.2
  7.5 0.0 copy-start.3
  7.5 0.8 copy-done.3
  8.4 0.0 copy-start.4
  8.4 0.8 copy-done.4
  9.2 1.5 shard_map.83
  10.7 0.0 all-gather.3.cloned.1.call-update
  10.8 0.0 copy-start.5
  10.8 1.0 broadcast_in_dim.23
  11.7 36.2 %all_to_all.20.x_ref = bf16[16,128,256]{2,1,0:T(8,128)(2,1)S(1)} all-to-all(bf16[16,128,256]{2,1,0:T(8,128)(2,1)S(1)} %broadcast_in_dim.23), channel_id=1, replica_groups=mesh['x_hi'=2,'core'=2,'y'=8,'x_lo'=2,'z_4'=2,'z_2'=2,'z_1'=2] {'y','x_lo'}, dimensions={0} | all-to-all | bytes 2097152 | tf_op jit(solution)/shard_map/all_to_all | solution.py:30
  47.9 0.9 shard_map.82
  48.8 1.9 collective-permute-start
  50.8 0.0 copy-done.5
  50.8 2.7 %collective-permute-start.1 = (bf16[1,128,256]{2,1,0:T(8,128)(2,1)S(1)}, bf16[1,128,256]{2,1,0:T(8,128)(2,1)S(1)}, u32[]{:S(2)}, u32[]{:S(2)}) collective-permute-start(bf16[1,128,256]{2,1,0:T(8,128)(2,1)S(1)} %bitcast.22), channel_id=1, source_target_pairs={{0,256},{256,0},{1,257},{257,1},{2,258},{258,2},{3,259},{259,3},{4... | collective-permute-start | bytes 196616 | tf_op jit(solution)/shard_map/ppermute | solution.py:34
  53.5 5.2 %collective-permute-done.1 = bf16[1,128,256]{2,1,0:T(8,128)(2,1)S(1)} collective-permute-done((bf16[1,128,256]{2,1,0:T(8,128)(2,1)S(1)}, bf16[1,128,256]{2,1,0:T(8,128)(2,1)S(1)}, u32[]{:S(2)}, u32[]{:S(2)}) %collective-permute-start.1) | collective-permute-done | bytes 65568 | tf_op jit(solution)/shard_map/ppermute | solution.py:34
  58.7 10.9 %collective-permute-start.2 = (bf16[1,128,256]{2,1,0:T(8,128)(2,1)S(1)}, bf16[1,128,256]{2,1,0:T(8,128)(2,1)S(1)}, u32[]{:S(2)}, u32[]{:S(2)}) collective-permute-start(bf16[1,128,256]{2,1,0:T(8,128)(2,1)S(1)} %collective-permute-done.1), channel_id=1, source_target_pairs={{0,4},{4,0},{1,5},{5,1},{2,6},{6,2},{3,7},{7,3},{8,12},{12,8},{9,1... | collective-permute-start | bytes 196616 | tf_op jit(solution)/shard_map/ppermute | solution.py:34
  69.6 2.8 %collective-permute-done.2 = bf16[1,128,256]{2,1,0:T(8,128)(2,1)S(1)} collective-permute-done((bf16[1,128,256]{2,1,0:T(8,128)(2,1)S(1)}, bf16[1,128,256]{2,1,0:T(8,128)(2,1)S(1)}, u32[]{:S(2)}, u32[]{:S(2)}) %collective-permute-start.2) | collective-permute-done | bytes 65568 | tf_op jit(solution)/shard_map/ppermute | solution.py:34
  72.4 4.8 %collective-permute-start.3 = (bf16[2,128,256]{2,1,0:T(8,128)(2,1)S(1)}, bf16[2,128,256]{2,1,0:T(8,128)(2,1)S(1)}, u32[]{:S(2)}, u32[]{:S(2)}) collective-permute-start(bf16[2,128,256]{2,1,0:T(8,128)(2,1)S(1)} %pad_maximum_fusion.1), channel_id=1, source_target_pairs={{0,2},{2,0},{1,3},{3,1},{4,6},{6,4},{5,7},{7,5},{8,10},{10,8},{9,1... | collective-permute-start | bytes 393224 | tf_op jit(solution)/shard_map/ppermute | solution.py:34
  77.3 0.0 collective-permute-done.other_ref
  77.3 0.1 pad_maximum_fusion
  77.4 2.7 %collective-permute-start.6 = (bf16[2,4,128,256]{3,2,1,0:T(8,128)(2,1)S(1)}, bf16[2,4,128,256]{3,2,1,0:T(8,128)(2,1)S(1)}, u32[]{:S(2)}, u32[]{:S(2)}) collective-permute-start(bf16[2,4,128,256]{3,2,1,0:T(8,128)(2,1)S(1)} %pad_maximum_fusion), channel_id=1, source_target_pairs={{0,256},{256,0},{1,257},{257,1},{2,258},{258,2},{3,259},{259,3},{4... | collective-permute-start | bytes 1572872 | tf_op jit(solution)/shard_map/ppermute | solution.py:34
  80.1 2.4 %collective-permute-done.3 = bf16[2,128,256]{2,1,0:T(8,128)(2,1)S(1)} collective-permute-done((bf16[2,128,256]{2,1,0:T(8,128)(2,1)S(1)}, bf16[2,128,256]{2,1,0:T(8,128)(2,1)S(1)}, u32[]{:S(2)}, u32[]{:S(2)}) %collective-permute-start.3) | collective-permute-done | bytes 131104 | tf_op jit(solution)/shard_map/ppermute | solution.py:34
  82.5 2.1 %collective-permute-start.4 = (bf16[4,128,256]{2,1,0:T(8,128)(2,1)S(1)}, bf16[4,128,256]{2,1,0:T(8,128)(2,1)S(1)}, u32[]{:S(2)}, u32[]{:S(2)}) collective-permute-start(bf16[4,128,256]{2,1,0:T(8,128)(2,1)S(1)} %constant_dynamic-update-slice_fusion.far_w_ref), channel_id=1, source_target_pairs={{0,1},{1,0},{2,3},{3,2},{4,5},{5,4},{6,7},{7,6},{8,9},{9,8},{10,11... | collective-permute-start | bytes 786440 | tf_op jit(solution)/shard_map/ppermute | solution.py:34
  84.6 7.6 %collective-permute-done.4.away_w_ref = bf16[4,128,256]{2,1,0:T(8,128)(2,1)S(1)} collective-permute-done((bf16[4,128,256]{2,1,0:T(8,128)(2,1)S(1)}, bf16[4,128,256]{2,1,0:T(8,128)(2,1)S(1)}, u32[]{:S(2)}, u32[]{:S(2)}) %collective-permute-start.4) | collective-permute-done | bytes 262176 | tf_op jit(solution)/shard_map/ppermute | solution.py:34
  92.2 0.0 all-gather.3.cloned.1.call-done
  92.2 1.6 shard_map.84
  93.8 1.9 collective-permute-start.5
  95.8 0.0 collective-permute-done.6.far_ref
  95.8 2.7 %shard_map.86 = (f32[128,512]{1,0:T(8,128)S(1)}, f32[128,512]{1,0:T(8,128)S(1)}, f32[2,128,512]{2,1,0:T(8,128)}) custom-call(s32[3]{0:T(128)S(1)} %pad_add_fusion.place_ref, bf16[2,4,128,256]{3,2,1,0:T(8,128)(2,1)S(1)} %get-tuple-element.14.keep_ref, bf16[2,4,128,256]{3,2,1,0:T(8,128)(2,1)S(1)} %collective-permute-done.other_ref, ...), custom_call_target="tpu_custom_call" | custom-call | tf_op jit(solution)/shard_map/pallas_call | solution.py:222
  98.5 0.0 copy-start
  98.5 2.5 %collective-permute-start.7 = (f32[2,128,512]{2,1,0:T(8,128)}, f32[2,128,512]{2,1,0:T(8,128)S(1)}, u32[]{:S(2)}, u32[]{:S(2)}) collective-permute-start(f32[2,128,512]{2,1,0:T(8,128)} %get-tuple-element.19), channel_id=1, source_target_pairs={{0,128},{128,0},{1,129},{129,1},{2,130},{130,2},{3,131},{131,3},{4... | collective-permute-start | bytes 1572872 | tf_op jit(solution)/shard_map/ppermute | solution.py:34
  101.0 0.0 collective-permute-done.5.other_ref
  101.1 1.4 shard_map.85
  102.4 5.5 %all-to-all-start.1 = ((bf16[8,128,256]{2,1,0:T(8,128)(2,1)}), bf16[8,128,256]{2,1,0:T(8,128)(2,1)S(1)}, u32[]{:S(2)}, u32[]{:S(2)}) async-start(bf16[8,128,256]{2,1,0:T(8,128)(2,1)} %shard_map.85), calls=%async_computation.1 | async-start | bytes 1048576 | tf_op jit(solution)/shard_map/all_to_all | solution.py:249
  107.9 0.0 collective-permute-done.7.refs_1_.refs_4_
  108.0 2.7 %collective-permute-start.8 = (f32[128,512]{1,0:T(8,128)S(1)}, f32[128,512]{1,0:T(8,128)S(1)}, u32[]{:S(2)}, u32[]{:S(2)}) collective-permute-start(f32[128,512]{1,0:T(8,128)S(1)} %fusion), channel_id=1, source_target_pairs={{0,256},{256,0},{1,257},{257,1},{2,258},{258,2},{3,259},{259,3},{4... | collective-permute-start | bytes 786440 | tf_op jit(solution)/shard_map/ppermute | solution.py:34
  112.0 1.1 slice.18.w_ref
  113.1 4.6 %collective-permute-start.9 = (bf16[8,128,256]{2,1,0:T(8,128)(2,1)S(1)}, bf16[8,128,256]{2,1,0:T(8,128)(2,1)}, u32[]{:S(2)}, u32[]{:S(2)}) collective-permute-start(bf16[8,128,256]{2,1,0:T(8,128)(2,1)S(1)} %slice.18.w_ref), channel_id=1, source_target_pairs={{0,256},{256,0},{1,257},{257,1},{2,258},{258,2},{3,259},{259,3},{4... | collective-permute-start | bytes 1572872 | tf_op jit(solution)/shard_map/ppermute | solution.py:34
  117.7 7.9 %all-to-all-done.1 = bf16[8,128,256]{2,1,0:T(8,128)(2,1)S(1)} async-done(((bf16[8,128,256]{2,1,0:T(8,128)(2,1)}), bf16[8,128,256]{2,1,0:T(8,128)(2,1)S(1)}, u32[]{:S(2)}, u32[]{:S(2)}) %all-to-all-start.1) | async-done | bytes 524320 | tf_op jit(solution)/shard_map/all_to_all | solution.py:249
  125.6 0.0 copy-done
  125.6 0.0 copy-start.1
  125.6 1.2 copy-done.1
  126.8 10.6 %attend_cache.1 = (f32[2,1024,128]{2,1,0:T(8,128)S(1)}, f32[2,1024,256]{2,1,0:T(8,128)S(1)}) custom-call(f32[8,2048]{1,0:T(8,128)S(1)} %broadcast_in_dim.27.bias_ref, bf16[1024,256]{1,0:T(8,128)(2,1)S(1)} %bitcast.18, bf16[2048,256]{1,0:T(8,128)(2,1)S(1)} %bitcast.20, bf16[2048,256]{1,0:T(8,128)(2,1)S(1)} %bitcast.21), custom_call_target="tpu_custom_call" | custom-call | tf_op jit(solution)/shard_map/attend_cache/pallas_call | solution.py:277
  137.5 0.0 collective-permute-done.8.refs_2_.refs_5_
  137.5 3.8 %attend_new.1 = bf16[8,144,256]{2,1,0:T(8,128)(2,1)} custom-call(s32[3]{0:T(128)S(1)} %pad_add_fusion.place_ref, bf16[1024,256]{1,0:T(8,128)(2,1)S(1)} %bitcast.19, f32[128,512]{1,0:T(8,128)S(1)} %get-tuple-element.18.refs_0_.refs_3_, f32[2,128,512]{2,1,0:T(8,128)S(1)} %collective-permute-done.7.refs_1_.refs_4_, ...), custom_call_target="tpu_custom_call" | custom-call | tf_op jit(solution)/shard_map/attend_new/pallas_call | solution.py:296
  141.3 3.5 %all-to-all-start.2 = ((bf16[8,144,256]{2,1,0:T(8,128)(2,1)}), bf16[8,144,256]{2,1,0:T(8,128)(2,1)S(1)}, u32[]{:S(2)}, u32[]{:S(2)}) async-start(bf16[8,144,256]{2,1,0:T(8,128)(2,1)} %attend_new.1), calls=%async_computation.2 | async-start | bytes 1179648 | tf_op jit(solution)/shard_map/all_to_all | solution.py:313
  144.8 1.9 collective-permute-start.10
  146.7 0.0 collective-permute-done.9.far_w_ref
  146.7 2.4 %collective-permute-start.11 = (bf16[8,128,256]{2,1,0:T(8,128)(2,1)}, bf16[8,128,256]{2,1,0:T(8,128)(2,1)S(1)}, u32[]{:S(2)}, u32[]{:S(2)}) collective-permute-start(bf16[8,128,256]{2,1,0:T(8,128)(2,1)} %collective-permute-done.9.far_w_ref), channel_id=1, source_target_pairs={{0,128},{128,0},{1,129},{129,1},{2,130},{130,2},{3,131},{131,3},{4... | collective-permute-start | bytes 1572872 | tf_op jit(solution)/shard_map/ppermute | solution.py:34
  149.2 0.0 collective-permute-done.10.swap_w_ref
  149.2 1.7 collective-permute-done.11.swap_far_w_ref
  150.9 13.2 %all-to-all-done.2.parts_ref = bf16[8,144,256]{2,1,0:T(8,128)(2,1)S(1)} async-done(((bf16[8,144,256]{2,1,0:T(8,128)(2,1)}), bf16[8,144,256]{2,1,0:T(8,128)(2,1)S(1)}, u32[]{:S(2)}, u32[]{:S(2)}) %all-to-all-start.2) | async-done | bytes 589856 | tf_op jit(solution)/shard_map/all_to_all | solution.py:313
  164.1 2.4 %shard_map.87 = bf16[16,128,256]{2,1,0:T(8,128)(2,1)S(1)} custom-call(s32[3]{0:T(128)S(1)} %pad_add_fusion.place_ref, bf16[8,144,256]{2,1,0:T(8,128)(2,1)S(1)} %all-to-all-done.2.parts_ref, bf16[8,128,256]{2,1,0:T(8,128)(2,1)S(1)} %slice.18.w_ref, bf16[8,128,256]{2,1,0:T(8,128)(2,1)} %collective-permute-done.9.far_w_ref, ...), custom_call_target="tpu_custom_call" | custom-call | tf_op jit(solution)/shard_map/pallas_call | solution.py:222
  166.5 32.2 %all_to_all.21 = bf16[16,128,256]{2,1,0:T(8,128)(2,1)S(1)} all-to-all(bf16[16,128,256]{2,1,0:T(8,128)(2,1)S(1)} %shard_map.87), channel_id=1, replica_groups=mesh['x_hi'=2,'core'=2,'y'=8,'x_lo'=2,'z_4'=2,'z_2'=2,'z_1'=2] {'y','x_lo'}, dimensions={0} | all-to-all | bytes 2097152 | tf_op jit(solution)/shard_map/all_to_all | solution.py:316
  198.7 0.8 reduce_sum.12
  (9 shorter events, 0.1 us)
Async XLA Ops:
  6.5 85.7 %all-gather.3.cloned.1.call-start = ((), (), s32[]{:S(2)}) async-start(), calls=%async_computation.4 | async-start | bytes 2359296 | tf_op jit(solution)/shard_map/all_gather | solution.py:236
  6.6 0.9 copy-start.2
  7.5 0.8 copy-start.3
  8.4 0.8 copy-start.4
  10.8 40.0 %copy-start.5 = (bf16[128,256]{1,0:T(8,128)(2,1)S(1)}, bf16[128,256]{1,0:T(8,128)(2,1)}, u32[]{:S(2)}) copy-start(bf16[128,256]{1,0:T(8,128)(2,1)} %query_ref.1) | copy-start | bytes 196612
  48.8 28.5 %collective-permute-start = (bf16[2,4,128,256]{3,2,1,0:T(8,128)(2,1)S(1)}, bf16[2,4,128,256]{3,2,1,0:T(8,128)(2,1)S(1)}, u32[]{:S(2)}, u32[]{:S(2)}) collective-permute-start(bf16[2,4,128,256]{3,2,1,0:T(8,128)(2,1)S(1)} %get-tuple-element.15), channel_id=1, source_target_pairs={{0,128},{128,0},{1,129},{129,1},{2,130},{130,2},{3,131},{131,3},{4... | collective-permute-start | bytes 1572872 | tf_op jit(solution)/shard_map/ppermute | solution.py:34
  50.8 7.9 %collective-permute-start.1 = (bf16[1,128,256]{2,1,0:T(8,128)(2,1)S(1)}, bf16[1,128,256]{2,1,0:T(8,128)(2,1)S(1)}, u32[]{:S(2)}, u32[]{:S(2)}) collective-permute-start(bf16[1,128,256]{2,1,0:T(8,128)(2,1)S(1)} %bitcast.22), channel_id=1, source_target_pairs={{0,256},{256,0},{1,257},{257,1},{2,258},{258,2},{3,259},{259,3},{4... | collective-permute-start | bytes 196616 | tf_op jit(solution)/shard_map/ppermute | solution.py:34
  58.7 13.8 %collective-permute-start.2 = (bf16[1,128,256]{2,1,0:T(8,128)(2,1)S(1)}, bf16[1,128,256]{2,1,0:T(8,128)(2,1)S(1)}, u32[]{:S(2)}, u32[]{:S(2)}) collective-permute-start(bf16[1,128,256]{2,1,0:T(8,128)(2,1)S(1)} %collective-permute-done.1), channel_id=1, source_target_pairs={{0,4},{4,0},{1,5},{5,1},{2,6},{6,2},{3,7},{7,3},{8,12},{12,8},{9,1... | collective-permute-start | bytes 196616 | tf_op jit(solution)/shard_map/ppermute | solution.py:34
  72.4 10.1 %collective-permute-start.3 = (bf16[2,128,256]{2,1,0:T(8,128)(2,1)S(1)}, bf16[2,128,256]{2,1,0:T(8,128)(2,1)S(1)}, u32[]{:S(2)}, u32[]{:S(2)}) collective-permute-start(bf16[2,128,256]{2,1,0:T(8,128)(2,1)S(1)} %pad_maximum_fusion.1), channel_id=1, source_target_pairs={{0,2},{2,0},{1,3},{3,1},{4,6},{6,4},{5,7},{7,5},{8,10},{10,8},{9,1... | collective-permute-start | bytes 393224 | tf_op jit(solution)/shard_map/ppermute | solution.py:34
  77.4 18.4 %collective-permute-start.6 = (bf16[2,4,128,256]{3,2,1,0:T(8,128)(2,1)S(1)}, bf16[2,4,128,256]{3,2,1,0:T(8,128)(2,1)S(1)}, u32[]{:S(2)}, u32[]{:S(2)}) collective-permute-start(bf16[2,4,128,256]{3,2,1,0:T(8,128)(2,1)S(1)} %pad_maximum_fusion), channel_id=1, source_target_pairs={{0,256},{256,0},{1,257},{257,1},{2,258},{258,2},{3,259},{259,3},{4... | collective-permute-start | bytes 1572872 | tf_op jit(solution)/shard_map/ppermute | solution.py:34
  82.5 9.7 %collective-permute-start.4 = (bf16[4,128,256]{2,1,0:T(8,128)(2,1)S(1)}, bf16[4,128,256]{2,1,0:T(8,128)(2,1)S(1)}, u32[]{:S(2)}, u32[]{:S(2)}) collective-permute-start(bf16[4,128,256]{2,1,0:T(8,128)(2,1)S(1)} %constant_dynamic-update-slice_fusion.far_w_ref), channel_id=1, source_target_pairs={{0,1},{1,0},{2,3},{3,2},{4,5},{5,4},{6,7},{7,6},{8,9},{9,8},{10,11... | collective-permute-start | bytes 786440 | tf_op jit(solution)/shard_map/ppermute | solution.py:34
  93.8 7.2 %collective-permute-start.5 = (f32[128,256]{1,0:T(8,128)S(1)}, f32[128,256]{1,0:T(8,128)S(1)}, u32[]{:S(2)}, u32[]{:S(2)}) collective-permute-start(f32[128,256]{1,0:T(8,128)S(1)} %get-tuple-element.17), channel_id=1, source_target_pairs={{0,128},{128,0},{1,129},{129,1},{2,130},{130,2},{3,131},{131,3},{4... | collective-permute-start | bytes 393224 | tf_op jit(solution)/shard_map/ppermute | solution.py:34
  98.5 27.1 %copy-start = (bf16[1,2048,256]{2,1,0:T(8,128)(2,1)S(1)}, bf16[1,2048,256]{2,1,0:T(8,128)(2,1)}, u32[]{:S(2)}) copy-start(bf16[1,2048,256]{2,1,0:T(8,128)(2,1)} %param.11) | copy-start | bytes 3145732
  98.5 9.4 %collective-permute-start.7 = (f32[2,128,512]{2,1,0:T(8,128)}, f32[2,128,512]{2,1,0:T(8,128)S(1)}, u32[]{:S(2)}, u32[]{:S(2)}) collective-permute-start(f32[2,128,512]{2,1,0:T(8,128)} %get-tuple-element.19), channel_id=1, source_target_pairs={{0,128},{128,0},{1,129},{129,1},{2,130},{130,2},{3,131},{131,3},{4... | collective-permute-start | bytes 1572872 | tf_op jit(solution)/shard_map/ppermute | solution.py:34
  102.4 23.1 %all-to-all-start.1 = ((bf16[8,128,256]{2,1,0:T(8,128)(2,1)}), bf16[8,128,256]{2,1,0:T(8,128)(2,1)S(1)}, u32[]{:S(2)}, u32[]{:S(2)}) async-start(bf16[8,128,256]{2,1,0:T(8,128)(2,1)} %shard_map.85), calls=%async_computation.1 | async-start | bytes 1048576 | tf_op jit(solution)/shard_map/all_to_all | solution.py:249
  108.0 29.5 %collective-permute-start.8 = (f32[128,512]{1,0:T(8,128)S(1)}, f32[128,512]{1,0:T(8,128)S(1)}, u32[]{:S(2)}, u32[]{:S(2)}) collective-permute-start(f32[128,512]{1,0:T(8,128)S(1)} %fusion), channel_id=1, source_target_pairs={{0,256},{256,0},{1,257},{257,1},{2,258},{258,2},{3,259},{259,3},{4... | collective-permute-start | bytes 786440 | tf_op jit(solution)/shard_map/ppermute | solution.py:34
  113.1 33.7 %collective-permute-start.9 = (bf16[8,128,256]{2,1,0:T(8,128)(2,1)S(1)}, bf16[8,128,256]{2,1,0:T(8,128)(2,1)}, u32[]{:S(2)}, u32[]{:S(2)}) collective-permute-start(bf16[8,128,256]{2,1,0:T(8,128)(2,1)S(1)} %slice.18.w_ref), channel_id=1, source_target_pairs={{0,256},{256,0},{1,257},{257,1},{2,258},{258,2},{3,259},{259,3},{4... | collective-permute-start | bytes 1572872 | tf_op jit(solution)/shard_map/ppermute | solution.py:34
  125.6 1.2 copy-start.1
  141.3 22.9 %all-to-all-start.2 = ((bf16[8,144,256]{2,1,0:T(8,128)(2,1)}), bf16[8,144,256]{2,1,0:T(8,128)(2,1)S(1)}, u32[]{:S(2)}, u32[]{:S(2)}) async-start(bf16[8,144,256]{2,1,0:T(8,128)(2,1)} %attend_new.1), calls=%async_computation.2 | async-start | bytes 1179648 | tf_op jit(solution)/shard_map/all_to_all | solution.py:313
  144.8 4.4 %collective-permute-start.10 = (bf16[8,128,256]{2,1,0:T(8,128)(2,1)S(1)}, bf16[8,128,256]{2,1,0:T(8,128)(2,1)S(1)}, u32[]{:S(2)}, u32[]{:S(2)}) collective-permute-start(bf16[8,128,256]{2,1,0:T(8,128)(2,1)S(1)} %slice.18.w_ref), channel_id=1, source_target_pairs={{0,128},{128,0},{1,129},{129,1},{2,130},{130,2},{3,131},{131,3},{4... | collective-permute-start | bytes 1572872 | tf_op jit(solution)/shard_map/ppermute | solution.py:34
  146.7 4.1 %collective-permute-start.11 = (bf16[8,128,256]{2,1,0:T(8,128)(2,1)}, bf16[8,128,256]{2,1,0:T(8,128)(2,1)S(1)}, u32[]{:S(2)}, u32[]{:S(2)}) collective-permute-start(bf16[8,128,256]{2,1,0:T(8,128)(2,1)} %collective-permute-done.9.far_w_ref), channel_id=1, source_target_pairs={{0,128},{128,0},{1,129},{129,1},{2,130},{130,2},{3,131},{131,3},{4... | collective-permute-start | bytes 1572872 | tf_op jit(solution)/shard_map/ppermute | solution.py:34
Sparse Core Ops, SparseCore 0:
  10.9 48.7 all-gather.2

commit v7 on v6

--- a/solution.py
+++ b/solution.py
@@ -88,18 +88,26 @@
             out_ref[:, lane : lane + width] = total[n * rows : (n + 1) * rows]
 
 
-def copies_kernel(place_ref, own_ref, other_ref, out_ref):
-    total = (own_ref[...] + other_ref[...]).astype(jnp.bfloat16)
-    for n in range(out_ref.shape[0]):
-        out_ref[n] = total
-
-
-def pack_kernel(place_ref, query_ref, pair_ref, out_w_ref, out_ref):
+def pack_kernel(query_ref, pair_ref, out_w_ref, out_ref, pair_buf, out_w_buf, split_buf, fold_buf, sems):
     rows = query_ref.shape[0]
-    out_ref[:rows] = query_ref[...]
-    out_ref[rows : 2 * rows] = pair_ref[:, 0]
-    out_ref[2 * rows : 3 * rows] = pair_ref[:, 1]
-    out_ref[3 * rows :] = jnp.concatenate([out_w_ref[:rows], out_w_ref[rows:]], axis=1)
+    query = pltpu.make_async_copy(query_ref, out_ref.at[:rows], sems.at[0])
+    pair = pltpu.make_async_copy(pair_ref, pair_buf, sems.at[1])
+    out_w = pltpu.make_async_copy(out_w_ref, out_w_buf, sems.at[2])
+    split = pltpu.make_async_copy(split_buf, out_ref.at[rows : 3 * rows], sems.at[3])
+    fold = pltpu.make_async_copy(fold_buf, out_ref.at[3 * rows :], sems.at[4])
+    pair.start()
+    out_w.start()
+    query.start()
+    pair.wait()
+    split_buf[:rows] = pair_buf[:, 0]
+    split_buf[rows:] = pair_buf[:, 1]
+    split.start()
+    out_w.wait()
+    fold_buf[...] = jnp.concatenate([out_w_buf[:rows], out_w_buf[rows:]], axis=1)
+    fold.start()
+    query.wait()
+    split.wait()
+    fold.wait()
 
 
 def thirds(value):
@@ -199,6 +207,10 @@
             out_ref[to, :, lane] = dot(attended, w).astype(jnp.bfloat16)
 
 
+def in_hbm(value):
+    return pltpu.with_memory_space_constraint(value, pltpu.HBM)
+
+
 def doubled(value, axes):
     for axis in axes[:-1]:
         value = jnp.concatenate([value, swapped(value, axis)], axis=0)
@@ -214,8 +226,7 @@
 
     def part_of_weights(index):
         block = (kv_count, local_rows, width)
-        operand = pltpu.with_memory_space_constraint(weights, pltpu.HBM)
-        return pl.BlockSpec(block, lambda i: (0, index, 0)), operand
+        return pl.BlockSpec(block, lambda i: (0, index, 0)), in_hbm(weights)
 
     def call(kernel, shapes, *operands):
         pairs = [o if isinstance(o, tuple) else (WHOLE, o) for o in operands]
@@ -231,8 +242,21 @@
     gathered = shared(tokens[0], HEAD)
     query_w_far = swapped(w_query[None], "x_hi")
     query_w_far = doubled(query_w_far, KV)
-    packed = jax.ShapeDtypeStruct((4 * local_rows, width), jnp.bfloat16)
-    weights = call(pack_kernel, packed, w_query, w_keyvalue, w_out)
+    sources = [in_hbm(w) for w in (w_query, w_keyvalue, w_out)]
+    weights = pl.pallas_call(
+        pack_kernel,
+        out_shape=jax.ShapeDtypeStruct((4 * local_rows, width), jnp.bfloat16),
+        in_specs=[pl.BlockSpec(memory_space=pl.ANY)] * 3,
+        out_specs=pl.BlockSpec(memory_space=pl.ANY),
+        scratch_shapes=[
+            pltpu.VMEM(w_keyvalue.shape, jnp.bfloat16),
+            pltpu.VMEM(w_out.shape, jnp.bfloat16),
+            pltpu.VMEM((2 * local_rows, width), jnp.bfloat16),
+            pltpu.VMEM((local_rows, width), jnp.bfloat16),
+            pltpu.SemaphoreType.DMA((5,)),
+        ],
+        name="pack",
+    )(*sources)
     weights = lax.all_gather(weights, KV, axis=0, tiled=False)
     out_w = weights[:, 3 * local_rows :]
     out_w_far = swapped(out_w, "x_hi")
@@ -244,10 +268,8 @@
     other = swapped(send, "core")
     partial = jax.ShapeDtypeStruct((local_rows, width), jnp.float32)
     mine, theirs = call(query_kernel, (partial, partial), keep, other, part_of_weights(0), *query_w_far)
-    copies = jax.ShapeDtypeStruct((kv_count, local_rows, width), jnp.bfloat16)
-    copies = call(copies_kernel, copies, mine, swapped(theirs, "core"))
-    queries = lax.all_to_all(copies, KV, split_axis=0, concat_axis=0, tiled=True)
-    queries = queries.reshape(-1, width)
+    queries = (mine + swapped(theirs, "core")).astype(jnp.bfloat16)
+    queries = shared(queries, KV).reshape(-1, width)
 
     far = swapped(jnp.stack([keep[1], other[1]]), "x_hi")
     partial = jax.ShapeDtypeStruct((local_rows, 2 * width), jnp.float32)
@@ -286,7 +308,7 @@
         scratch_shapes=[pltpu.VMEM((QUERY_ROWS, cache_rows), jnp.float32)],
         compiler_params=VMEM,
         name="attend_cache",
-    )(bias, queries, cache_keys[0], cache_values[0])
+    )(bias, queries, in_hbm(cache_keys[0]), in_hbm(cache_values[0]))
 
     def pair_specs(first):
         flat = pl.BlockSpec((local_rows, HD), lambda h, i: (0, h + first))

time: 207 us -> 205 us (level)
  blocking collectives: 68.4 us -> 32.2 us
  waiting for transfers between devices: 40.9 us -> 69.7 us
  starting transfers between devices: 50.3 us -> 57.8 us
    all_to_all x1 -> x0, blocking collectives: 36.2 us -> none  [shared(): return lax.all_to_all(copies, axes, split_axis=0, concat_axis=0, tiled=True)]
    all_to_all x1 -> x2, waiting for transfers between devices: 7.86 us -> 36.5 us  [shared(): return lax.all_to_all(copies, axes, split_axis=0, concat_axis=0, tiled=True)]
    all_to_all x1 -> x2, starting transfers between devices: 5.47 us -> 13.3 us  [shared(): return lax.all_to_all(copies, axes, split_axis=0, concat_axis=0, tiled=True)]
    pallas_call x6 -> x4, Pallas kernels: 10.5 us -> 6.29 us  [call(): pl.pallas_call(kernel, grid=(1,), out_shape=shapes, in_specs=[SCALAR] + [...]
    unnamed x14 -> x4, local copies, waits for them, and re-layouts: 3.83 us -> 0.02 us
    pallas_call x0 -> x1, Pallas kernels: none -> 3.13 us  [shards(): pl.pallas_call(pack_kernel, out_shape=jax.ShapeDtypeStruct((4 * local_row...]
  transfers between devices with their start and end apart: 15 -> 16, of which waited for: 7 -> 8; matrix products, arithmetic and copies ran while one was open for 1% -> 2% of each run, Pallas kernels for 10% -> 10%
where the time goes in v7:
time: 205 us; the launch traced here: 204 us
  waiting for transfers between devices  69.7 us (34%)
  starting transfers between devices  57.8 us (28%)
  blocking collectives  32.2 us (16%)
  Pallas kernels  24.7 us (12%)
  between operations  15 us (7%)
  local copies, waits for them, and re-layouts  3.93 us (2%)
    ppermute x12, starting transfers between devices, swapped(): return lax.ppermute(value, axis, [(0, 1), (1, 0)])  40.9 us
    all_to_all x2, waiting for transfers between devices, shared(): return lax.all_to_all(copies, axes, split_axis=0, concat_axis=0, tiled=True)  36.5 us
    all_to_all x1, blocking collectives, shards(): lax.all_to_all(columns, HEAD, split_axis=0, concat_axis=0, tiled=True)  32.2 us
    ppermute x12, waiting for transfers between devices, swapped(): return lax.ppermute(value, axis, [(0, 1), (1, 0)])  19.7 us
    all_to_all x1, waiting for transfers between devices, shards(): arrived = lax.all_to_all(parts, KV, split_axis=0, concat_axis=0, tiled=True)  13.4 us
    all_to_all x2, starting transfers between devices, shared(): return lax.all_to_all(copies, axes, split_axis=0, concat_axis=0, tiled=True)  13.3 us
    pallas_call x1, Pallas kernels, shards(): pl.pallas_call(cache_kernel, grid=grid, out_shape=(jax.ShapeDtypeStruct((...  11.5 us
    pallas_call x4, Pallas kernels, call(): pl.pallas_call(kernel, grid=(1,), out_shape=shapes, in_specs=[SCALAR] + [...  6.29 us
  transfers between devices with their start and end apart: 16, of which 8 were waited for; matrix products, arithmetic and copies ran while one was open for 2% of the time, Pallas kernels for 10%

profile of v7, /device:TPU:4, one launch (start us, length us, event | category | flops | bytes accessed | tf_op | source)
XLA Modules:
  0.0 204.4 jit_solution(7780640776986458818)
XLA Ops:
  6.5 0.0 all-gather.3.cloned.1.call-start
  6.5 3.1 %pack.1 = bf16[512,256]{1,0:T(8,128)(2,1)} custom-call(bf16[128,256]{1,0:T(8,128)(2,1)} %query_ref.1, bf16[128,2,256]{2,1,0:T(2,128)(2,1)} %pair_ref.1, bf16[256,128]{1,0:T(8,128)(2,1)} %out_w_ref.1), custom_call_target="tpu_custom_call" | custom-call | tf_op jit(solution)/shard_map/pack/pallas_call | solution.py:246
  9.7 0.0 all-gather.3.cloned.1.call-update
  9.7 0.0 copy-start
  9.7 2.0 broadcast_in_dim.26
  11.7 7.8 %all-to-all-start = ((bf16[16,128,256]{2,1,0:T(8,128)(2,1)}), bf16[16,128,256]{2,1,0:T(8,128)(2,1)S(1)}, u32[]{:S(2)}, u32[]{:S(2)}) async-start(bf16[16,128,256]{2,1,0:T(8,128)(2,1)} %broadcast_in_dim.26), calls=%async_computation | async-start | bytes 2097152 | tf_op jit(solution)/shard_map/all_to_all | solution.py:30
  19.5 0.1 pad_add_fusion.place_ref
  19.6 28.6 %all-to-all-done.x_ref = bf16[16,128,256]{2,1,0:T(8,128)(2,1)S(1)} async-done(((bf16[16,128,256]{2,1,0:T(8,128)(2,1)}), bf16[16,128,256]{2,1,0:T(8,128)(2,1)S(1)}, u32[]{:S(2)}, u32[]{:S(2)}) %all-to-all-start) | async-done | bytes 1048608 | tf_op jit(solution)/shard_map/all_to_all | solution.py:30
  48.2 0.9 shard_map.82
  49.2 1.9 collective-permute-start
  51.1 0.0 copy-done
  51.1 2.5 %collective-permute-start.1 = (bf16[1,128,256]{2,1,0:T(8,128)(2,1)S(1)}, bf16[1,128,256]{2,1,0:T(8,128)(2,1)S(1)}, u32[]{:S(2)}, u32[]{:S(2)}) collective-permute-start(bf16[1,128,256]{2,1,0:T(8,128)(2,1)S(1)} %bitcast.27), channel_id=1, source_target_pairs={{0,256},{256,0},{1,257},{257,1},{2,258},{258,2},{3,259},{259,3},{4... | collective-permute-start | bytes 196616 | tf_op jit(solution)/shard_map/ppermute | solution.py:34
  53.6 5.4 %collective-permute-done.1 = bf16[1,128,256]{2,1,0:T(8,128)(2,1)S(1)} collective-permute-done((bf16[1,128,256]{2,1,0:T(8,128)(2,1)S(1)}, bf16[1,128,256]{2,1,0:T(8,128)(2,1)S(1)}, u32[]{:S(2)}, u32[]{:S(2)}) %collective-permute-start.1) | collective-permute-done | bytes 65568 | tf_op jit(solution)/shard_map/ppermute | solution.py:34
  59.0 10.9 %collective-permute-start.2 = (bf16[1,128,256]{2,1,0:T(8,128)(2,1)S(1)}, bf16[1,128,256]{2,1,0:T(8,128)(2,1)S(1)}, u32[]{:S(2)}, u32[]{:S(2)}) collective-permute-start(bf16[1,128,256]{2,1,0:T(8,128)(2,1)S(1)} %collective-permute-done.1), channel_id=1, source_target_pairs={{0,4},{4,0},{1,5},{5,1},{2,6},{6,2},{3,7},{7,3},{8,12},{12,8},{9,1... | collective-permute-start | bytes 196616 | tf_op jit(solution)/shard_map/ppermute | solution.py:34
  69.9 2.8 %collective-permute-done.2 = bf16[1,128,256]{2,1,0:T(8,128)(2,1)S(1)} collective-permute-done((bf16[1,128,256]{2,1,0:T(8,128)(2,1)S(1)}, bf16[1,128,256]{2,1,0:T(8,128)(2,1)S(1)}, u32[]{:S(2)}, u32[]{:S(2)}) %collective-permute-start.2) | collective-permute-done | bytes 65568 | tf_op jit(solution)/shard_map/ppermute | solution.py:34
  72.8 4.8 %collective-permute-start.3 = (bf16[2,128,256]{2,1,0:T(8,128)(2,1)S(1)}, bf16[2,128,256]{2,1,0:T(8,128)(2,1)S(1)}, u32[]{:S(2)}, u32[]{:S(2)}) collective-permute-start(bf16[2,128,256]{2,1,0:T(8,128)(2,1)S(1)} %pad_maximum_fusion.1), channel_id=1, source_target_pairs={{0,2},{2,0},{1,3},{3,1},{4,6},{6,4},{5,7},{7,5},{8,10},{10,8},{9,1... | collective-permute-start | bytes 393224 | tf_op jit(solution)/shard_map/ppermute | solution.py:34
  77.6 0.0 collective-permute-done.other_ref
  77.6 0.1 pad_maximum_fusion
  77.7 2.7 %collective-permute-start.6 = (bf16[2,4,128,256]{3,2,1,0:T(8,128)(2,1)S(1)}, bf16[2,4,128,256]{3,2,1,0:T(8,128)(2,1)S(1)}, u32[]{:S(2)}, u32[]{:S(2)}) collective-permute-start(bf16[2,4,128,256]{3,2,1,0:T(8,128)(2,1)S(1)} %pad_maximum_fusion), channel_id=1, source_target_pairs={{0,256},{256,0},{1,257},{257,1},{2,258},{258,2},{3,259},{259,3},{4... | collective-permute-start | bytes 1572872 | tf_op jit(solution)/shard_map/ppermute | solution.py:34
  80.4 2.4 %collective-permute-done.3 = bf16[2,128,256]{2,1,0:T(8,128)(2,1)S(1)} collective-permute-done((bf16[2,128,256]{2,1,0:T(8,128)(2,1)S(1)}, bf16[2,128,256]{2,1,0:T(8,128)(2,1)S(1)}, u32[]{:S(2)}, u32[]{:S(2)}) %collective-permute-start.3) | collective-permute-done | bytes 131104 | tf_op jit(solution)/shard_map/ppermute | solution.py:34
  82.8 2.1 %collective-permute-start.4 = (bf16[4,128,256]{2,1,0:T(8,128)(2,1)S(1)}, bf16[4,128,256]{2,1,0:T(8,128)(2,1)S(1)}, u32[]{:S(2)}, u32[]{:S(2)}) collective-permute-start(bf16[4,128,256]{2,1,0:T(8,128)(2,1)S(1)} %constant_dynamic-update-slice_fusion.far_w_ref), channel_id=1, source_target_pairs={{0,1},{1,0},{2,3},{3,2},{4,5},{5,4},{6,7},{7,6},{8,9},{9,8},{10,11... | collective-permute-start | bytes 786440 | tf_op jit(solution)/shard_map/ppermute | solution.py:34
  84.9 7.6 %collective-permute-done.4.away_w_ref = bf16[4,128,256]{2,1,0:T(8,128)(2,1)S(1)} collective-permute-done((bf16[4,128,256]{2,1,0:T(8,128)(2,1)S(1)}, bf16[4,128,256]{2,1,0:T(8,128)(2,1)S(1)}, u32[]{:S(2)}, u32[]{:S(2)}) %collective-permute-start.4) | collective-permute-done | bytes 262176 | tf_op jit(solution)/shard_map/ppermute | solution.py:34
  92.6 0.0 all-gather.3.cloned.1.call-done
  92.6 1.6 shard_map.83
  94.2 1.9 collective-permute-start.5
  96.1 0.0 collective-permute-done.6.far_ref
  96.1 1.9 shard_map.84
  98.0 2.4 %collective-permute-start.7 = (f32[2,128,512]{2,1,0:T(8,128)S(1)}, f32[2,128,512]{2,1,0:T(8,128)S(1)}, u32[]{:S(2)}, u32[]{:S(2)}) collective-permute-start(f32[2,128,512]{2,1,0:T(8,128)S(1)} %get-tuple-element.19), channel_id=1, source_target_pairs={{0,128},{128,0},{1,129},{129,1},{2,130},{130,2},{3,131},{131,3},{4... | collective-permute-start | bytes 1572872 | tf_op jit(solution)/shard_map/ppermute | solution.py:34
  100.5 0.0 collective-permute-done.5
  100.5 0.8 broadcast_in_dim.28
  101.3 5.5 %all-to-all-start.1 = ((bf16[8,128,256]{2,1,0:T(8,128)(2,1)}), bf16[8,128,256]{2,1,0:T(8,128)(2,1)S(1)}, u32[]{:S(2)}, u32[]{:S(2)}) async-start(bf16[8,128,256]{2,1,0:T(8,128)(2,1)} %broadcast_in_dim.28), calls=%async_computation.1 | async-start | bytes 1048576 | tf_op jit(solution)/shard_map/all_to_all | solution.py:30
  106.8 0.0 collective-permute-done.7.refs_1_.refs_4_
  106.8 2.7 %collective-permute-start.8 = (f32[128,512]{1,0:T(8,128)S(1)}, f32[128,512]{1,0:T(8,128)S(1)}, u32[]{:S(2)}, u32[]{:S(2)}) collective-permute-start(f32[128,512]{1,0:T(8,128)S(1)} %fusion), channel_id=1, source_target_pairs={{0,256},{256,0},{1,257},{257,1},{2,258},{258,2},{3,259},{259,3},{4... | collective-permute-start | bytes 786440 | tf_op jit(solution)/shard_map/ppermute | solution.py:34
  110.8 1.1 slice.18.w_ref
  111.9 4.6 %collective-permute-start.9 = (bf16[8,128,256]{2,1,0:T(8,128)(2,1)S(1)}, bf16[8,128,256]{2,1,0:T(8,128)(2,1)S(1)}, u32[]{:S(2)}, u32[]{:S(2)}) collective-permute-start(bf16[8,128,256]{2,1,0:T(8,128)(2,1)S(1)} %slice.18.w_ref), channel_id=1, source_target_pairs={{0,256},{256,0},{1,257},{257,1},{2,258},{258,2},{3,259},{259,3},{4... | collective-permute-start | bytes 1572872 | tf_op jit(solution)/shard_map/ppermute | solution.py:34
  116.6 7.9 %all-to-all-done.1 = bf16[8,128,256]{2,1,0:T(8,128)(2,1)S(1)} async-done(((bf16[8,128,256]{2,1,0:T(8,128)(2,1)}), bf16[8,128,256]{2,1,0:T(8,128)(2,1)S(1)}, u32[]{:S(2)}, u32[]{:S(2)}) %all-to-all-start.1) | async-done | bytes 524320 | tf_op jit(solution)/shard_map/all_to_all | solution.py:30
  124.5 11.5 %attend_cache.1 = (f32[2,1024,128]{2,1,0:T(8,128)S(1)}, f32[2,1024,256]{2,1,0:T(8,128)S(1)}) custom-call(f32[8,2048]{1,0:T(8,128)S(1)} %broadcast_in_dim.31.bias_ref, bf16[1024,256]{1,0:T(8,128)(2,1)S(1)} %bitcast.18, bf16[2048,256]{1,0:T(8,128)(2,1)} %bitcast.24, bf16[2048,256]{1,0:T(8,128)(2,1)} %bitcast.25), custom_call_target="tpu_custom_call" | custom-call | tf_op jit(solution)/shard_map/attend_cache/pallas_call | solution.py:299
  136.0 0.0 collective-permute-done.8.refs_2_.refs_5_
  136.0 3.8 %attend_new.1 = bf16[8,144,256]{2,1,0:T(8,128)(2,1)} custom-call(s32[3]{0:T(128)S(1)} %pad_add_fusion.place_ref, bf16[1024,256]{1,0:T(8,128)(2,1)S(1)} %bitcast.19, f32[128,512]{1,0:T(8,128)S(1)} %get-tuple-element.18.refs_0_.refs_3_, f32[2,128,512]{2,1,0:T(8,128)S(1)} %collective-permute-done.7.refs_1_.refs_4_, ...), custom_call_target="tpu_custom_call" | custom-call | tf_op jit(solution)/shard_map/attend_new/pallas_call | solution.py:318
  139.8 3.5 %all-to-all-start.2 = ((bf16[8,144,256]{2,1,0:T(8,128)(2,1)}), bf16[8,144,256]{2,1,0:T(8,128)(2,1)S(1)}, u32[]{:S(2)}, u32[]{:S(2)}) async-start(bf16[8,144,256]{2,1,0:T(8,128)(2,1)} %attend_new.1), calls=%async_computation.2 | async-start | bytes 1179648 | tf_op jit(solution)/shard_map/all_to_all | solution.py:335
  143.3 1.9 collective-permute-start.10
  145.3 0.0 collective-permute-done.9.far_w_ref
  145.3 2.4 %collective-permute-start.11 = (bf16[8,128,256]{2,1,0:T(8,128)(2,1)S(1)}, bf16[8,128,256]{2,1,0:T(8,128)(2,1)S(1)}, u32[]{:S(2)}, u32[]{:S(2)}) collective-permute-start(bf16[8,128,256]{2,1,0:T(8,128)(2,1)S(1)} %collective-permute-done.9.far_w_ref), channel_id=1, source_target_pairs={{0,128},{128,0},{1,129},{129,1},{2,130},{130,2},{3,131},{131,3},{4... | collective-permute-start | bytes 1572872 | tf_op jit(solution)/shard_map/ppermute | solution.py:34
  147.7 0.0 collective-permute-done.10.swap_w_ref
  147.7 1.5 collective-permute-done.11.swap_far_w_ref
  149.2 13.4 %all-to-all-done.2.parts_ref = bf16[8,144,256]{2,1,0:T(8,128)(2,1)S(1)} async-done(((bf16[8,144,256]{2,1,0:T(8,128)(2,1)}), bf16[8,144,256]{2,1,0:T(8,128)(2,1)S(1)}, u32[]{:S(2)}, u32[]{:S(2)}) %all-to-all-start.2) | async-done | bytes 589856 | tf_op jit(solution)/shard_map/all_to_all | solution.py:335
  162.6 1.9 shard_map.85
  164.5 32.2 %all_to_all.20 = bf16[16,128,256]{2,1,0:T(8,128)(2,1)S(1)} all-to-all(bf16[16,128,256]{2,1,0:T(8,128)(2,1)S(1)} %shard_map.85), channel_id=1, replica_groups=mesh['x_hi'=2,'core'=2,'y'=8,'x_lo'=2,'z_4'=2,'z_2'=2,'z_1'=2] {'y','x_lo'}, dimensions={0} | all-to-all | bytes 2097152 | tf_op jit(solution)/shard_map/all_to_all | solution.py:338
  196.7 0.8 reduce_sum.12
  (10 shorter events, 0.1 us)
Async XLA Ops:
  6.5 86.0 %all-gather.3.cloned.1.call-start = ((), (), s32[]{:S(2)}) async-start(), calls=%async_computation.4 | async-start | bytes 2359296 | tf_op jit(solution)/shard_map/all_gather | solution.py:260
  9.7 41.4 %copy-start = (bf16[128,256]{1,0:T(8,128)(2,1)S(1)}, bf16[128,256]{1,0:T(8,128)(2,1)}, u32[]{:S(2)}) copy-start(bf16[128,256]{1,0:T(8,128)(2,1)} %query_ref.1) | copy-start | bytes 196612
  11.7 36.6 %all-to-all-start = ((bf16[16,128,256]{2,1,0:T(8,128)(2,1)}), bf16[16,128,256]{2,1,0:T(8,128)(2,1)S(1)}, u32[]{:S(2)}, u32[]{:S(2)}) async-start(bf16[16,128,256]{2,1,0:T(8,128)(2,1)} %broadcast_in_dim.26), calls=%async_computation | async-start | bytes 2097152 | tf_op jit(solution)/shard_map/all_to_all | solution.py:30
  49.2 28.5 %collective-permute-start = (bf16[2,4,128,256]{3,2,1,0:T(8,128)(2,1)S(1)}, bf16[2,4,128,256]{3,2,1,0:T(8,128)(2,1)S(1)}, u32[]{:S(2)}, u32[]{:S(2)}) collective-permute-start(bf16[2,4,128,256]{3,2,1,0:T(8,128)(2,1)S(1)} %get-tuple-element.15), channel_id=1, source_target_pairs={{0,128},{128,0},{1,129},{129,1},{2,130},{130,2},{3,131},{131,3},{4... | collective-permute-start | bytes 1572872 | tf_op jit(solution)/shard_map/ppermute | solution.py:34
  51.1 7.9 %collective-permute-start.1 = (bf16[1,128,256]{2,1,0:T(8,128)(2,1)S(1)}, bf16[1,128,256]{2,1,0:T(8,128)(2,1)S(1)}, u32[]{:S(2)}, u32[]{:S(2)}) collective-permute-start(bf16[1,128,256]{2,1,0:T(8,128)(2,1)S(1)} %bitcast.27), channel_id=1, source_target_pairs={{0,256},{256,0},{1,257},{257,1},{2,258},{258,2},{3,259},{259,3},{4... | collective-permute-start | bytes 196616 | tf_op jit(solution)/shard_map/ppermute | solution.py:34
  59.0 13.8 %collective-permute-start.2 = (bf16[1,128,256]{2,1,0:T(8,128)(2,1)S(1)}, bf16[1,128,256]{2,1,0:T(8,128)(2,1)S(1)}, u32[]{:S(2)}, u32[]{:S(2)}) collective-permute-start(bf16[1,128,256]{2,1,0:T(8,128)(2,1)S(1)} %collective-permute-done.1), channel_id=1, source_target_pairs={{0,4},{4,0},{1,5},{5,1},{2,6},{6,2},{3,7},{7,3},{8,12},{12,8},{9,1... | collective-permute-start | bytes 196616 | tf_op jit(solution)/shard_map/ppermute | solution.py:34
  72.8 10.1 %collective-permute-start.3 = (bf16[2,128,256]{2,1,0:T(8,128)(2,1)S(1)}, bf16[2,128,256]{2,1,0:T(8,128)(2,1)S(1)}, u32[]{:S(2)}, u32[]{:S(2)}) collective-permute-start(bf16[2,128,256]{2,1,0:T(8,128)(2,1)S(1)} %pad_maximum_fusion.1), channel_id=1, source_target_pairs={{0,2},{2,0},{1,3},{3,1},{4,6},{6,4},{5,7},{7,5},{8,10},{10,8},{9,1... | collective-permute-start | bytes 393224 | tf_op jit(solution)/shard_map/ppermute | solution.py:34
  77.7 18.4 %collective-permute-start.6 = (bf16[2,4,128,256]{3,2,1,0:T(8,128)(2,1)S(1)}, bf16[2,4,128,256]{3,2,1,0:T(8,128)(2,1)S(1)}, u32[]{:S(2)}, u32[]{:S(2)}) collective-permute-start(bf16[2,4,128,256]{3,2,1,0:T(8,128)(2,1)S(1)} %pad_maximum_fusion), channel_id=1, source_target_pairs={{0,256},{256,0},{1,257},{257,1},{2,258},{258,2},{3,259},{259,3},{4... | collective-permute-start | bytes 1572872 | tf_op jit(solution)/shard_map/ppermute | solution.py:34
  82.8 9.7 %collective-permute-start.4 = (bf16[4,128,256]{2,1,0:T(8,128)(2,1)S(1)}, bf16[4,128,256]{2,1,0:T(8,128)(2,1)S(1)}, u32[]{:S(2)}, u32[]{:S(2)}) collective-permute-start(bf16[4,128,256]{2,1,0:T(8,128)(2,1)S(1)} %constant_dynamic-update-slice_fusion.far_w_ref), channel_id=1, source_target_pairs={{0,1},{1,0},{2,3},{3,2},{4,5},{5,4},{6,7},{7,6},{8,9},{9,8},{10,11... | collective-permute-start | bytes 786440 | tf_op jit(solution)/shard_map/ppermute | solution.py:34
  94.2 6.3 %collective-permute-start.5 = (f32[128,256]{1,0:T(8,128)S(1)}, f32[128,256]{1,0:T(8,128)S(1)}, u32[]{:S(2)}, u32[]{:S(2)}) collective-permute-start(f32[128,256]{1,0:T(8,128)S(1)} %get-tuple-element.17), channel_id=1, source_target_pairs={{0,128},{128,0},{1,129},{129,1},{2,130},{130,2},{3,131},{131,3},{4... | collective-permute-start | bytes 393224 | tf_op jit(solution)/shard_map/ppermute | solution.py:34
  98.0 8.7 %collective-permute-start.7 = (f32[2,128,512]{2,1,0:T(8,128)S(1)}, f32[2,128,512]{2,1,0:T(8,128)S(1)}, u32[]{:S(2)}, u32[]{:S(2)}) collective-permute-start(f32[2,128,512]{2,1,0:T(8,128)S(1)} %get-tuple-element.19), channel_id=1, source_target_pairs={{0,128},{128,0},{1,129},{129,1},{2,130},{130,2},{3,131},{131,3},{4... | collective-permute-start | bytes 1572872 | tf_op jit(solution)/shard_map/ppermute | solution.py:34
  101.3 23.1 %all-to-all-start.1 = ((bf16[8,128,256]{2,1,0:T(8,128)(2,1)}), bf16[8,128,256]{2,1,0:T(8,128)(2,1)S(1)}, u32[]{:S(2)}, u32[]{:S(2)}) async-start(bf16[8,128,256]{2,1,0:T(8,128)(2,1)} %broadcast_in_dim.28), calls=%async_computation.1 | async-start | bytes 1048576 | tf_op jit(solution)/shard_map/all_to_all | solution.py:30
  106.8 29.2 %collective-permute-start.8 = (f32[128,512]{1,0:T(8,128)S(1)}, f32[128,512]{1,0:T(8,128)S(1)}, u32[]{:S(2)}, u32[]{:S(2)}) collective-permute-start(f32[128,512]{1,0:T(8,128)S(1)} %fusion), channel_id=1, source_target_pairs={{0,256},{256,0},{1,257},{257,1},{2,258},{258,2},{3,259},{259,3},{4... | collective-permute-start | bytes 786440 | tf_op jit(solution)/shard_map/ppermute | solution.py:34
  111.9 33.3 %collective-permute-start.9 = (bf16[8,128,256]{2,1,0:T(8,128)(2,1)S(1)}, bf16[8,128,256]{2,1,0:T(8,128)(2,1)S(1)}, u32[]{:S(2)}, u32[]{:S(2)}) collective-permute-start(bf16[8,128,256]{2,1,0:T(8,128)(2,1)S(1)} %slice.18.w_ref), channel_id=1, source_target_pairs={{0,256},{256,0},{1,257},{257,1},{2,258},{258,2},{3,259},{259,3},{4... | collective-permute-start | bytes 1572872 | tf_op jit(solution)/shard_map/ppermute | solution.py:34
  139.8 22.8 %all-to-all-start.2 = ((bf16[8,144,256]{2,1,0:T(8,128)(2,1)}), bf16[8,144,256]{2,1,0:T(8,128)(2,1)S(1)}, u32[]{:S(2)}, u32[]{:S(2)}) async-start(bf16[8,144,256]{2,1,0:T(8,128)(2,1)} %attend_new.1), calls=%async_computation.2 | async-start | bytes 1179648 | tf_op jit(solution)/shard_map/all_to_all | solution.py:335
  143.3 4.4 %collective-permute-start.10 = (bf16[8,128,256]{2,1,0:T(8,128)(2,1)S(1)}, bf16[8,128,256]{2,1,0:T(8,128)(2,1)S(1)}, u32[]{:S(2)}, u32[]{:S(2)}) collective-permute-start(bf16[8,128,256]{2,1,0:T(8,128)(2,1)S(1)} %slice.18.w_ref), channel_id=1, source_target_pairs={{0,128},{128,0},{1,129},{129,1},{2,130},{130,2},{3,131},{131,3},{4... | collective-permute-start | bytes 1572872 | tf_op jit(solution)/shard_map/ppermute | solution.py:34
  145.3 3.9 %collective-permute-start.11 = (bf16[8,128,256]{2,1,0:T(8,128)(2,1)S(1)}, bf16[8,128,256]{2,1,0:T(8,128)(2,1)S(1)}, u32[]{:S(2)}, u32[]{:S(2)}) collective-permute-start(bf16[8,128,256]{2,1,0:T(8,128)(2,1)S(1)} %collective-permute-done.9.far_w_ref), channel_id=1, source_target_pairs={{0,128},{128,0},{1,129},{129,1},{2,130},{130,2},{3,131},{131,3},{4... | collective-permute-start | bytes 1572872 | tf_op jit(solution)/shard_map/ppermute | solution.py:34
Sparse Core Ops, SparseCore 0:
  9.8 48.7 all-gather.2

commit v8 on v7

--- a/solution.py
+++ b/solution.py
@@ -19,6 +19,7 @@
 VMEM = pltpu.CompilerParams(vmem_limit_bytes=48 * 1024 * 1024)
 SCALAR = pl.BlockSpec(memory_space=pltpu.SMEM)
 WHOLE = pl.BlockSpec(memory_space=pltpu.VMEM)
+IN_PLACE = pl.BlockSpec(memory_space=pl.ANY)
 
 
 def dot(a, b):
@@ -75,7 +76,11 @@
     other_out[...] = total[own_out.shape[0] :]
 
 
-def pair_kernel(place_ref, keep_ref, other_ref, far_ref, key_w_ref, value_w_ref, near_out, far_out, other_out):
+def pair_kernel(place_ref, keep_ref, other_ref, far_ref, key_w_ref, value_w_ref, packed_ref, *refs):
+    near_out, far_out, other_out, out_w_ref, sem = refs
+    last = packed_ref.shape[1] - out_w_ref.shape[1]
+    out_w = pltpu.make_async_copy(packed_ref.at[:, last:], out_w_ref, sem)
+    out_w.start()
     rows, width = near_out.shape[0], key_w_ref.shape[2]
     outs = (near_out, far_out, other_out.at[0], other_out.at[1])
     for lane, w_ref in ((0, key_w_ref), (width, value_w_ref)):
@@ -86,6 +91,7 @@
             total = part if total is None else total + part
         for n, out_ref in enumerate(outs):
             out_ref[:, lane : lane + width] = total[n * rows : (n + 1) * rows]
+    out_w.wait()
 
 
 def pack_kernel(query_ref, pair_ref, out_w_ref, out_ref, pair_buf, out_w_buf, split_buf, fold_buf, sems):
@@ -228,14 +234,15 @@
         block = (kv_count, local_rows, width)
         return pl.BlockSpec(block, lambda i: (0, index, 0)), in_hbm(weights)
 
-    def call(kernel, shapes, *operands):
+    def call(kernel, shapes, *operands, out_specs=None, scratch=()):
         pairs = [o if isinstance(o, tuple) else (WHOLE, o) for o in operands]
         return pl.pallas_call(
             kernel,
             grid=(1,),
             out_shape=shapes,
             in_specs=[SCALAR] + [spec for spec, _ in pairs],
-            out_specs=jax.tree.map(lambda _: WHOLE, shapes),
+            out_specs=out_specs or jax.tree.map(lambda _: WHOLE, shapes),
+            scratch_shapes=scratch,
             compiler_params=VMEM,
         )(own, *(operand for _, operand in pairs))
 
@@ -258,10 +265,6 @@
         name="pack",
     )(*sources)
     weights = lax.all_gather(weights, KV, axis=0, tiled=False)
-    out_w = weights[:, 3 * local_rows :]
-    out_w_far = swapped(out_w, "x_hi")
-    out_w_core = swapped(out_w, "core")
-    out_w_both = swapped(out_w_far, "core")
 
     half = jax.ShapeDtypeStruct((2, 4, local_rows, width), jnp.bfloat16)
     keep, send = call(normalize_kernel, (half, half), gathered)
@@ -274,17 +277,24 @@
     far = swapped(jnp.stack([keep[1], other[1]]), "x_hi")
     partial = jax.ShapeDtypeStruct((local_rows, 2 * width), jnp.float32)
     both = jax.ShapeDtypeStruct((2, local_rows, 2 * width), jnp.float32)
-    pair_near, pair_far, theirs = call(
+    pair_near, pair_far, theirs, out_w = call(
         pair_kernel,
-        (partial, partial, both),
+        (partial, partial, both, jax.ShapeDtypeStruct((kv_count, local_rows, width), jnp.bfloat16)),
         keep,
         other,
         far,
         part_of_weights(1),
         part_of_weights(2),
+        (IN_PLACE, in_hbm(weights)),
+        out_specs=(WHOLE, WHOLE, WHOLE, IN_PLACE),
+        scratch=[pltpu.SemaphoreType.DMA],
     )
     pair_core = swapped(theirs, "core")
     pair_far = swapped(pair_far + pair_core[1], "x_hi")
+    out_w_far = swapped(out_w, "x_hi")
+    out_w_core = swapped(out_w, "core")
+    out_w_both = swapped(out_w_far, "core")
+
     place = kv * cache_rows + lax.iota(jnp.int32, cache_rows)
     usable = (place >= key_start[0]) & (place < key_end[0])
     bias = jnp.broadcast_to(jnp.where(usable, 0.0, DEAD).astype(jnp.float32)[None], (8, cache_rows))

time: 205 us -> 206 us (level)
  transfers between devices with their start and end apart: 16 -> 16, of which waited for: 8 -> 8; matrix products, arithmetic and copies ran while one was open for 2% -> 1% of each run, Pallas kernels for 10% -> 10%
where the time goes in v8:
time: 206 us; the launch traced here: 205 us
  waiting for transfers between devices  70.8 us (34%)
  starting transfers between devices  57.8 us (28%)
  blocking collectives  32.2 us (16%)
  Pallas kernels  25.5 us (12%)
  between operations  15 us (7%)
  local copies, waits for them, and re-layouts  2.86 us (1%)
    ppermute x12, starting transfers between devices, swapped(): return lax.ppermute(value, axis, [(0, 1), (1, 0)])  40.9 us
    all_to_all x2, waiting for transfers between devices, shared(): return lax.all_to_all(copies, axes, split_axis=0, concat_axis=0, tiled=True)  37.6 us
    all_to_all x1, blocking collectives, shards(): lax.all_to_all(columns, HEAD, split_axis=0, concat_axis=0, tiled=True)  32.2 us
    ppermute x12, waiting for transfers between devices, swapped(): return lax.ppermute(value, axis, [(0, 1), (1, 0)])  19.7 us
    all_to_all x1, waiting for transfers between devices, shards(): arrived = lax.all_to_all(parts, KV, split_axis=0, concat_axis=0, tiled=True)  13.4 us
    all_to_all x2, starting transfers between devices, shared(): return lax.all_to_all(copies, axes, split_axis=0, concat_axis=0, tiled=True)  13.3 us
    pallas_call x1, Pallas kernels, shards(): pl.pallas_call(cache_kernel, grid=grid, out_shape=(jax.ShapeDtypeStruct((...  11.5 us
    pallas_call x4, Pallas kernels, call(): pl.pallas_call(kernel, grid=(1,), out_shape=shapes, in_specs=[SCALAR] + [...  7.06 us
  transfers between devices with their start and end apart: 16, of which 8 were waited for; matrix products, arithmetic and copies ran while one was open for 1% of the time, Pallas kernels for 10%

profile of v8, /device:TPU:4, one launch (start us, length us, event | category | flops | bytes accessed | tf_op | source)
XLA Modules:
  0.0 205.2 jit_solution(601201593341477368)
XLA Ops:
  6.5 0.0 all-gather.3.cloned.1.call-start
  6.5 3.1 %pack.1 = bf16[512,256]{1,0:T(8,128)(2,1)} custom-call(bf16[128,256]{1,0:T(8,128)(2,1)} %query_ref.1, bf16[128,2,256]{2,1,0:T(2,128)(2,1)} %pair_ref.1, bf16[256,128]{1,0:T(8,128)(2,1)} %out_w_ref.1), custom_call_target="tpu_custom_call" | custom-call | tf_op jit(solution)/shard_map/pack/pallas_call | solution.py:253
  9.7 0.0 all-gather.3.cloned.1.call-update
  9.7 0.0 copy-start
  9.7 2.0 broadcast_in_dim.26
  11.7 7.8 %all-to-all-start = ((bf16[16,128,256]{2,1,0:T(8,128)(2,1)}), bf16[16,128,256]{2,1,0:T(8,128)(2,1)S(1)}, u32[]{:S(2)}, u32[]{:S(2)}) async-start(bf16[16,128,256]{2,1,0:T(8,128)(2,1)} %broadcast_in_dim.26), calls=%async_computation | async-start | bytes 2097152 | tf_op jit(solution)/shard_map/all_to_all | solution.py:31
  19.5 0.1 pad_add_fusion.place_ref
  19.6 28.6 %all-to-all-done.x_ref = bf16[16,128,256]{2,1,0:T(8,128)(2,1)S(1)} async-done(((bf16[16,128,256]{2,1,0:T(8,128)(2,1)}), bf16[16,128,256]{2,1,0:T(8,128)(2,1)S(1)}, u32[]{:S(2)}, u32[]{:S(2)}) %all-to-all-start) | async-done | bytes 1048608 | tf_op jit(solution)/shard_map/all_to_all | solution.py:31
  48.2 0.9 shard_map.82
  49.2 1.9 collective-permute-start
  51.1 0.0 copy-done
  51.1 2.5 %collective-permute-start.1 = (bf16[1,128,256]{2,1,0:T(8,128)(2,1)S(1)}, bf16[1,128,256]{2,1,0:T(8,128)(2,1)S(1)}, u32[]{:S(2)}, u32[]{:S(2)}) collective-permute-start(bf16[1,128,256]{2,1,0:T(8,128)(2,1)S(1)} %bitcast.27), channel_id=1, source_target_pairs={{0,256},{256,0},{1,257},{257,1},{2,258},{258,2},{3,259},{259,3},{4... | collective-permute-start | bytes 196616 | tf_op jit(solution)/shard_map/ppermute | solution.py:35
  53.6 5.4 %collective-permute-done.1 = bf16[1,128,256]{2,1,0:T(8,128)(2,1)S(1)} collective-permute-done((bf16[1,128,256]{2,1,0:T(8,128)(2,1)S(1)}, bf16[1,128,256]{2,1,0:T(8,128)(2,1)S(1)}, u32[]{:S(2)}, u32[]{:S(2)}) %collective-permute-start.1) | collective-permute-done | bytes 65568 | tf_op jit(solution)/shard_map/ppermute | solution.py:35
  59.0 10.9 %collective-permute-start.2 = (bf16[1,128,256]{2,1,0:T(8,128)(2,1)S(1)}, bf16[1,128,256]{2,1,0:T(8,128)(2,1)S(1)}, u32[]{:S(2)}, u32[]{:S(2)}) collective-permute-start(bf16[1,128,256]{2,1,0:T(8,128)(2,1)S(1)} %collective-permute-done.1), channel_id=1, source_target_pairs={{0,4},{4,0},{1,5},{5,1},{2,6},{6,2},{3,7},{7,3},{8,12},{12,8},{9,1... | collective-permute-start | bytes 196616 | tf_op jit(solution)/shard_map/ppermute | solution.py:35
  69.9 2.8 %collective-permute-done.2 = bf16[1,128,256]{2,1,0:T(8,128)(2,1)S(1)} collective-permute-done((bf16[1,128,256]{2,1,0:T(8,128)(2,1)S(1)}, bf16[1,128,256]{2,1,0:T(8,128)(2,1)S(1)}, u32[]{:S(2)}, u32[]{:S(2)}) %collective-permute-start.2) | collective-permute-done | bytes 65568 | tf_op jit(solution)/shard_map/ppermute | solution.py:35
  72.8 4.8 %collective-permute-start.3 = (bf16[2,128,256]{2,1,0:T(8,128)(2,1)S(1)}, bf16[2,128,256]{2,1,0:T(8,128)(2,1)S(1)}, u32[]{:S(2)}, u32[]{:S(2)}) collective-permute-start(bf16[2,128,256]{2,1,0:T(8,128)(2,1)S(1)} %pad_maximum_fusion.1), channel_id=1, source_target_pairs={{0,2},{2,0},{1,3},{3,1},{4,6},{6,4},{5,7},{7,5},{8,10},{10,8},{9,1... | collective-permute-start | bytes 393224 | tf_op jit(solution)/shard_map/ppermute | solution.py:35
  77.6 0.0 collective-permute-done.other_ref
  77.6 0.1 pad_maximum_fusion
  77.7 2.7 %collective-permute-start.6 = (bf16[2,4,128,256]{3,2,1,0:T(8,128)(2,1)S(1)}, bf16[2,4,128,256]{3,2,1,0:T(8,128)(2,1)S(1)}, u32[]{:S(2)}, u32[]{:S(2)}) collective-permute-start(bf16[2,4,128,256]{3,2,1,0:T(8,128)(2,1)S(1)} %pad_maximum_fusion), channel_id=1, source_target_pairs={{0,256},{256,0},{1,257},{257,1},{2,258},{258,2},{3,259},{259,3},{4... | collective-permute-start | bytes 1572872 | tf_op jit(solution)/shard_map/ppermute | solution.py:35
  80.4 2.4 %collective-permute-done.3 = bf16[2,128,256]{2,1,0:T(8,128)(2,1)S(1)} collective-permute-done((bf16[2,128,256]{2,1,0:T(8,128)(2,1)S(1)}, bf16[2,128,256]{2,1,0:T(8,128)(2,1)S(1)}, u32[]{:S(2)}, u32[]{:S(2)}) %collective-permute-start.3) | collective-permute-done | bytes 131104 | tf_op jit(solution)/shard_map/ppermute | solution.py:35
  82.8 2.1 %collective-permute-start.4 = (bf16[4,128,256]{2,1,0:T(8,128)(2,1)S(1)}, bf16[4,128,256]{2,1,0:T(8,128)(2,1)S(1)}, u32[]{:S(2)}, u32[]{:S(2)}) collective-permute-start(bf16[4,128,256]{2,1,0:T(8,128)(2,1)S(1)} %constant_dynamic-update-slice_fusion.far_w_ref), channel_id=1, source_target_pairs={{0,1},{1,0},{2,3},{3,2},{4,5},{5,4},{6,7},{7,6},{8,9},{9,8},{10,11... | collective-permute-start | bytes 786440 | tf_op jit(solution)/shard_map/ppermute | solution.py:35
  84.9 7.6 %collective-permute-done.4.away_w_ref = bf16[4,128,256]{2,1,0:T(8,128)(2,1)S(1)} collective-permute-done((bf16[4,128,256]{2,1,0:T(8,128)(2,1)S(1)}, bf16[4,128,256]{2,1,0:T(8,128)(2,1)S(1)}, u32[]{:S(2)}, u32[]{:S(2)}) %collective-permute-start.4) | collective-permute-done | bytes 262176 | tf_op jit(solution)/shard_map/ppermute | solution.py:35
  92.6 0.0 all-gather.3.cloned.1.call-done
  92.6 1.6 shard_map.83
  94.2 1.9 collective-permute-start.5
  96.1 0.0 collective-permute-done.6.far_ref
  96.1 2.7 %shard_map.84 = (f32[128,512]{1,0:T(8,128)S(1)}, f32[128,512]{1,0:T(8,128)S(1)}, f32[2,128,512]{2,1,0:T(8,128)S(1)}, bf16[8,128,256]{2,1,0:T(8,128)(2,1)S(1)}) custom-call(s32[3]{0:T(128)S(1)} %pad_add_fusion.place_ref, bf16[2,4,128,256]{3,2,1,0:T(8,128)(2,1)S(1)} %get-tuple-element.15.keep_ref, bf16[2,4,128,256]{3,2,1,0:T(8,128)(2,1)S(1)} %collective-permute-done.other_ref, ...), custom_call_target="tpu_custom_call" | custom-call | tf_op jit(solution)/shard_map/pallas_call | solution.py:239
  98.8 2.4 %collective-permute-start.7 = (f32[2,128,512]{2,1,0:T(8,128)S(1)}, f32[2,128,512]{2,1,0:T(8,128)S(1)}, u32[]{:S(2)}, u32[]{:S(2)}) collective-permute-start(f32[2,128,512]{2,1,0:T(8,128)S(1)} %get-tuple-element.20), channel_id=1, source_target_pairs={{0,128},{128,0},{1,129},{129,1},{2,130},{130,2},{3,131},{131,3},{4... | collective-permute-start | bytes 1572872 | tf_op jit(solution)/shard_map/ppermute | solution.py:35
  101.2 0.0 collective-permute-done.5
  101.3 0.8 broadcast_in_dim.28
  102.1 5.5 %all-to-all-start.1 = ((bf16[8,128,256]{2,1,0:T(8,128)(2,1)}), bf16[8,128,256]{2,1,0:T(8,128)(2,1)S(1)}, u32[]{:S(2)}, u32[]{:S(2)}) async-start(bf16[8,128,256]{2,1,0:T(8,128)(2,1)} %broadcast_in_dim.28), calls=%async_computation.1 | async-start | bytes 1048576 | tf_op jit(solution)/shard_map/all_to_all | solution.py:31
  107.6 0.0 collective-permute-done.7.refs_1_.refs_4_
  107.6 2.7 %collective-permute-start.8 = (f32[128,512]{1,0:T(8,128)S(1)}, f32[128,512]{1,0:T(8,128)S(1)}, u32[]{:S(2)}, u32[]{:S(2)}) collective-permute-start(f32[128,512]{1,0:T(8,128)S(1)} %fusion), channel_id=1, source_target_pairs={{0,256},{256,0},{1,257},{257,1},{2,258},{258,2},{3,259},{259,3},{4... | collective-permute-start | bytes 786440 | tf_op jit(solution)/shard_map/ppermute | solution.py:35
  111.6 4.6 %collective-permute-start.9 = (bf16[8,128,256]{2,1,0:T(8,128)(2,1)S(1)}, bf16[8,128,256]{2,1,0:T(8,128)(2,1)S(1)}, u32[]{:S(2)}, u32[]{:S(2)}) collective-permute-start(bf16[8,128,256]{2,1,0:T(8,128)(2,1)S(1)} %get-tuple-element.24.w_ref), channel_id=1, source_target_pairs={{0,256},{256,0},{1,257},{257,1},{2,258},{258,2},{3,259},{259,3},{4... | collective-permute-start | bytes 1572872 | tf_op jit(solution)/shard_map/ppermute | solution.py:35
  116.3 8.9 %all-to-all-done.1 = bf16[8,128,256]{2,1,0:T(8,128)(2,1)S(1)} async-done(((bf16[8,128,256]{2,1,0:T(8,128)(2,1)}), bf16[8,128,256]{2,1,0:T(8,128)(2,1)S(1)}, u32[]{:S(2)}, u32[]{:S(2)}) %all-to-all-start.1) | async-done | bytes 524320 | tf_op jit(solution)/shard_map/all_to_all | solution.py:31
  125.2 11.5 %attend_cache.1 = (f32[2,1024,128]{2,1,0:T(8,128)S(1)}, f32[2,1024,256]{2,1,0:T(8,128)S(1)}) custom-call(f32[8,2048]{1,0:T(8,128)S(1)} %broadcast_in_dim.31.bias_ref, bf16[1024,256]{1,0:T(8,128)(2,1)S(1)} %bitcast.18, bf16[2048,256]{1,0:T(8,128)(2,1)} %bitcast.24, bf16[2048,256]{1,0:T(8,128)(2,1)} %bitcast.25), custom_call_target="tpu_custom_call" | custom-call | tf_op jit(solution)/shard_map/attend_cache/pallas_call | solution.py:309
  136.8 0.0 collective-permute-done.8.refs_2_.refs_5_
  136.8 3.8 %attend_new.1 = bf16[8,144,256]{2,1,0:T(8,128)(2,1)} custom-call(s32[3]{0:T(128)S(1)} %pad_add_fusion.place_ref, bf16[1024,256]{1,0:T(8,128)(2,1)S(1)} %bitcast.19, f32[128,512]{1,0:T(8,128)S(1)} %get-tuple-element.19.refs_0_.refs_3_, f32[2,128,512]{2,1,0:T(8,128)S(1)} %collective-permute-done.7.refs_1_.refs_4_, ...), custom_call_target="tpu_custom_call" | custom-call | tf_op jit(solution)/shard_map/attend_new/pallas_call | solution.py:328
  140.6 3.5 %all-to-all-start.2 = ((bf16[8,144,256]{2,1,0:T(8,128)(2,1)}), bf16[8,144,256]{2,1,0:T(8,128)(2,1)S(1)}, u32[]{:S(2)}, u32[]{:S(2)}) async-start(bf16[8,144,256]{2,1,0:T(8,128)(2,1)} %attend_new.1), calls=%async_computation.2 | async-start | bytes 1179648 | tf_op jit(solution)/shard_map/all_to_all | solution.py:345
  144.1 1.9 collective-permute-start.10
  146.1 0.0 collective-permute-done.9.far_w_ref
  146.1 2.4 %collective-permute-start.11 = (bf16[8,128,256]{2,1,0:T(8,128)(2,1)S(1)}, bf16[8,128,256]{2,1,0:T(8,128)(2,1)S(1)}, u32[]{:S(2)}, u32[]{:S(2)}) collective-permute-start(bf16[8,128,256]{2,1,0:T(8,128)(2,1)S(1)} %collective-permute-done.9.far_w_ref), channel_id=1, source_target_pairs={{0,128},{128,0},{1,129},{129,1},{2,130},{130,2},{3,131},{131,3},{4... | collective-permute-start | bytes 1572872 | tf_op jit(solution)/shard_map/ppermute | solution.py:35
  148.5 0.0 collective-permute-done.10.swap_w_ref
  148.5 1.5 collective-permute-done.11.swap_far_w_ref
  150.0 13.4 %all-to-all-done.2.parts_ref = bf16[8,144,256]{2,1,0:T(8,128)(2,1)S(1)} async-done(((bf16[8,144,256]{2,1,0:T(8,128)(2,1)}), bf16[8,144,256]{2,1,0:T(8,128)(2,1)S(1)}, u32[]{:S(2)}, u32[]{:S(2)}) %all-to-all-start.2) | async-done | bytes 589856 | tf_op jit(solution)/shard_map/all_to_all | solution.py:345
  163.5 1.9 shard_map.85
  165.3 32.2 %all_to_all.20 = bf16[16,128,256]{2,1,0:T(8,128)(2,1)S(1)} all-to-all(bf16[16,128,256]{2,1,0:T(8,128)(2,1)S(1)} %shard_map.85), channel_id=1, replica_groups=mesh['x_hi'=2,'core'=2,'y'=8,'x_lo'=2,'z_4'=2,'z_2'=2,'z_1'=2] {'y','x_lo'}, dimensions={0} | all-to-all | bytes 2097152 | tf_op jit(solution)/shard_map/all_to_all | solution.py:348
  197.6 0.8 reduce_sum.12
  (10 shorter events, 0.1 us)
Async XLA Ops:
  6.5 86.0 %all-gather.3.cloned.1.call-start = ((), (), s32[]{:S(2)}) async-start(), calls=%async_computation.4 | async-start | bytes 2359296 | tf_op jit(solution)/shard_map/all_gather | solution.py:267
  9.7 41.4 %copy-start = (bf16[128,256]{1,0:T(8,128)(2,1)S(1)}, bf16[128,256]{1,0:T(8,128)(2,1)}, u32[]{:S(2)}) copy-start(bf16[128,256]{1,0:T(8,128)(2,1)} %query_ref.1) | copy-start | bytes 196612
  11.7 36.6 %all-to-all-start = ((bf16[16,128,256]{2,1,0:T(8,128)(2,1)}), bf16[16,128,256]{2,1,0:T(8,128)(2,1)S(1)}, u32[]{:S(2)}, u32[]{:S(2)}) async-start(bf16[16,128,256]{2,1,0:T(8,128)(2,1)} %broadcast_in_dim.26), calls=%async_computation | async-start | bytes 2097152 | tf_op jit(solution)/shard_map/all_to_all | solution.py:31
  49.2 28.5 %collective-permute-start = (bf16[2,4,128,256]{3,2,1,0:T(8,128)(2,1)S(1)}, bf16[2,4,128,256]{3,2,1,0:T(8,128)(2,1)S(1)}, u32[]{:S(2)}, u32[]{:S(2)}) collective-permute-start(bf16[2,4,128,256]{3,2,1,0:T(8,128)(2,1)S(1)} %get-tuple-element.16), channel_id=1, source_target_pairs={{0,128},{128,0},{1,129},{129,1},{2,130},{130,2},{3,131},{131,3},{4... | collective-permute-start | bytes 1572872 | tf_op jit(solution)/shard_map/ppermute | solution.py:35
  51.1 7.9 %collective-permute-start.1 = (bf16[1,128,256]{2,1,0:T(8,128)(2,1)S(1)}, bf16[1,128,256]{2,1,0:T(8,128)(2,1)S(1)}, u32[]{:S(2)}, u32[]{:S(2)}) collective-permute-start(bf16[1,128,256]{2,1,0:T(8,128)(2,1)S(1)} %bitcast.27), channel_id=1, source_target_pairs={{0,256},{256,0},{1,257},{257,1},{2,258},{258,2},{3,259},{259,3},{4... | collective-permute-start | bytes 196616 | tf_op jit(solution)/shard_map/ppermute | solution.py:35
  59.0 13.8 %collective-permute-start.2 = (bf16[1,128,256]{2,1,0:T(8,128)(2,1)S(1)}, bf16[1,128,256]{2,1,0:T(8,128)(2,1)S(1)}, u32[]{:S(2)}, u32[]{:S(2)}) collective-permute-start(bf16[1,128,256]{2,1,0:T(8,128)(2,1)S(1)} %collective-permute-done.1), channel_id=1, source_target_pairs={{0,4},{4,0},{1,5},{5,1},{2,6},{6,2},{3,7},{7,3},{8,12},{12,8},{9,1... | collective-permute-start | bytes 196616 | tf_op jit(solution)/shard_map/ppermute | solution.py:35
  72.8 10.1 %collective-permute-start.3 = (bf16[2,128,256]{2,1,0:T(8,128)(2,1)S(1)}, bf16[2,128,256]{2,1,0:T(8,128)(2,1)S(1)}, u32[]{:S(2)}, u32[]{:S(2)}) collective-permute-start(bf16[2,128,256]{2,1,0:T(8,128)(2,1)S(1)} %pad_maximum_fusion.1), channel_id=1, source_target_pairs={{0,2},{2,0},{1,3},{3,1},{4,6},{6,4},{5,7},{7,5},{8,10},{10,8},{9,1... | collective-permute-start | bytes 393224 | tf_op jit(solution)/shard_map/ppermute | solution.py:35
  77.7 18.4 %collective-permute-start.6 = (bf16[2,4,128,256]{3,2,1,0:T(8,128)(2,1)S(1)}, bf16[2,4,128,256]{3,2,1,0:T(8,128)(2,1)S(1)}, u32[]{:S(2)}, u32[]{:S(2)}) collective-permute-start(bf16[2,4,128,256]{3,2,1,0:T(8,128)(2,1)S(1)} %pad_maximum_fusion), channel_id=1, source_target_pairs={{0,256},{256,0},{1,257},{257,1},{2,258},{258,2},{3,259},{259,3},{4... | collective-permute-start | bytes 1572872 | tf_op jit(solution)/shard_map/ppermute | solution.py:35
  82.8 9.7 %collective-permute-start.4 = (bf16[4,128,256]{2,1,0:T(8,128)(2,1)S(1)}, bf16[4,128,256]{2,1,0:T(8,128)(2,1)S(1)}, u32[]{:S(2)}, u32[]{:S(2)}) collective-permute-start(bf16[4,128,256]{2,1,0:T(8,128)(2,1)S(1)} %constant_dynamic-update-slice_fusion.far_w_ref), channel_id=1, source_target_pairs={{0,1},{1,0},{2,3},{3,2},{4,5},{5,4},{6,7},{7,6},{8,9},{9,8},{10,11... | collective-permute-start | bytes 786440 | tf_op jit(solution)/shard_map/ppermute | solution.py:35
  94.2 7.1 %collective-permute-start.5 = (f32[128,256]{1,0:T(8,128)S(1)}, f32[128,256]{1,0:T(8,128)S(1)}, u32[]{:S(2)}, u32[]{:S(2)}) collective-permute-start(f32[128,256]{1,0:T(8,128)S(1)} %get-tuple-element.18), channel_id=1, source_target_pairs={{0,128},{128,0},{1,129},{129,1},{2,130},{130,2},{3,131},{131,3},{4... | collective-permute-start | bytes 393224 | tf_op jit(solution)/shard_map/ppermute | solution.py:35
  98.8 8.8 %collective-permute-start.7 = (f32[2,128,512]{2,1,0:T(8,128)S(1)}, f32[2,128,512]{2,1,0:T(8,128)S(1)}, u32[]{:S(2)}, u32[]{:S(2)}) collective-permute-start(f32[2,128,512]{2,1,0:T(8,128)S(1)} %get-tuple-element.20), channel_id=1, source_target_pairs={{0,128},{128,0},{1,129},{129,1},{2,130},{130,2},{3,131},{131,3},{4... | collective-permute-start | bytes 1572872 | tf_op jit(solution)/shard_map/ppermute | solution.py:35
  102.1 23.1 %all-to-all-start.1 = ((bf16[8,128,256]{2,1,0:T(8,128)(2,1)}), bf16[8,128,256]{2,1,0:T(8,128)(2,1)S(1)}, u32[]{:S(2)}, u32[]{:S(2)}) async-start(bf16[8,128,256]{2,1,0:T(8,128)(2,1)} %broadcast_in_dim.28), calls=%async_computation.1 | async-start | bytes 1048576 | tf_op jit(solution)/shard_map/all_to_all | solution.py:31
  107.6 29.2 %collective-permute-start.8 = (f32[128,512]{1,0:T(8,128)S(1)}, f32[128,512]{1,0:T(8,128)S(1)}, u32[]{:S(2)}, u32[]{:S(2)}) collective-permute-start(f32[128,512]{1,0:T(8,128)S(1)} %fusion), channel_id=1, source_target_pairs={{0,256},{256,0},{1,257},{257,1},{2,258},{258,2},{3,259},{259,3},{4... | collective-permute-start | bytes 786440 | tf_op jit(solution)/shard_map/ppermute | solution.py:35
  111.6 34.4 %collective-permute-start.9 = (bf16[8,128,256]{2,1,0:T(8,128)(2,1)S(1)}, bf16[8,128,256]{2,1,0:T(8,128)(2,1)S(1)}, u32[]{:S(2)}, u32[]{:S(2)}) collective-permute-start(bf16[8,128,256]{2,1,0:T(8,128)(2,1)S(1)} %get-tuple-element.24.w_ref), channel_id=1, source_target_pairs={{0,256},{256,0},{1,257},{257,1},{2,258},{258,2},{3,259},{259,3},{4... | collective-permute-start | bytes 1572872 | tf_op jit(solution)/shard_map/ppermute | solution.py:35
  140.6 22.9 %all-to-all-start.2 = ((bf16[8,144,256]{2,1,0:T(8,128)(2,1)}), bf16[8,144,256]{2,1,0:T(8,128)(2,1)S(1)}, u32[]{:S(2)}, u32[]{:S(2)}) async-start(bf16[8,144,256]{2,1,0:T(8,128)(2,1)} %attend_new.1), calls=%async_computation.2 | async-start | bytes 1179648 | tf_op jit(solution)/shard_map/all_to_all | solution.py:345
  144.1 4.4 %collective-permute-start.10 = (bf16[8,128,256]{2,1,0:T(8,128)(2,1)S(1)}, bf16[8,128,256]{2,1,0:T(8,128)(2,1)S(1)}, u32[]{:S(2)}, u32[]{:S(2)}) collective-permute-start(bf16[8,128,256]{2,1,0:T(8,128)(2,1)S(1)} %get-tuple-element.24.w_ref), channel_id=1, source_target_pairs={{0,128},{128,0},{1,129},{129,1},{2,130},{130,2},{3,131},{131,3},{4... | collective-permute-start | bytes 1572872 | tf_op jit(solution)/shard_map/ppermute | solution.py:35
  146.1 3.9 %collective-permute-start.11 = (bf16[8,128,256]{2,1,0:T(8,128)(2,1)S(1)}, bf16[8,128,256]{2,1,0:T(8,128)(2,1)S(1)}, u32[]{:S(2)}, u32[]{:S(2)}) collective-permute-start(bf16[8,128,256]{2,1,0:T(8,128)(2,1)S(1)} %collective-permute-done.9.far_w_ref), channel_id=1, source_target_pairs={{0,128},{128,0},{1,129},{129,1},{2,130},{130,2},{3,131},{131,3},{4... | collective-permute-start | bytes 1572872 | tf_op jit(solution)/shard_map/ppermute | solution.py:35
Sparse Core Ops, SparseCore 0:
  9.8 48.7 all-gather.2

commit v9 on v8

--- a/solution.py
+++ b/solution.py
@@ -12,6 +12,7 @@
 KV = ("z_4", "z_2", "z_1")
 STAT_ROWS = 16
 QUERY_ROWS = 512
+NEW_ROWS = 1024
 KEY_ROWS = 512
 DEAD = -1e30
 SCALE = HD**-0.5
@@ -158,7 +159,7 @@
         (near[...] + core[0] + far[...]).astype(jnp.bfloat16) for near, core, far in (pair_refs[:3], pair_refs[3:])
     ]
     s = score(q_ref[...], keys)
-    row = pl.program_id(1) * QUERY_ROWS + lax.broadcasted_iota(jnp.int32, s.shape, 0)
+    row = pl.program_id(1) * NEW_ROWS + lax.broadcasted_iota(jnp.int32, s.shape, 0)
     column = place_ref[2] * keys.shape[0] + lax.broadcasted_iota(jnp.int32, s.shape, 1)
     s = jnp.where(column <= row, s, DEAD)
     cache_peak = peak_ref[0]
@@ -327,17 +328,17 @@
     padded = local_rows + STAT_ROWS
     parts = pl.pallas_call(
         new_kernel,
-        grid=grid,
+        grid=(heads, rows // NEW_ROWS),
         out_shape=jax.ShapeDtypeStruct((kv_count, padded, width), jnp.bfloat16),
         in_specs=[
             SCALAR,
-            query_spec,
+            pl.BlockSpec((NEW_ROWS, HD), lambda h, i: (i, h)),
             *pair_specs(0),
             *pair_specs(heads),
-            peak_spec,
-            total_spec,
+            pl.BlockSpec((1, NEW_ROWS, HD), lambda h, i: (h, i, 0)),
+            pl.BlockSpec((1, NEW_ROWS, 2 * HD), lambda h, i: (h, i, 0)),
         ],
-        out_specs=pl.BlockSpec((QUERY_ROWS // local_rows, padded, HD), lambda h, i: (i, 0, h)),
+        out_specs=pl.BlockSpec((NEW_ROWS // local_rows, padded, HD), lambda h, i: (i, 0, h)),
         compiler_params=VMEM,
         name="attend_new",
     )(own, queries, *(pair_near, pair_core, pair_far) * 2, peaks, totals)

time: 206 us -> 205 us (level)
  no operation moved by 1% of the time
where the time goes in v9:
time: 205 us; the launch traced here: 204 us
  waiting for transfers between devices  70.8 us (35%)
  starting transfers between devices  57.8 us (28%)
  blocking collectives  32.2 us (16%)
  Pallas kernels  24.6 us (12%)
  between operations  15 us (7%)
  local copies, waits for them, and re-layouts  2.86 us (1%)
    ppermute x12, starting transfers between devices, swapped(): return lax.ppermute(value, axis, [(0, 1), (1, 0)])  40.9 us
    all_to_all x2, waiting for transfers between devices, shared(): return lax.all_to_all(copies, axes, split_axis=0, concat_axis=0, tiled=True)  37.6 us
    all_to_all x1, blocking collectives, shards(): lax.all_to_all(columns, HEAD, split_axis=0, concat_axis=0, tiled=True)  32.2 us
    ppermute x12, waiting for transfers between devices, swapped(): return lax.ppermute(value, axis, [(0, 1), (1, 0)])  19.7 us
    all_to_all x1, waiting for transfers between devices, shards(): arrived = lax.all_to_all(parts, KV, split_axis=0, concat_axis=0, tiled=True)  13.4 us
    all_to_all x2, starting transfers between devices, shared(): return lax.all_to_all(copies, axes, split_axis=0, concat_axis=0, tiled=True)  13.3 us
    pallas_call x1, Pallas kernels, shards(): pl.pallas_call(cache_kernel, grid=grid, out_shape=(jax.ShapeDtypeStruct((...  11.5 us
    pallas_call x4, Pallas kernels, call(): pl.pallas_call(kernel, grid=(1,), out_shape=shapes, in_specs=[SCALAR] + [...  7.06 us
  transfers between devices with their start and end apart: 16, of which 8 were waited for; matrix products, arithmetic and copies ran while one was open for 1% of the time, Pallas kernels for 10%

profile of v9, /device:TPU:4, one launch (start us, length us, event | category | flops | bytes accessed | tf_op | source)
XLA Modules:
  0.0 204.3 jit_solution(12152350332500202082)
XLA Ops:
  6.5 0.0 all-gather.3.cloned.1.call-start
  6.5 3.1 %pack.1 = bf16[512,256]{1,0:T(8,128)(2,1)} custom-call(bf16[128,256]{1,0:T(8,128)(2,1)} %query_ref.1, bf16[128,2,256]{2,1,0:T(2,128)(2,1)} %pair_ref.1, bf16[256,128]{1,0:T(8,128)(2,1)} %out_w_ref.1), custom_call_target="tpu_custom_call" | custom-call | tf_op jit(solution)/shard_map/pack/pallas_call | solution.py:254
  9.7 0.0 all-gather.3.cloned.1.call-update
  9.7 0.0 copy-start
  9.7 2.0 broadcast_in_dim.26
  11.7 7.8 %all-to-all-start = ((bf16[16,128,256]{2,1,0:T(8,128)(2,1)}), bf16[16,128,256]{2,1,0:T(8,128)(2,1)S(1)}, u32[]{:S(2)}, u32[]{:S(2)}) async-start(bf16[16,128,256]{2,1,0:T(8,128)(2,1)} %broadcast_in_dim.26), calls=%async_computation | async-start | bytes 2097152 | tf_op jit(solution)/shard_map/all_to_all | solution.py:32
  19.5 0.1 pad_add_fusion.place_ref
  19.6 28.6 %all-to-all-done.x_ref = bf16[16,128,256]{2,1,0:T(8,128)(2,1)S(1)} async-done(((bf16[16,128,256]{2,1,0:T(8,128)(2,1)}), bf16[16,128,256]{2,1,0:T(8,128)(2,1)S(1)}, u32[]{:S(2)}, u32[]{:S(2)}) %all-to-all-start) | async-done | bytes 1048608 | tf_op jit(solution)/shard_map/all_to_all | solution.py:32
  48.2 0.9 shard_map.82
  49.2 1.9 collective-permute-start
  51.1 0.0 copy-done
  51.1 2.5 %collective-permute-start.1 = (bf16[1,128,256]{2,1,0:T(8,128)(2,1)S(1)}, bf16[1,128,256]{2,1,0:T(8,128)(2,1)S(1)}, u32[]{:S(2)}, u32[]{:S(2)}) collective-permute-start(bf16[1,128,256]{2,1,0:T(8,128)(2,1)S(1)} %bitcast.27), channel_id=1, source_target_pairs={{0,256},{256,0},{1,257},{257,1},{2,258},{258,2},{3,259},{259,3},{4... | collective-permute-start | bytes 196616 | tf_op jit(solution)/shard_map/ppermute | solution.py:36
  53.6 5.4 %collective-permute-done.1 = bf16[1,128,256]{2,1,0:T(8,128)(2,1)S(1)} collective-permute-done((bf16[1,128,256]{2,1,0:T(8,128)(2,1)S(1)}, bf16[1,128,256]{2,1,0:T(8,128)(2,1)S(1)}, u32[]{:S(2)}, u32[]{:S(2)}) %collective-permute-start.1) | collective-permute-done | bytes 65568 | tf_op jit(solution)/shard_map/ppermute | solution.py:36
  59.0 10.9 %collective-permute-start.2 = (bf16[1,128,256]{2,1,0:T(8,128)(2,1)S(1)}, bf16[1,128,256]{2,1,0:T(8,128)(2,1)S(1)}, u32[]{:S(2)}, u32[]{:S(2)}) collective-permute-start(bf16[1,128,256]{2,1,0:T(8,128)(2,1)S(1)} %collective-permute-done.1), channel_id=1, source_target_pairs={{0,4},{4,0},{1,5},{5,1},{2,6},{6,2},{3,7},{7,3},{8,12},{12,8},{9,1... | collective-permute-start | bytes 196616 | tf_op jit(solution)/shard_map/ppermute | solution.py:36
  69.9 2.8 %collective-permute-done.2 = bf16[1,128,256]{2,1,0:T(8,128)(2,1)S(1)} collective-permute-done((bf16[1,128,256]{2,1,0:T(8,128)(2,1)S(1)}, bf16[1,128,256]{2,1,0:T(8,128)(2,1)S(1)}, u32[]{:S(2)}, u32[]{:S(2)}) %collective-permute-start.2) | collective-permute-done | bytes 65568 | tf_op jit(solution)/shard_map/ppermute | solution.py:36
  72.8 4.8 %collective-permute-start.3 = (bf16[2,128,256]{2,1,0:T(8,128)(2,1)S(1)}, bf16[2,128,256]{2,1,0:T(8,128)(2,1)S(1)}, u32[]{:S(2)}, u32[]{:S(2)}) collective-permute-start(bf16[2,128,256]{2,1,0:T(8,128)(2,1)S(1)} %pad_maximum_fusion.1), channel_id=1, source_target_pairs={{0,2},{2,0},{1,3},{3,1},{4,6},{6,4},{5,7},{7,5},{8,10},{10,8},{9,1... | collective-permute-start | bytes 393224 | tf_op jit(solution)/shard_map/ppermute | solution.py:36
  77.6 0.0 collective-permute-done.other_ref
  77.6 0.1 pad_maximum_fusion
  77.7 2.7 %collective-permute-start.6 = (bf16[2,4,128,256]{3,2,1,0:T(8,128)(2,1)S(1)}, bf16[2,4,128,256]{3,2,1,0:T(8,128)(2,1)S(1)}, u32[]{:S(2)}, u32[]{:S(2)}) collective-permute-start(bf16[2,4,128,256]{3,2,1,0:T(8,128)(2,1)S(1)} %pad_maximum_fusion), channel_id=1, source_target_pairs={{0,256},{256,0},{1,257},{257,1},{2,258},{258,2},{3,259},{259,3},{4... | collective-permute-start | bytes 1572872 | tf_op jit(solution)/shard_map/ppermute | solution.py:36
  80.4 2.4 %collective-permute-done.3 = bf16[2,128,256]{2,1,0:T(8,128)(2,1)S(1)} collective-permute-done((bf16[2,128,256]{2,1,0:T(8,128)(2,1)S(1)}, bf16[2,128,256]{2,1,0:T(8,128)(2,1)S(1)}, u32[]{:S(2)}, u32[]{:S(2)}) %collective-permute-start.3) | collective-permute-done | bytes 131104 | tf_op jit(solution)/shard_map/ppermute | solution.py:36
  82.8 2.1 %collective-permute-start.4 = (bf16[4,128,256]{2,1,0:T(8,128)(2,1)S(1)}, bf16[4,128,256]{2,1,0:T(8,128)(2,1)S(1)}, u32[]{:S(2)}, u32[]{:S(2)}) collective-permute-start(bf16[4,128,256]{2,1,0:T(8,128)(2,1)S(1)} %constant_dynamic-update-slice_fusion.far_w_ref), channel_id=1, source_target_pairs={{0,1},{1,0},{2,3},{3,2},{4,5},{5,4},{6,7},{7,6},{8,9},{9,8},{10,11... | collective-permute-start | bytes 786440 | tf_op jit(solution)/shard_map/ppermute | solution.py:36
  84.9 7.6 %collective-permute-done.4.away_w_ref = bf16[4,128,256]{2,1,0:T(8,128)(2,1)S(1)} collective-permute-done((bf16[4,128,256]{2,1,0:T(8,128)(2,1)S(1)}, bf16[4,128,256]{2,1,0:T(8,128)(2,1)S(1)}, u32[]{:S(2)}, u32[]{:S(2)}) %collective-permute-start.4) | collective-permute-done | bytes 262176 | tf_op jit(solution)/shard_map/ppermute | solution.py:36
  92.6 0.0 all-gather.3.cloned.1.call-done
  92.6 1.6 shard_map.83
  94.2 1.9 collective-permute-start.5
  96.1 0.0 collective-permute-done.6.far_ref
  96.1 2.7 %shard_map.84 = (f32[128,512]{1,0:T(8,128)S(1)}, f32[128,512]{1,0:T(8,128)S(1)}, f32[2,128,512]{2,1,0:T(8,128)S(1)}, bf16[8,128,256]{2,1,0:T(8,128)(2,1)S(1)}) custom-call(s32[3]{0:T(128)S(1)} %pad_add_fusion.place_ref, bf16[2,4,128,256]{3,2,1,0:T(8,128)(2,1)S(1)} %get-tuple-element.15.keep_ref, bf16[2,4,128,256]{3,2,1,0:T(8,128)(2,1)S(1)} %collective-permute-done.other_ref, ...), custom_call_target="tpu_custom_call" | custom-call | tf_op jit(solution)/shard_map/pallas_call | solution.py:240
  98.8 2.4 %collective-permute-start.7 = (f32[2,128,512]{2,1,0:T(8,128)S(1)}, f32[2,128,512]{2,1,0:T(8,128)S(1)}, u32[]{:S(2)}, u32[]{:S(2)}) collective-permute-start(f32[2,128,512]{2,1,0:T(8,128)S(1)} %get-tuple-element.20), channel_id=1, source_target_pairs={{0,128},{128,0},{1,129},{129,1},{2,130},{130,2},{3,131},{131,3},{4... | collective-permute-start | bytes 1572872 | tf_op jit(solution)/shard_map/ppermute | solution.py:36
  101.2 0.0 collective-permute-done.5
  101.3 0.8 broadcast_in_dim.28
  102.1 5.5 %all-to-all-start.1 = ((bf16[8,128,256]{2,1,0:T(8,128)(2,1)}), bf16[8,128,256]{2,1,0:T(8,128)(2,1)S(1)}, u32[]{:S(2)}, u32[]{:S(2)}) async-start(bf16[8,128,256]{2,1,0:T(8,128)(2,1)} %broadcast_in_dim.28), calls=%async_computation.1 | async-start | bytes 1048576 | tf_op jit(solution)/shard_map/all_to_all | solution.py:32
  107.6 0.0 collective-permute-done.7.refs_1_.refs_4_
  107.6 2.7 %collective-permute-start.8 = (f32[128,512]{1,0:T(8,128)S(1)}, f32[128,512]{1,0:T(8,128)S(1)}, u32[]{:S(2)}, u32[]{:S(2)}) collective-permute-start(f32[128,512]{1,0:T(8,128)S(1)} %fusion), channel_id=1, source_target_pairs={{0,256},{256,0},{1,257},{257,1},{2,258},{258,2},{3,259},{259,3},{4... | collective-permute-start | bytes 786440 | tf_op jit(solution)/shard_map/ppermute | solution.py:36
  111.6 4.6 %collective-permute-start.9 = (bf16[8,128,256]{2,1,0:T(8,128)(2,1)S(1)}, bf16[8,128,256]{2,1,0:T(8,128)(2,1)S(1)}, u32[]{:S(2)}, u32[]{:S(2)}) collective-permute-start(bf16[8,128,256]{2,1,0:T(8,128)(2,1)S(1)} %get-tuple-element.24.w_ref), channel_id=1, source_target_pairs={{0,256},{256,0},{1,257},{257,1},{2,258},{258,2},{3,259},{259,3},{4... | collective-permute-start | bytes 1572872 | tf_op jit(solution)/shard_map/ppermute | solution.py:36
  116.3 8.9 %all-to-all-done.1 = bf16[8,128,256]{2,1,0:T(8,128)(2,1)S(1)} async-done(((bf16[8,128,256]{2,1,0:T(8,128)(2,1)}), bf16[8,128,256]{2,1,0:T(8,128)(2,1)S(1)}, u32[]{:S(2)}, u32[]{:S(2)}) %all-to-all-start.1) | async-done | bytes 524320 | tf_op jit(solution)/shard_map/all_to_all | solution.py:32
  125.2 11.5 %attend_cache.1 = (f32[2,1024,128]{2,1,0:T(8,128)S(1)}, f32[2,1024,256]{2,1,0:T(8,128)S(1)}) custom-call(f32[8,2048]{1,0:T(8,128)S(1)} %broadcast_in_dim.31.bias_ref, bf16[1024,256]{1,0:T(8,128)(2,1)S(1)} %bitcast.18, bf16[2048,256]{1,0:T(8,128)(2,1)} %bitcast.24, bf16[2048,256]{1,0:T(8,128)(2,1)} %bitcast.25), custom_call_target="tpu_custom_call" | custom-call | tf_op jit(solution)/shard_map/attend_cache/pallas_call | solution.py:310
  136.8 0.0 collective-permute-done.8.refs_2_.refs_5_
  136.8 2.9 %attend_new.1 = bf16[8,144,256]{2,1,0:T(8,128)(2,1)} custom-call(s32[3]{0:T(128)S(1)} %pad_add_fusion.place_ref, bf16[1024,256]{1,0:T(8,128)(2,1)S(1)} %bitcast.19, f32[128,512]{1,0:T(8,128)S(1)} %get-tuple-element.19.refs_0_.refs_3_, f32[2,128,512]{2,1,0:T(8,128)S(1)} %collective-permute-done.7.refs_1_.refs_4_, ...), custom_call_target="tpu_custom_call" | custom-call | tf_op jit(solution)/shard_map/attend_new/pallas_call | solution.py:329
  139.7 3.5 %all-to-all-start.2 = ((bf16[8,144,256]{2,1,0:T(8,128)(2,1)}), bf16[8,144,256]{2,1,0:T(8,128)(2,1)S(1)}, u32[]{:S(2)}, u32[]{:S(2)}) async-start(bf16[8,144,256]{2,1,0:T(8,128)(2,1)} %attend_new.1), calls=%async_computation.2 | async-start | bytes 1179648 | tf_op jit(solution)/shard_map/all_to_all | solution.py:346
  143.3 1.9 collective-permute-start.10
  145.2 0.0 collective-permute-done.9.far_w_ref
  145.2 2.4 %collective-permute-start.11 = (bf16[8,128,256]{2,1,0:T(8,128)(2,1)S(1)}, bf16[8,128,256]{2,1,0:T(8,128)(2,1)S(1)}, u32[]{:S(2)}, u32[]{:S(2)}) collective-permute-start(bf16[8,128,256]{2,1,0:T(8,128)(2,1)S(1)} %collective-permute-done.9.far_w_ref), channel_id=1, source_target_pairs={{0,128},{128,0},{1,129},{129,1},{2,130},{130,2},{3,131},{131,3},{4... | collective-permute-start | bytes 1572872 | tf_op jit(solution)/shard_map/ppermute | solution.py:36
  147.6 0.0 collective-permute-done.10.swap_w_ref
  147.6 1.5 collective-permute-done.11.swap_far_w_ref
  149.1 13.4 %all-to-all-done.2.parts_ref = bf16[8,144,256]{2,1,0:T(8,128)(2,1)S(1)} async-done(((bf16[8,144,256]{2,1,0:T(8,128)(2,1)}), bf16[8,144,256]{2,1,0:T(8,128)(2,1)S(1)}, u32[]{:S(2)}, u32[]{:S(2)}) %all-to-all-start.2) | async-done | bytes 589856 | tf_op jit(solution)/shard_map/all_to_all | solution.py:346
  162.6 1.9 shard_map.85
  164.4 32.2 %all_to_all.20 = bf16[16,128,256]{2,1,0:T(8,128)(2,1)S(1)} all-to-all(bf16[16,128,256]{2,1,0:T(8,128)(2,1)S(1)} %shard_map.85), channel_id=1, replica_groups=mesh['x_hi'=2,'core'=2,'y'=8,'x_lo'=2,'z_4'=2,'z_2'=2,'z_1'=2] {'y','x_lo'}, dimensions={0} | all-to-all | bytes 2097152 | tf_op jit(solution)/shard_map/all_to_all | solution.py:349
  196.7 0.8 reduce_sum.12
  (10 shorter events, 0.1 us)
Async XLA Ops:
  6.5 86.0 %all-gather.3.cloned.1.call-start = ((), (), s32[]{:S(2)}) async-start(), calls=%async_computation.4 | async-start | bytes 2359296 | tf_op jit(solution)/shard_map/all_gather | solution.py:268
  9.7 41.4 %copy-start = (bf16[128,256]{1,0:T(8,128)(2,1)S(1)}, bf16[128,256]{1,0:T(8,128)(2,1)}, u32[]{:S(2)}) copy-start(bf16[128,256]{1,0:T(8,128)(2,1)} %query_ref.1) | copy-start | bytes 196612
  11.7 36.6 %all-to-all-start = ((bf16[16,128,256]{2,1,0:T(8,128)(2,1)}), bf16[16,128,256]{2,1,0:T(8,128)(2,1)S(1)}, u32[]{:S(2)}, u32[]{:S(2)}) async-start(bf16[16,128,256]{2,1,0:T(8,128)(2,1)} %broadcast_in_dim.26), calls=%async_computation | async-start | bytes 2097152 | tf_op jit(solution)/shard_map/all_to_all | solution.py:32
  49.2 28.5 %collective-permute-start = (bf16[2,4,128,256]{3,2,1,0:T(8,128)(2,1)S(1)}, bf16[2,4,128,256]{3,2,1,0:T(8,128)(2,1)S(1)}, u32[]{:S(2)}, u32[]{:S(2)}) collective-permute-start(bf16[2,4,128,256]{3,2,1,0:T(8,128)(2,1)S(1)} %get-tuple-element.16), channel_id=1, source_target_pairs={{0,128},{128,0},{1,129},{129,1},{2,130},{130,2},{3,131},{131,3},{4... | collective-permute-start | bytes 1572872 | tf_op jit(solution)/shard_map/ppermute | solution.py:36
  51.1 7.9 %collective-permute-start.1 = (bf16[1,128,256]{2,1,0:T(8,128)(2,1)S(1)}, bf16[1,128,256]{2,1,0:T(8,128)(2,1)S(1)}, u32[]{:S(2)}, u32[]{:S(2)}) collective-permute-start(bf16[1,128,256]{2,1,0:T(8,128)(2,1)S(1)} %bitcast.27), channel_id=1, source_target_pairs={{0,256},{256,0},{1,257},{257,1},{2,258},{258,2},{3,259},{259,3},{4... | collective-permute-start | bytes 196616 | tf_op jit(solution)/shard_map/ppermute | solution.py:36
  59.0 13.8 %collective-permute-start.2 = (bf16[1,128,256]{2,1,0:T(8,128)(2,1)S(1)}, bf16[1,128,256]{2,1,0:T(8,128)(2,1)S(1)}, u32[]{:S(2)}, u32[]{:S(2)}) collective-permute-start(bf16[1,128,256]{2,1,0:T(8,128)(2,1)S(1)} %collective-permute-done.1), channel_id=1, source_target_pairs={{0,4},{4,0},{1,5},{5,1},{2,6},{6,2},{3,7},{7,3},{8,12},{12,8},{9,1... | collective-permute-start | bytes 196616 | tf_op jit(solution)/shard_map/ppermute | solution.py:36
  72.8 10.1 %collective-permute-start.3 = (bf16[2,128,256]{2,1,0:T(8,128)(2,1)S(1)}, bf16[2,128,256]{2,1,0:T(8,128)(2,1)S(1)}, u32[]{:S(2)}, u32[]{:S(2)}) collective-permute-start(bf16[2,128,256]{2,1,0:T(8,128)(2,1)S(1)} %pad_maximum_fusion.1), channel_id=1, source_target_pairs={{0,2},{2,0},{1,3},{3,1},{4,6},{6,4},{5,7},{7,5},{8,10},{10,8},{9,1... | collective-permute-start | bytes 393224 | tf_op jit(solution)/shard_map/ppermute | solution.py:36
  77.7 18.4 %collective-permute-start.6 = (bf16[2,4,128,256]{3,2,1,0:T(8,128)(2,1)S(1)}, bf16[2,4,128,256]{3,2,1,0:T(8,128)(2,1)S(1)}, u32[]{:S(2)}, u32[]{:S(2)}) collective-permute-start(bf16[2,4,128,256]{3,2,1,0:T(8,128)(2,1)S(1)} %pad_maximum_fusion), channel_id=1, source_target_pairs={{0,256},{256,0},{1,257},{257,1},{2,258},{258,2},{3,259},{259,3},{4... | collective-permute-start | bytes 1572872 | tf_op jit(solution)/shard_map/ppermute | solution.py:36
  82.8 9.7 %collective-permute-start.4 = (bf16[4,128,256]{2,1,0:T(8,128)(2,1)S(1)}, bf16[4,128,256]{2,1,0:T(8,128)(2,1)S(1)}, u32[]{:S(2)}, u32[]{:S(2)}) collective-permute-start(bf16[4,128,256]{2,1,0:T(8,128)(2,1)S(1)} %constant_dynamic-update-slice_fusion.far_w_ref), channel_id=1, source_target_pairs={{0,1},{1,0},{2,3},{3,2},{4,5},{5,4},{6,7},{7,6},{8,9},{9,8},{10,11... | collective-permute-start | bytes 786440 | tf_op jit(solution)/shard_map/ppermute | solution.py:36
  94.2 7.1 %collective-permute-start.5 = (f32[128,256]{1,0:T(8,128)S(1)}, f32[128,256]{1,0:T(8,128)S(1)}, u32[]{:S(2)}, u32[]{:S(2)}) collective-permute-start(f32[128,256]{1,0:T(8,128)S(1)} %get-tuple-element.18), channel_id=1, source_target_pairs={{0,128},{128,0},{1,129},{129,1},{2,130},{130,2},{3,131},{131,3},{4... | collective-permute-start | bytes 393224 | tf_op jit(solution)/shard_map/ppermute | solution.py:36
  98.8 8.8 %collective-permute-start.7 = (f32[2,128,512]{2,1,0:T(8,128)S(1)}, f32[2,128,512]{2,1,0:T(8,128)S(1)}, u32[]{:S(2)}, u32[]{:S(2)}) collective-permute-start(f32[2,128,512]{2,1,0:T(8,128)S(1)} %get-tuple-element.20), channel_id=1, source_target_pairs={{0,128},{128,0},{1,129},{129,1},{2,130},{130,2},{3,131},{131,3},{4... | collective-permute-start | bytes 1572872 | tf_op jit(solution)/shard_map/ppermute | solution.py:36
  102.1 23.1 %all-to-all-start.1 = ((bf16[8,128,256]{2,1,0:T(8,128)(2,1)}), bf16[8,128,256]{2,1,0:T(8,128)(2,1)S(1)}, u32[]{:S(2)}, u32[]{:S(2)}) async-start(bf16[8,128,256]{2,1,0:T(8,128)(2,1)} %broadcast_in_dim.28), calls=%async_computation.1 | async-start | bytes 1048576 | tf_op jit(solution)/shard_map/all_to_all | solution.py:32
  107.6 29.2 %collective-permute-start.8 = (f32[128,512]{1,0:T(8,128)S(1)}, f32[128,512]{1,0:T(8,128)S(1)}, u32[]{:S(2)}, u32[]{:S(2)}) collective-permute-start(f32[128,512]{1,0:T(8,128)S(1)} %fusion), channel_id=1, source_target_pairs={{0,256},{256,0},{1,257},{257,1},{2,258},{258,2},{3,259},{259,3},{4... | collective-permute-start | bytes 786440 | tf_op jit(solution)/shard_map/ppermute | solution.py:36
  111.6 33.6 %collective-permute-start.9 = (bf16[8,128,256]{2,1,0:T(8,128)(2,1)S(1)}, bf16[8,128,256]{2,1,0:T(8,128)(2,1)S(1)}, u32[]{:S(2)}, u32[]{:S(2)}) collective-permute-start(bf16[8,128,256]{2,1,0:T(8,128)(2,1)S(1)} %get-tuple-element.24.w_ref), channel_id=1, source_target_pairs={{0,256},{256,0},{1,257},{257,1},{2,258},{258,2},{3,259},{259,3},{4... | collective-permute-start | bytes 1572872 | tf_op jit(solution)/shard_map/ppermute | solution.py:36
  139.7 22.9 %all-to-all-start.2 = ((bf16[8,144,256]{2,1,0:T(8,128)(2,1)}), bf16[8,144,256]{2,1,0:T(8,128)(2,1)S(1)}, u32[]{:S(2)}, u32[]{:S(2)}) async-start(bf16[8,144,256]{2,1,0:T(8,128)(2,1)} %attend_new.1), calls=%async_computation.2 | async-start | bytes 1179648 | tf_op jit(solution)/shard_map/all_to_all | solution.py:346
  143.3 4.4 %collective-permute-start.10 = (bf16[8,128,256]{2,1,0:T(8,128)(2,1)S(1)}, bf16[8,128,256]{2,1,0:T(8,128)(2,1)S(1)}, u32[]{:S(2)}, u32[]{:S(2)}) collective-permute-start(bf16[8,128,256]{2,1,0:T(8,128)(2,1)S(1)} %get-tuple-element.24.w_ref), channel_id=1, source_target_pairs={{0,128},{128,0},{1,129},{129,1},{2,130},{130,2},{3,131},{131,3},{4... | collective-permute-start | bytes 1572872 | tf_op jit(solution)/shard_map/ppermute | solution.py:36
  145.2 3.9 %collective-permute-start.11 = (bf16[8,128,256]{2,1,0:T(8,128)(2,1)S(1)}, bf16[8,128,256]{2,1,0:T(8,128)(2,1)S(1)}, u32[]{:S(2)}, u32[]{:S(2)}) collective-permute-start(bf16[8,128,256]{2,1,0:T(8,128)(2,1)S(1)} %collective-permute-done.9.far_w_ref), channel_id=1, source_target_pairs={{0,128},{128,0},{1,129},{129,1},{2,130},{130,2},{3,131},{131,3},{4... | collective-permute-start | bytes 1572872 | tf_op jit(solution)/shard_map/ppermute | solution.py:36
Sparse Core Ops, SparseCore 0:
  9.8 48.7 all-gather.2
